TPU v7x, 32 devices: a whole 2x2x4 slice. The times are simulated.
32 devices in a mesh: freq: 8 (over z, y), tm: 4 (over x, core).
Axes of the slice: x: 2, y: 2, z: 4, core: 2. Of those that a mesh axis runs over, the one named last changes fastest.
Arguments:
- visibility: bfloat16 [8, 4, 8, 4096], P('freq', 'tm'), may hold values from -6 to 6
- model_visibility: bfloat16 [8, 4, 8, 4096], P('freq', 'tm'), may hold values from -6 to 6
- keep_mask: int32 [8, 4, 4096], P('freq', 'tm'), may hold values 0 or 1
- gains_in: float32 [8, 8, 512], P('freq'), may hold values from -6 to 6
- consensus_in: float32 [8, 8, 512], P('freq'), may hold values from -6 to 6
- dual_in: float32 [8, 8, 512], P('freq'), may hold values from -4 to 4
- penalty: float32 [512], replicated, may hold values from 30 to 600
- channel_index: int32 [8], P('freq'), may hold values from 0 to 7, each once
- first_station: int32 [4096], replicated, may hold values from 0 to 511, as said below
- second_station: int32 [4096], replicated, may hold values from 0 to 511
Outputs:
- gains_out: float32 [8, 8, 512], P('freq', None, 'tm')
- consensus_out: float32 [8, 8, 512], P('freq', None, 'tm')
- dual_out: float32 [8, 8, 512], P('freq', None, 'tm')
Inputs may be any that keep to these rules, and one draw needn't show every extreme that they name: first_station and second_station of a baseline differ; station numbers repeat over baselines. channel_index holds each channel number once.
All inputs are finite; a program needn't handle non-finite values. No bound on the sum of `keep_mask` on one device may be relied on, other than what follows from the above.
Results may differ from a plain program's by a relative error of at most 0.0003.
Values sent between devices are 32-bit elements; how exact they have to be, the bound alone decides.
No kernel may reach another device: no remote copies, remote signals or barrier semaphores. Data moves between devices by JAX's collectives and lax.ppermute only.
A program may use at most 64 MiB of HBM per device.

v0:
```python
import jax
import jax.numpy as jnp
from jax import lax
from jax.sharding import PartitionSpec as P

SWEEPS = 2


def entries(array, axis):
    return [
        (
            lax.index_in_dim(array, 2 * index, axis, False),
            lax.index_in_dim(array, 2 * index + 1, axis, False),
        )
        for index in range(4)
    ]


def stack_jones(matrix, axis):
    return jnp.stack([matrix[index][part] for index in range(4) for part in range(2)], axis=axis)


def complex_mul(leading_entry, second):
    return (
        leading_entry[0] * second[0] - leading_entry[1] * second[1],
        leading_entry[0] * second[1] + leading_entry[1] * second[0],
    )


def complex_add(leading_entry, second):
    return (leading_entry[0] + second[0], leading_entry[1] + second[1])


def matrix_mul(leading_entry, second):
    return [
        complex_add(
            complex_mul(leading_entry[0], second[0]), complex_mul(leading_entry[1], second[2])
        ),
        complex_add(
            complex_mul(leading_entry[0], second[1]), complex_mul(leading_entry[1], second[3])
        ),
        complex_add(
            complex_mul(leading_entry[2], second[0]), complex_mul(leading_entry[3], second[2])
        ),
        complex_add(
            complex_mul(leading_entry[2], second[1]), complex_mul(leading_entry[3], second[3])
        ),
    ]


def adjoint(matrix):
    return [
        (matrix[0][0], -matrix[0][1]),
        (matrix[2][0], -matrix[2][1]),
        (matrix[1][0], -matrix[1][1]),
        (matrix[3][0], -matrix[3][1]),
    ]


def weighted(matrix, weight):
    return [(entry[0] * weight, entry[1] * weight) for entry in matrix]


def one_hot_table(station_list, stations):
    return (jnp.arange(stations, dtype=jnp.int32)[:, None] == station_list[None, :]).astype(
        jnp.float32
    )


def normal_sums(vis_block, model_block, flag_block, gains, first_hot, second_hot):
    gains_first = jnp.einsum("cjs,sb->cjb", gains, first_hot, precision=lax.Precision.HIGHEST)[
        :, None
    ]
    gains_second = jnp.einsum("cjs,sb->cjb", gains, second_hot, precision=lax.Precision.HIGHEST)[
        :, None
    ]
    observed = entries(vis_block.astype(jnp.float32), 2)
    modelled = entries(model_block.astype(jnp.float32), 2)
    weight = flag_block.astype(jnp.float32)
    left = matrix_mul(modelled, adjoint(entries(gains_second, 2)))
    right = matrix_mul(adjoint(modelled), adjoint(entries(gains_first, 2)))
    num_first = weighted(matrix_mul(observed, adjoint(left)), weight)
    den_first = weighted(matrix_mul(left, adjoint(left)), weight)
    num_second = weighted(matrix_mul(adjoint(observed), adjoint(right)), weight)
    den_second = weighted(matrix_mul(right, adjoint(right)), weight)
    term_first = jnp.sum(
        jnp.concatenate([stack_jones(num_first, 1), stack_jones(den_first, 1)], axis=1), axis=2
    )
    term_second = jnp.sum(
        jnp.concatenate([stack_jones(num_second, 1), stack_jones(den_second, 1)], axis=1), axis=2
    )
    totals = jnp.einsum("cjb,sb->cjs", term_first, first_hot, precision=lax.Precision.HIGHEST)
    return totals + jnp.einsum(
        "cjb,sb->cjs", term_second, second_hot, precision=lax.Precision.HIGHEST
    )


def solve_jones(totals, gains_old, consensus, dual, penalty):
    numer = entries(totals[:, :8], 1)
    denom = entries(totals[:, 8:], 1)
    target = entries(consensus - dual, 1)
    rhs_side = [
        (numer[index][0] + penalty * target[index][0], numer[index][1] + penalty * target[index][1])
        for index in range(4)
    ]
    regular = [
        (denom[0][0] + penalty, denom[0][1]),
        denom[1],
        denom[2],
        (denom[3][0] + penalty, denom[3][1]),
    ]
    determ = complex_add(
        complex_mul(regular[0], regular[3]),
        complex_mul((-regular[1][0], -regular[1][1]), regular[2]),
    )
    magnitude = determ[0] * determ[0] + determ[1] * determ[1]
    recip = (determ[0] / magnitude, -determ[1] / magnitude)
    inverse = [
        complex_mul(regular[3], recip),
        complex_mul((-regular[1][0], -regular[1][1]), recip),
        complex_mul((-regular[2][0], -regular[2][1]), recip),
        complex_mul(regular[0], recip),
    ]
    solved = stack_jones(matrix_mul(rhs_side, inverse), 1)
    return 0.5 * (solved + gains_old)


def legendre(position):
    square = position * position
    return jnp.stack(
        [jnp.ones_like(position), position, 1.5 * square - 0.5, (2.5 * square - 1.5) * position],
        axis=-1,
    )


def channel_basis(index, total):
    return legendre(2.0 * index.astype(jnp.float32) / (total - 1.0) - 1.0)


def poly_fit(moments, total):
    basis_all = channel_basis(jnp.arange(total, dtype=jnp.int32), float(total))
    gram = jnp.dot(basis_all.T, basis_all, precision=lax.Precision.HIGHEST)
    factor = jnp.linalg.cholesky(gram)
    flat = moments.reshape(4, -1)
    middle = lax.linalg.triangular_solve(factor, flat, left_side=True, lower=True)
    coeffs = lax.linalg.triangular_solve(
        factor, middle, left_side=True, lower=True, transpose_a=True
    )
    return coeffs.reshape(moments.shape)


def shards(
    visibility,
    model_visibility,
    keep_mask,
    gains_in,
    consensus_in,
    dual_in,
    penalty,
    channel_index,
    first_station,
    second_station,
):
    stations = gains_in.shape[2]
    width = stations // lax.axis_size("tm")
    start_shift = lax.axis_index("tm") * width
    first_hot = one_hot_table(first_station, stations)
    second_hot = one_hot_table(second_station, stations)

    def own_part(array):
        return lax.dynamic_slice_in_dim(array, start_shift, width, array.ndim - 1)

    current = gains_in
    for sweep_index in range(SWEEPS):
        totals = normal_sums(
            visibility, model_visibility, keep_mask, current, first_hot, second_hot
        )
        summed = lax.psum(totals, "tm")
        current = solve_jones(summed, current, consensus_in, dual_in, penalty)
    gains_part = own_part(current)
    dual_part = own_part(dual_in)
    total_channels = channel_index.shape[0] * lax.axis_size("freq")
    basis = channel_basis(channel_index, float(total_channels))
    combined = gains_part + dual_part
    local_moments = jnp.einsum("fk,fjs->kjs", basis, combined, precision=lax.Precision.HIGHEST)
    moments = lax.psum(local_moments, "freq")
    coeffs = poly_fit(moments, total_channels)
    consensus_out = jnp.einsum("fk,kjs->fjs", basis, coeffs, precision=lax.Precision.HIGHEST)
    dual_out = dual_part + gains_part - consensus_out
    return (gains_part, consensus_out, dual_out)


def solution(mesh):
    placed = (
        P("freq", "tm", None, None),
        P("freq", "tm", None, None),
        P("freq", "tm", None),
        P("freq", None, None),
        P("freq", None, None),
        P("freq", None, None),
        P(),
        P("freq"),
        P(),
        P(),
    )
    return jax.shard_map(
        shards,
        mesh=mesh,
        in_specs=placed,
        out_specs=(P("freq", None, "tm"), P("freq", None, "tm"), P("freq", None, "tm")),
        check_vma=False,
    )
```

profile of v0, /device:TPU:0, one launch (start us, length us, event | category | flops | bytes accessed | tf_op | source)
XLA Modules:
  0.0 103.6 jit_solution(14120705225545996013)
XLA Ops:
  0.6 0.9 convert_element_type.39
  1.5 0.9 convert_element_type.40
  2.4 3.4 %fusion.10 = f32[1,1,8,4096]{3,2,1,0:T(8,128)S(1)} fusion(s32[4096]{0:T(1024)} %param.18, f32[1,8,512]{2,1,0:T(8,128)} %param.13), kind=kOutput, calls=%fused_computation.12 | convolution fusion | flops 203423744 | bytes 163840 | tf_op jit(solution)/shard_map/cjs,sb->cjb/dot_general | solution.py:71
  5.7 0.3 constant_dynamic-update-slice_fusion.31
  6.1 0.1 constant_dynamic-update-slice_fusion.30
  6.2 0.3 constant_dynamic-update-slice_fusion.29
  6.5 0.1 constant_dynamic-update-slice_fusion.28
  6.7 0.1 constant_dynamic-update-slice_fusion.26
  6.9 2.7 %fusion.8 = f32[1,1,8,4096]{3,2,1,0:T(8,128)S(1)} fusion(s32[4096]{0:T(1024)S(1)} %copy-done.8, f32[1,8,512]{2,1,0:T(8,128)S(1)} %copy-done.4), kind=kOutput, calls=%fused_computation.10 | convolution fusion | flops 203423744 | bytes 163840 | tf_op jit(solution)/shard_map/cjs,sb->cjb/dot_general | solution.py:74
  9.6 0.3 constant_dynamic-update-slice_fusion.15
  9.9 0.2 constant_dynamic-update-slice_fusion.24
  10.5 0.3 constant_dynamic-update-slice_fusion.13
  10.9 0.1 constant_dynamic-update-slice_fusion.16
  11.0 0.1 constant_dynamic-update-slice_fusion.11
  11.1 0.1 constant_dynamic-update-slice_fusion.10
  11.2 0.1 constant_dynamic-update-slice_fusion.9
  11.3 0.1 constant_dynamic-update-slice_fusion.8
  11.9 0.1 copy-done.7
  12.1 3.8 %fusion.3 = f32[16,512]{1,0:T(8,128)S(1)} fusion(s32[4096]{0:T(1024)S(1)} %copy-done.7, f32[1,16,1,4096]{3,2,1,0:T(1,128)S(1)} %constant_dynamic-update-slice_fusion), kind=kOutput, calls=%fused_computation.4 | convolution fusion | flops 404750336 | bytes 311296 | tf_op jit(solution)/shard_map/cjb,sb->cjs/dot_general | solution.py:92
  16.0 4.0 %fusion.21 = f32[1,16,512]{2,1,0:T(8,128)S(1)} fusion(f32[16,512]{1,0:T(8,128)S(1)} %fusion.3, s32[4096]{0:T(1024)S(1)} %copy-done.8, f32[1,16,1,4096]{3,2,1,0:T(1,128)S(1)} %get-tuple-element.151), kind=kOutput, calls=%fused_computation.23 | convolution fusion | flops 404758528 | bytes 344064 | tf_op jit(solution)/shard_map/cjb,sb->cjs/dot_general | solution.py:93
  20.0 12.9 %psum.21 = f32[1,16,512]{2,1,0:T(8,128)S(1)} all-reduce(f32[1,16,512]{2,1,0:T(8,128)S(1)} %fusion.21), channel_id=1, replica_groups=mesh['freq'=8,'tm'=4] {'tm'}, use_global_device_ids=true, to_apply=%region_0.0 | all-reduce | flops 8192 | bytes 65536 | tf_op jit(solution)/shard_map/psum | solution.py:178
  33.2 2.7 %fusion.11 = f32[1,1,8,4096]{3,2,1,0:T(8,128)S(1)} fusion(s32[4096]{0:T(1024)S(1)} %copy-done.7, f32[1,8,512]{2,1,0:T(8,128)S(1)} %add_multiply_fusion), kind=kOutput, calls=%fused_computation.13 | convolution fusion | flops 203423744 | bytes 163840 | tf_op jit(solution)/shard_map/cjs,sb->cjb/dot_general | solution.py:71
  35.9 0.3 constant_dynamic-update-slice_fusion.63
  36.2 0.1 constant_dynamic-update-slice_fusion.62
  36.3 0.3 constant_dynamic-update-slice_fusion.61
  36.6 0.1 constant_dynamic-update-slice_fusion.60
  36.8 0.1 constant_dynamic-update-slice_fusion.58
  37.0 2.7 %fusion.9 = f32[1,1,8,4096]{3,2,1,0:T(8,128)S(1)} fusion(s32[4096]{0:T(1024)S(1)} %copy-done.8, f32[1,8,512]{2,1,0:T(8,128)S(1)} %add_multiply_fusion), kind=kOutput, calls=%fused_computation.11 | convolution fusion | flops 203423744 | bytes 163840 | tf_op jit(solution)/shard_map/cjs,sb->cjb/dot_general | solution.py:74
  39.6 0.3 constant_dynamic-update-slice_fusion.47
  39.9 0.2 constant_dynamic-update-slice_fusion.56
  40.1 0.3 constant_dynamic-update-slice_fusion.45
  40.9 0.1 constant_dynamic-update-slice_fusion.48
  41.0 0.1 constant_dynamic-update-slice_fusion.43
  41.3 0.1 constant_dynamic-update-slice_fusion.40
  42.0 3.8 %fusion.1 = f32[16,512]{1,0:T(8,128)S(1)} fusion(s32[4096]{0:T(1024)S(1)} %copy-done.7, f32[1,16,1,4096]{3,2,1,0:T(1,128)S(1)} %constant_dynamic-update-slice_fusion.32), kind=kOutput, calls=%fused_computation.2 | convolution fusion | flops 404750336 | bytes 311296 | tf_op jit(solution)/shard_map/cjb,sb->cjs/dot_general | solution.py:92
  45.8 4.1 %fusion.23 = f32[1,16,512]{2,1,0:T(8,128)S(1)} fusion(f32[16,512]{1,0:T(8,128)S(1)} %fusion.1, s32[4096]{0:T(1024)S(1)} %copy-done.8, f32[1,16,1,4096]{3,2,1,0:T(1,128)S(1)} %get-tuple-element.139), kind=kOutput, calls=%fused_computation.25 | convolution fusion | flops 404758528 | bytes 344064 | tf_op jit(solution)/shard_map/cjb,sb->cjs/dot_general | solution.py:93
  49.9 10.3 %psum.22 = f32[1,16,512]{2,1,0:T(8,128)S(1)} all-reduce(f32[1,16,512]{2,1,0:T(8,128)S(1)} %fusion.23), channel_id=1, replica_groups=mesh['freq'=8,'tm'=4] {'tm'}, use_global_device_ids=true, to_apply=%region_1.0 | all-reduce | flops 8192 | bytes 65536 | tf_op jit(solution)/shard_map/psum | solution.py:178
  61.3 37.5 %psum.23 = f32[8,128,4]{1,0,2:T(8,128)S(1)} all-reduce(f32[8,128,4]{1,0,2:T(8,128)S(1)} %bitcast.1387), channel_id=1, replica_groups=mesh['freq'=8,'tm'=4] {'freq'}, use_global_device_ids=true, to_apply=%region_4.0 | all-reduce | flops 4096 | bytes 32768 | tf_op jit(solution)/shard_map/psum | solution.py:186
  98.8 0.3 fusion.55
  99.0 0.1 copy.13
  99.1 0.4 cholesky.16
  99.6 0.7 compare_reduce_fusion
  100.2 0.6 fusion.62
  100.9 0.3 custom-call.8
  101.2 1.0 fusion.44
  102.2 0.5 fusion.65
  102.7 0.2 fusion.72
  103.0 0.6 fusion.70
  (80 shorter events, 3.4 us)
Async XLA Ops:
  2.3 3.4 %copy-start = (s32[1,1,4096]{2,1,0:T(1,128)S(1)}, s32[1,1,4096]{2,1,0:T(1,128)}, u32[]{:S(2)}) copy-start(s32[1,1,4096]{2,1,0:T(1,128)} %param.12) | copy-start | bytes 49156
  6.2 0.7 copy-start.4
  6.2 0.7 copy-start.8
  11.4 0.7 copy-start.7
  15.9 17.0 %copy-start.2 = (f32[512]{0:T(512)S(1)}, f32[512]{0:T(512)}, u32[]{:S(2)}) copy-start(f32[512]{0:T(512)} %param.16) | copy-start | bytes 6148
  15.9 17.0 %copy-start.1 = (f32[1,8,512]{2,1,0:T(8,128)S(1)}, f32[1,8,512]{2,1,0:T(8,128)}, u32[]{:S(2)}) copy-start(f32[1,8,512]{2,1,0:T(8,128)} %param.15) | copy-start | bytes 49156
  15.9 17.0 %copy-start.3 = (f32[1,8,512]{2,1,0:T(8,128)S(1)}, f32[1,8,512]{2,1,0:T(8,128)}, u32[]{:S(2)}) copy-start(f32[1,8,512]{2,1,0:T(8,128)} %param.14) | copy-start | bytes 49156
  60.4 42.6 %copy-start.5 = (f32[1,8,128]{2,1,0:T(8,128)}, f32[1,8,128]{2,1,0:T(8,128)S(1)}, u32[]{:S(2)}) copy-start(f32[1,8,128]{2,1,0:T(8,128)S(1)} %get-tuple-element.4) | copy-start | bytes 12292
  103.0 0.6 copy-start.6
where the time goes:
time: 104 us
  blocking collectives  60.6 us (58%)
  matrix products  29.2 us (28%)
  other arithmetic  11.7 us (11%)
  between operations  1.64 us (2%)
    psum x1, blocking collectives, shards(): moments = lax.psum(local_moments, 'freq')  37.5 us
    psum x2, blocking collectives, shards(): summed = lax.psum(totals, 'tm')  23.2 us
    dot_general x2, matrix products, normal_sums(): jnp.einsum('cjb,sb->cjs', term_second, second_hot, precision=lax.Precisio...  8.11 us
    dot_general x2, matrix products, normal_sums(): jnp.einsum('cjb,sb->cjs', term_first, first_hot, precision=lax.Precision....  7.68 us
    unnamed x57, other arithmetic  6.62 us
    dot_general x2, matrix products, normal_sums(): jnp.einsum('cjs,sb->cjb', gains, first_hot, precision=lax.Precision.HIGHEST)  6.05 us
    dot_general x2, matrix products, normal_sums(): jnp.einsum('cjs,sb->cjb', gains, second_hot, precision=lax.Precision.HIGH...  5.31 us

commit v1 on v0

v1 whole, which is shorter than its diff:
```python
import jax
import jax.numpy as jnp
import numpy as np
from jax import lax
from jax.experimental import pallas as pl
from jax.experimental.pallas import tpu as pltpu
from jax.sharding import PartitionSpec as P

SWEEPS = 2
LANES = 128
SUBS = 8
LO = 256
ROWS = 16
SPLITS = 2
PRODS = 48


def vmem():
    return pl.BlockSpec(memory_space=pltpu.VMEM)


def smem():
    return pl.BlockSpec(memory_space=pltpu.SMEM)


def split_bf16(value):
    parts = []
    for index in range(SPLITS):
        part = value.astype(jnp.bfloat16)
        parts.append(part)
        if index + 1 < SPLITS:
            value = value - part.astype(jnp.float32)
    return parts


def mul_conj(a, b):
    return (a[0] * b[0] + a[1] * b[1], a[1] * b[0] - a[0] * b[1])


def widen_kernel(vis_ref, model_ref, keep_ref, out_ref):
    tiles = vis_ref.shape[1] // LANES
    for tile in range(tiles):
        lanes = pl.ds(tile * LANES, LANES)
        keep = keep_ref[:, lanes].astype(jnp.float32)
        out_ref[pl.ds(tile * SUBS, SUBS), :] = vis_ref[:, lanes].astype(jnp.float32)
        out_ref[pl.ds((tiles + tile) * SUBS, SUBS), :] = (
            model_ref[:, lanes].astype(jnp.float32) * keep
        )


def slot_products(slot_ref, group, tiles):
    def load(part, component):
        start = (part * tiles + group * SUBS) * SUBS + component
        return slot_ref[pl.ds(start, SUBS, stride=SUBS), :]

    seen = [(load(0, 2 * e), load(0, 2 * e + 1)) for e in range(4)]
    model = [(load(1, 2 * e), load(1, 2 * e + 1)) for e in range(4)]
    rows = []
    for v in range(4):
        for m in range(4):
            rows.extend(mul_conj(seen[v], model[m]))
    rows.extend(entry[0] * entry[0] + entry[1] * entry[1] for entry in model)
    for left, right in ((0, 1), (2, 3), (0, 2), (1, 3)):
        rows.extend(mul_conj(model[left], model[right]))
    a = mul_conj(model[0], model[3])
    b = mul_conj(model[1], model[2])
    rows.extend((a[0] + b[0], a[0] - b[0], a[1] + b[1], a[1] - b[1]))
    return rows


def add_products(slot_refs, before_ref, out_ref):
    tiles = slot_refs[0].shape[0] // (2 * SUBS)
    for group in range(tiles // SUBS):
        at = pl.ds(group * SUBS, SUBS)
        total = None
        for slot_ref in slot_refs:
            rows = slot_products(slot_ref, group, tiles)
            total = rows if total is None else [x + y for x, y in zip(total, rows)]
        for index, row in enumerate(total):
            if before_ref is not None:
                row = row + before_ref[index, at, :]
            out_ref[index, at, :] = row


def tables_kernel(count, *refs):
    first_ref, second_ref = refs[:2]
    slot_refs = refs[2 : 2 + count]
    hot_ref, prod_ref = refs[2 + count :]
    baselines = first_ref.shape[1]
    step = 512
    for part, station_ref in enumerate((first_ref, second_ref)):
        for start in range(0, baselines, step):
            offset = station_ref[:, pl.ds(start, step)] & (LO - 1)
            row = lax.broadcasted_iota(jnp.int32, (LO, step), 0)
            hot_ref[:, pl.ds(part * baselines + start, step)] = jnp.where(
                row == offset, 1.0, 0.0
            ).astype(jnp.bfloat16)
    add_products(slot_refs, None, prod_ref)


def more_kernel(slot_ref, before_ref, out_ref):
    add_products([slot_ref], before_ref, out_ref)


def gram_rows(gain):
    entry = [(gain[2 * e : 2 * e + 1], gain[2 * e + 1 : 2 * e + 2]) for e in range(4)]
    h00 = sum(part * part for part in entry[0] + entry[2])
    h11 = sum(part * part for part in entry[1] + entry[3])
    top = mul_conj(entry[1], entry[0])
    low = mul_conj(entry[3], entry[2])
    zero = jnp.zeros((ROWS - 12, gain.shape[1]), jnp.float32)
    return jnp.concatenate([gain, h00, h11, top[0] + low[0], top[1] + low[1], zero], axis=0)


def baseline_terms(prod, gain_second, gain_first):
    def num(gain, swap):
        out = []
        for i in range(2):
            for l in range(2):
                real = imag = None
                for j in range(2):
                    for k in range(2):
                        if swap:
                            index = 4 * (2 * j + i) + 2 * k + l
                        else:
                            index = 4 * (2 * i + j) + 2 * l + k
                        tr, ti = prod(2 * index), prod(2 * index + 1)
                        gr, gi = gain[2 * (2 * j + k)], gain[2 * (2 * j + k) + 1]
                        if swap:
                            addr, addi = tr * gr + ti * gi, tr * gi - ti * gr
                        else:
                            addr, addi = tr * gr - ti * gi, tr * gi + ti * gr
                        real = addr if real is None else real + addr
                        imag = addi if imag is None else imag + addi
                out.extend((real, imag))
        return out

    n00, n01, n10, n11, pr, pi, qr, qi, rr, ri, sr, si, apr, amr, api, ami = (
        prod(32 + index) for index in range(16)
    )
    h00, h11, hr, hi = gain_second[8:12]
    den_first = [
        n00 * h00 + n01 * h11 + 2.0 * (pr * hr - pi * hi),
        n10 * h00 + n11 * h11 + 2.0 * (qr * hr - qi * hi),
        rr * h00 + sr * h11 + apr * hr - ami * hi,
        ri * h00 + si * h11 + api * hr + amr * hi,
    ]
    h00, h11, hr, hi = gain_first[8:12]
    den_second = [
        n00 * h00 + n10 * h11 + 2.0 * (rr * hr + ri * hi),
        n01 * h00 + n11 * h11 + 2.0 * (sr * hr + si * hi),
        pr * h00 + qr * h11 + apr * hr + api * hi,
        amr * hi - pi * h00 - qi * h11 - ami * hr,
    ]
    return num(gain_second, False) + den_first, num(gain_first, True) + den_second


def solve(total, gain, target, penalty):
    def row(array, index):
        return array[index : index + 1]

    rhs = [
        tuple(
            row(total, 2 * e + part) + penalty * row(target, 2 * e + part) for part in range(2)
        )
        for e in range(4)
    ]
    r00, r11 = row(total, 8) + penalty, row(total, 9) + penalty
    r01 = (row(total, 10), row(total, 11))
    scale = 1.0 / (r00 * r11 - (r01[0] * r01[0] + r01[1] * r01[1]))
    out = []
    for i in range(2):
        a, b = rhs[2 * i], rhs[2 * i + 1]
        cross = mul_conj(b, r01)
        out.extend(((a[part] * r11 - cross[part]) * scale for part in range(2)))
        out.append((b[0] * r00 - (a[0] * r01[0] - a[1] * r01[1])) * scale)
        out.append((b[1] * r00 - (a[0] * r01[1] + a[1] * r01[0])) * scale)
    return 0.5 * (jnp.concatenate(out, axis=0) + gain)


def sweeps_kernel(
    place_ref,
    channel_ref,
    first_ref,
    second_ref,
    gains_ref,
    consensus_ref,
    dual_ref,
    penalty_ref,
    hot_ref,
    before_ref,
    *rest,
):
    count = len(rest) - 7
    slot_refs = rest[:count]
    gain_out_ref, send_ref, prod_ref, seen_ref, term_ref, lhs_ref, full_ref = rest[count:]
    baselines = first_ref.shape[1]
    stations = gains_ref.shape[1]
    blocks = stations // LO
    tiles = baselines // LANES
    add_products(slot_refs, before_ref, prod_ref)
    term_ref[...] = jnp.zeros(term_ref.shape, jnp.float32)
    block_of = [ref[...] >> 8 for ref in (first_ref, second_ref)]
    gains = [gains_ref[:, pl.ds(h * LO, LO)] for h in range(blocks)]
    target = [
        consensus_ref[:, pl.ds(h * LO, LO)] - dual_ref[:, pl.ds(h * LO, LO)]
        for h in range(blocks)
    ]
    penalty = [penalty_ref[:, pl.ds(h * LO, LO)] for h in range(blocks)]
    for _ in range(SWEEPS):
        table = jnp.concatenate([gram_rows(gain) for gain in gains], axis=0)
        table = jnp.concatenate(split_bf16(table), axis=0)
        for part in range(2):
            found = jnp.dot(
                table,
                hot_ref[:, pl.ds(part * baselines, baselines)],
                preferred_element_type=jnp.float32,
            )
            high = blocks * ROWS
            found = sum(found[index * high : (index + 1) * high] for index in range(SPLITS))
            chosen = found[:ROWS]
            for h in range(1, blocks):
                chosen = jnp.where(
                    block_of[part] == h, found[h * ROWS : (h + 1) * ROWS], chosen
                )
            for tile in range(tiles):
                seen_ref[part, pl.ds(tile * ROWS, ROWS), :] = chosen[
                    :, tile * LANES : (tile + 1) * LANES
                ]
        for group in range(tiles // SUBS):
            start = group * SUBS * ROWS

            def prod(index):
                return prod_ref[index, pl.ds(group * SUBS, SUBS), :]

            gain_first, gain_second = (
                [seen_ref[part, pl.ds(start + j, SUBS, stride=ROWS), :] for j in range(12)]
                for part in range(2)
            )
            for part, rows in enumerate(baseline_terms(prod, gain_second, gain_first)):
                for j, row in enumerate(rows):
                    term_ref[part, pl.ds(start + j, SUBS, stride=ROWS), :] = row
        for part in range(2):
            for tile in range(tiles):
                lanes = slice(tile * LANES, (tile + 1) * LANES)
                block = block_of[part][:, lanes]
                value = term_ref[part, pl.ds(tile * ROWS, ROWS), :]
                rows = []
                for h in range(blocks):
                    rows.append(split_bf16(jnp.where(block == h, value, 0.0)))
                for index in range(SPLITS):
                    for h in range(blocks):
                        lhs_ref[
                            pl.ds((index * blocks + h) * ROWS, ROWS),
                            pl.ds(part * baselines + tile * LANES, LANES),
                        ] = rows[h][index]
        summed = lax.dot_general(
            lhs_ref[...],
            hot_ref[...],
            (((1,), (1,)), ((), ())),
            preferred_element_type=jnp.float32,
        )
        high = blocks * ROWS
        summed = sum(summed[index * high : (index + 1) * high] for index in range(SPLITS))
        gains = [
            solve(summed[h * ROWS : (h + 1) * ROWS], gains[h], target[h], penalty[h])
            for h in range(blocks)
        ]
    for h in range(blocks):
        full_ref[:, pl.ds(h * LO, LO)] = gains[h]
    width = gain_out_ref.shape[1]
    own = pl.ds(pl.multiple_of(place_ref[0] * width, width), width)
    part = full_ref[:, own]
    gain_out_ref[...] = part
    channels = send_ref.shape[0]
    mark = jnp.full((SUBS, width), channel_ref[0].astype(jnp.float32))
    combined = part + dual_ref[:, own]
    for channel in range(channels):
        send_ref[channel, :SUBS, :] = combined
        send_ref[channel, SUBS:, :] = mark


def legendre(position):
    square = position * position
    return [None, position, 1.5 * square - 0.5, (2.5 * square - 1.5) * position]


def fit_kernel(gram_factor, place_ref, channel_ref, parts_ref, gain_ref, dual_ref, *out_refs):
    consensus_ref, dual_out_ref = out_refs
    channels = parts_ref.shape[0]
    width = gain_ref.shape[1]
    scale = float(channels) - 1.0

    def basis(channel):
        return legendre(2.0 * channel / scale - 1.0)

    moments = [None] * 4
    for channel in range(channels):
        value = parts_ref[channel, :SUBS, :]
        for k, weight in enumerate(basis(parts_ref[channel, SUBS:, :])):
            add = value if weight is None else weight * value
            moments[k] = add if moments[k] is None else moments[k] + add
    middle = []
    for k in range(4):
        rest = moments[k]
        for earlier in range(k):
            rest = rest - gram_factor[k][earlier] * middle[earlier]
        middle.append(rest * (1.0 / gram_factor[k][k]))
    coeffs = [None] * 4
    for k in reversed(range(4)):
        rest = middle[k]
        for later in range(k + 1, 4):
            rest = rest - gram_factor[later][k] * coeffs[later]
        coeffs[k] = rest * (1.0 / gram_factor[k][k])
    own = basis(jnp.full((SUBS, width), channel_ref[0].astype(jnp.float32)))
    fitted = coeffs[0]
    for k in range(1, 4):
        fitted = fitted + own[k] * coeffs[k]
    consensus_ref[...] = fitted
    start = pl.multiple_of(place_ref[0] * width, width)
    dual_out_ref[...] = dual_ref[:, pl.ds(start, width)] + gain_ref[...] - fitted


def gram_cholesky(channels):
    x = 2.0 * np.arange(channels, dtype=np.float64) / (channels - 1.0) - 1.0
    basis = np.stack([np.ones_like(x), x, 1.5 * x * x - 0.5, (2.5 * x * x - 1.5) * x], -1)
    factor = np.linalg.cholesky(basis.T @ basis)
    return [[float(value) for value in row] for row in factor]


def call(kernel, shapes, spaces, scratch=()):
    single = isinstance(shapes, jax.ShapeDtypeStruct)
    return pl.pallas_call(
        kernel,
        out_shape=shapes,
        in_specs=[smem() if space == "s" else vmem() for space in spaces],
        out_specs=vmem() if single else [vmem() for _ in shapes],
        scratch_shapes=list(scratch),
    )


def shards(
    visibility,
    model_visibility,
    keep_mask,
    gains_in,
    consensus_in,
    dual_in,
    penalty,
    channel_index,
    first_station,
    second_station,
):
    f32 = jnp.float32
    baselines = visibility.shape[3]
    stations = gains_in.shape[2]
    slots = lax.axis_size("tm")
    channels = lax.axis_size("freq")
    width = stations // slots
    tiles = baselines // LANES
    blocks = stations // LO
    shape = jax.ShapeDtypeStruct
    place = lax.axis_index("tm").astype(jnp.int32).reshape(1)

    def swap(array, step):
        return lax.ppermute(array, "tm", [(i, i ^ step) for i in range(slots)])

    own = call(widen_kernel, shape((2 * tiles * SUBS, LANES), f32), "vvv")(
        visibility.reshape(SUBS, baselines),
        model_visibility.reshape(SUBS, baselines),
        keep_mask.reshape(1, baselines),
    )
    held = [own]
    step = slots // 2
    while step:
        held += [swap(array, step) for array in held]
        step //= 2
    first = first_station.reshape(1, baselines)
    second = second_station.reshape(1, baselines)
    products = shape((PRODS, tiles, LANES), f32)
    half = slots // 2
    near = [held[0], held[half]]
    hot, summed = call(
        lambda *refs: tables_kernel(len(near), *refs),
        [shape((LO, 2 * baselines), jnp.bfloat16), products],
        "vv" + "v" * len(near),
    )(first, second, *near)
    far = [array for index, array in enumerate(held) if index not in (0, half)]
    for array in far[: half - 1]:
        summed = call(more_kernel, products, "vv")(array, summed)
    rest = far[half - 1 :]
    gains, consensus, dual = (
        array.reshape(SUBS, stations) for array in (gains_in, consensus_in, dual_in)
    )
    gain_part, send = call(
        sweeps_kernel,
        [shape((SUBS, width), f32), shape((channels, 2 * SUBS, width), f32)],
        "ss" + "v" * (8 + len(rest)),
        [
            pltpu.VMEM((PRODS, tiles, LANES), f32),
            pltpu.VMEM((2, tiles * ROWS, LANES), f32),
            pltpu.VMEM((2, tiles * ROWS, LANES), f32),
            pltpu.VMEM((SPLITS * blocks * ROWS, 2 * baselines), jnp.bfloat16),
            pltpu.VMEM((SUBS, stations), f32),
        ],
    )(
        place,
        channel_index,
        first,
        second,
        gains,
        consensus,
        dual,
        penalty.reshape(1, stations),
        hot,
        summed,
        *rest,
    )
    parts = lax.all_to_all(send, "freq", 0, 0)
    factor = gram_cholesky(channels)
    consensus_out, dual_out = call(
        lambda *refs: fit_kernel(factor, *refs),
        [shape((SUBS, width), f32), shape((SUBS, width), f32)],
        "ssvvv",
    )(place, channel_index, parts, gain_part, dual)
    return tuple(array[None] for array in (gain_part, consensus_out, dual_out))


def solution(mesh):
    placed = (
        P("freq", "tm", None, None),
        P("freq", "tm", None, None),
        P("freq", "tm", None),
        P("freq", None, None),
        P("freq", None, None),
        P("freq", None, None),
        P(),
        P("freq"),
        P(),
        P(),
    )
    return jax.shard_map(
        shards,
        mesh=mesh,
        in_specs=placed,
        out_specs=(P("freq", None, "tm"), P("freq", None, "tm"), P("freq", None, "tm")),
        check_vma=False,
    )
```

time: 104 us -> 44.8 us (0.43)
  blocking collectives: 60.6 us -> 13.1 us
  matrix products: 29.2 us -> 0 us
  Pallas kernels: 0 us -> 19.2 us
  other arithmetic: 11.7 us -> 0 us
  waiting for transfers between devices: 0 us -> 6.51 us
  starting transfers between devices: 0 us -> 2.94 us
    psum x3 -> x0, blocking collectives: 60.6 us -> none  [the longest x1 37.5 us: shards(): moments = lax.psum(local_moments, 'freq')]
    dot_general x10 -> x0, matrix products: 27.7 us -> none  [the longest x2 8.11 us: normal_sums(): jnp.einsum('cjb,sb->cjs', term_second, second_hot, precision=lax.Precisio...]
    pallas_call x0 -> x5, Pallas kernels: none -> 19.2 us  [the longest x1 9.81 us: shards(): call(sweeps_kernel, [shape((SUBS, width), f32), shape((channels, 2 * SUBS...]
    all_to_all x0 -> x1, blocking collectives: none -> 13.1 us  [shards(): parts = lax.all_to_all(send, 'freq', 0, 0)]
    unnamed x57 -> x0, other arithmetic: 6.62 us -> none
    ppermute x0 -> x3, waiting for transfers between devices: none -> 6.51 us  [swap(): return lax.ppermute(array, 'tm', [(i, i ^ step) for i in range(slots)])]
    ppermute x0 -> x3, starting transfers between devices: none -> 2.94 us  [swap(): return lax.ppermute(array, 'tm', [(i, i ^ step) for i in range(slots)])]
    another operation x7 -> x0, other arithmetic: 2.14 us -> none  [the longest x3 1.08 us: poly_fit(): factor = jnp.linalg.cholesky(gram)]
  transfers between devices with their start and end apart: 0 -> 3, of which waited for: 0 -> 1; matrix products, arithmetic and copies ran while one was open for 0% -> 0% of each run, Pallas kernels for 0% -> 14%
where the time goes in v1:
time: 44.8 us; the launch traced here: 44.4 us
  Pallas kernels  19.2 us (43%)
  blocking collectives  13.1 us (29%)
  waiting for transfers between devices  6.51 us (15%)
  starting transfers between devices  2.94 us (7%)
  local copies, waits for them, and re-layouts  1.42 us (3%)
  between operations  1.31 us (3%)
    all_to_all x1, blocking collectives, shards(): parts = lax.all_to_all(send, 'freq', 0, 0)  13.1 us
    pallas_call x1, Pallas kernels, shards(): call(sweeps_kernel, [shape((SUBS, width), f32), shape((channels, 2 * SUBS...  9.81 us
    ppermute x3, waiting for transfers between devices, swap(): return lax.ppermute(array, 'tm', [(i, i ^ step) for i in range(slots)])  6.51 us
    pallas_call x1, Pallas kernels, shards(): call(lambda *refs: tables_kernel(len(near), *refs), [shape((LO, 2 * basel...  3.98 us
    ppermute x3, starting transfers between devices, swap(): return lax.ppermute(array, 'tm', [(i, i ^ step) for i in range(slots)])  2.94 us
    pallas_call x1, Pallas kernels, shards(): summed = call(more_kernel, products, 'vv')(array, summed)  2.27 us
    pallas_call x1, Pallas kernels, shards(): call(widen_kernel, shape((2 * tiles * SUBS, LANES), f32), 'vvv')  1.59 us
    pallas_call x1, Pallas kernels, shards(): call(lambda *refs: fit_kernel(factor, *refs), [shape((SUBS, width), f32),...  1.5 us
  transfers between devices with their start and end apart: 3, of which 1 were waited for; matrix products, arithmetic and copies ran while one was open for 0% of the time, Pallas kernels for 14%

profile of v1, /device:TPU:0, one launch (start us, length us, event | category | flops | bytes accessed | tf_op | source)
XLA Modules:
  0.0 44.4 jit_solution(15936527828970408745)
XLA Ops:
  0.6 1.6 %shard_map.121.refs_2_ = f32[512,128]{1,0:T(8,128)} custom-call(bf16[8,4096]{1,0:T(8,128)(2,1)} %bitcast.19, bf16[8,4096]{1,0:T(8,128)(2,1)} %bitcast.20, s32[1,4096]{1,0:T(1,128)} %bitcast.23), custom_call_target="tpu_custom_call" | custom-call | tf_op jit(solution)/shard_map/pallas_call | solution.py:368
  2.2 2.9 %collective-permute-start.1 = (f32[512,128]{1,0:T(8,128)}, f32[512,128]{1,0:T(8,128)S(1)}, u32[]{:S(2)}, u32[]{:S(2)}) collective-permute-start(f32[512,128]{1,0:T(8,128)} %shard_map.121.refs_2_), channel_id=1, source_target_pairs={{0,2},{1,3},{2,0},{3,1},{4,6},{5,7},{6,4},{7,5},{8,10},{9,11},{10,... | collective-permute-start | bytes 786440 | tf_op jit(solution)/shard_map/ppermute | solution.py:366
  5.2 0.0 collective-permute-start
  5.2 6.5 %collective-permute-done.1.slot_ref = f32[512,128]{1,0:T(8,128)S(1)} collective-permute-done((f32[512,128]{1,0:T(8,128)}, f32[512,128]{1,0:T(8,128)S(1)}, u32[]{:S(2)}, u32[]{:S(2)}) %collective-permute-start.1) | collective-permute-done | bytes 262176 | tf_op jit(solution)/shard_map/ppermute | solution.py:366
  11.7 0.0 copy-start
  11.7 0.0 collective-permute-start.2
  12.3 0.0 collective-permute-done.refs_3_
  12.3 0.0 copy-start.1
  12.4 0.7 %copy-done.1 = f32[512,128]{1,0:T(8,128)} copy-done((f32[512,128]{1,0:T(8,128)}, f32[512,128]{1,0:T(8,128)S(1)}, u32[]{:S(2)}) %copy-start.1) | copy-done | bytes 262168
  13.1 4.0 %shard_map.122 = (bf16[256,8192]{1,0:T(8,128)(2,1)}, f32[48,32,128]{2,1,0:T(8,128)}) custom-call(s32[1,4096]{1,0:T(1,128)} %bitcast.13, s32[1,4096]{1,0:T(1,128)} %bitcast.15, f32[512,128]{1,0:T(8,128)} %shard_map.121.refs_2_, f32[512,128]{1,0:T(8,128)} %copy-done.1), custom_call_target="tpu_custom_call" | custom-call | tf_op jit(solution)/shard_map/pallas_call | solution.py:383
  17.1 0.0 copy-done
  17.1 2.3 %shard_map.123.before_ref = f32[48,32,128]{2,1,0:T(8,128)} custom-call(f32[512,128]{1,0:T(8,128)} %copy-done, f32[48,32,128]{2,1,0:T(8,128)} %get-tuple-element.10.before_ref), custom_call_target="tpu_custom_call" | custom-call | tf_op jit(solution)/shard_map/pallas_call | solution.py:390
  19.3 0.0 collective-permute-done.2.rest_0_
  19.3 0.0 copy-start.2
  19.3 0.7 %copy-done.2 = f32[512,128]{1,0:T(8,128)} copy-done((f32[512,128]{1,0:T(8,128)}, f32[512,128]{1,0:T(8,128)S(1)}, u32[]{:S(2)}) %copy-start.2) | copy-done | bytes 262168
  20.0 9.8 %shard_map.124 = (f32[8,128]{1,0:T(8,128)}, f32[8,16,128]{2,1,0:T(8,128)}) custom-call(s32[1]{0:T(128)} %bitcast.place_ref.refs_0_, s32[1]{0:T(128)S(6)} %copy.13.channel_ref.refs_1_, s32[1,4096]{1,0:T(1,128)} %bitcast.14, s32[1,4096]{1,0:T(1,128)} %bitcast.16, f32[8,512]{1,0:T(8,128)} %bitcast.21, f32[8,512]{1,0:T(8,128)} %bitcast.22, f32[8,512]{1,0:T(8,128)} %bitcast.17, ...), custom_call_target="tpu_custom_call" | custom-call | tf_op jit(solution)/shard_map/pallas_call | solution.py:395
  29.8 13.1 %all_to_all.5.refs_2_ = f32[8,16,128]{2,1,0:T(8,128)} all-to-all(f32[8,16,128]{2,1,0:T(8,128)} %get-tuple-element.12), channel_id=1, replica_groups=mesh['freq'=8,'tm'=4] {'freq'}, dimensions={0} | all-to-all | bytes 131072 | tf_op jit(solution)/shard_map/all_to_all | solution.py:419
  42.9 1.5 %shard_map.125 = (f32[8,128]{1,0:T(8,128)}, f32[8,128]{1,0:T(8,128)}) custom-call(s32[1]{0:T(128)} %bitcast.place_ref.refs_0_, s32[1]{0:T(128)S(6)} %copy.13.channel_ref.refs_1_, f32[8,16,128]{2,1,0:T(8,128)} %all_to_all.5.refs_2_, f32[8,128]{1,0:T(8,128)} %get-tuple-element.11.refs_3_, f32[8,512]{1,0:T(8,128)} %bitcast.18), custom_call_target="tpu_custom_call" | custom-call | tf_op jit(solution)/shard_map/pallas_call | solution.py:421
Async XLA Ops:
  2.2 9.5 %collective-permute-start.1 = (f32[512,128]{1,0:T(8,128)}, f32[512,128]{1,0:T(8,128)S(1)}, u32[]{:S(2)}, u32[]{:S(2)}) collective-permute-start(f32[512,128]{1,0:T(8,128)} %shard_map.121.refs_2_), channel_id=1, source_target_pairs={{0,2},{1,3},{2,0},{3,1},{4,6},{5,7},{6,4},{7,5},{8,10},{9,11},{10,... | collective-permute-start | bytes 786440 | tf_op jit(solution)/shard_map/ppermute | solution.py:366
  5.2 7.2 %collective-permute-start = (f32[512,128]{1,0:T(8,128)}, f32[512,128]{1,0:T(8,128)S(1)}, u32[]{:S(2)}, u32[]{:S(2)}) collective-permute-start(f32[512,128]{1,0:T(8,128)} %shard_map.121.refs_2_), channel_id=1, source_target_pairs={{0,1},{1,0},{2,3},{3,2},{4,5},{5,4},{6,7},{7,6},{8,9},{9,8},{10,11... | collective-permute-start | bytes 786440 | tf_op jit(solution)/shard_map/ppermute | solution.py:366
  11.7 5.4 %copy-start = (f32[512,128]{1,0:T(8,128)}, f32[512,128]{1,0:T(8,128)S(1)}, u32[]{:S(2)}) copy-start(f32[512,128]{1,0:T(8,128)S(1)} %collective-permute-done.1.slot_ref) | copy-start | bytes 786436
  11.7 7.6 %collective-permute-start.2 = (f32[512,128]{1,0:T(8,128)S(1)}, f32[512,128]{1,0:T(8,128)S(1)}, u32[]{:S(2)}, u32[]{:S(2)}) collective-permute-start(f32[512,128]{1,0:T(8,128)S(1)} %collective-permute-done.1.slot_ref), channel_id=1, source_target_pairs={{0,1},{1,0},{2,3},{3,2},{4,5},{5,4},{6,7},{7,6},{8,9},{9,8},{10,11... | collective-permute-start | bytes 786440 | tf_op jit(solution)/shard_map/ppermute | solution.py:366
  12.3 0.7 %copy-start.1 = (f32[512,128]{1,0:T(8,128)}, f32[512,128]{1,0:T(8,128)S(1)}, u32[]{:S(2)}) copy-start(f32[512,128]{1,0:T(8,128)S(1)} %collective-permute-done.refs_3_) | copy-start | bytes 786436
  19.3 0.7 %copy-start.2 = (f32[512,128]{1,0:T(8,128)}, f32[512,128]{1,0:T(8,128)S(1)}, u32[]{:S(2)}) copy-start(f32[512,128]{1,0:T(8,128)S(1)} %collective-permute-done.2.rest_0_) | copy-start | bytes 786436

commit v2 on v1

v2 whole, which is shorter than its diff:
```python
import jax
import jax.numpy as jnp
import numpy as np
from jax import lax
from jax.experimental import pallas as pl
from jax.experimental.pallas import tpu as pltpu
from jax.sharding import PartitionSpec as P

SWEEPS = 2
LANES = 128
SUBS = 8
PRODS = 48
TERMS = 24
PACK = 16
F32 = jnp.float32
BF16 = jnp.bfloat16


def mul_conj(a, b):
    return (a[0] * b[0] + a[1] * b[1], a[1] * b[0] - a[0] * b[1])


def copy_in(pairs, sem):
    copies = [
        pltpu.make_async_copy(source, target, sem.at[index])
        for index, (source, target) in enumerate(pairs)
    ]
    for copy in copies:
        copy.start()
    return copies


def widen_kernel(vis_hbm, model_hbm, keep_hbm, out_ref, vis_ref, model_ref, keep_ref, sem):
    copies = copy_in(
        [(vis_hbm, vis_ref), (keep_hbm, keep_ref), (model_hbm, model_ref)], sem
    )
    tiles = vis_ref.shape[1] // LANES
    copies[0].wait()
    for tile in range(tiles):
        lanes = pl.ds(tile * LANES, LANES)
        out_ref[pl.ds(tile * SUBS, SUBS), :] = vis_ref[:, lanes].astype(F32)
    copies[1].wait()
    copies[2].wait()
    for tile in range(tiles):
        lanes = pl.ds(tile * LANES, LANES)
        out_ref[pl.ds((tiles + tile) * SUBS, SUBS), :] = model_ref[:, lanes].astype(
            F32
        ) * keep_ref[:, lanes].astype(F32)


def slot_products(slot_ref, group, tiles):
    def load(part, component):
        start = (part * tiles + group * SUBS) * SUBS + component
        return slot_ref[pl.ds(start, SUBS, stride=SUBS), :]

    seen = [(load(0, 2 * e), load(0, 2 * e + 1)) for e in range(4)]
    model = [(load(1, 2 * e), load(1, 2 * e + 1)) for e in range(4)]
    rows = []
    for v in range(4):
        for m in range(4):
            rows.extend(mul_conj(seen[v], model[m]))
    rows.extend(entry[0] * entry[0] + entry[1] * entry[1] for entry in model)
    for left, right in ((0, 1), (2, 3), (0, 2), (1, 3)):
        rows.extend(mul_conj(model[left], model[right]))
    a = mul_conj(model[0], model[3])
    b = mul_conj(model[1], model[2])
    rows.extend((a[0] + b[0], a[0] - b[0], a[1] + b[1], a[1] - b[1]))
    return rows


def add_products(slot_refs, before_ref, out_ref):
    tiles = slot_refs[0].shape[0] // (2 * SUBS)
    for group in range(tiles // SUBS):
        at = pl.ds(group * SUBS, SUBS)
        total = None
        for slot_ref in slot_refs:
            rows = slot_products(slot_ref, group, tiles)
            total = rows if total is None else [x + y for x, y in zip(total, rows)]
        for index, row in enumerate(total):
            if before_ref is not None:
                row = row + before_ref[index, at, :]
            out_ref[index, at, :] = row


def gather_gains(gains, station_refs, seen_ref):
    blocks = gains[0].shape[0]
    tables = [
        [jnp.broadcast_to(gain[h : h + 1], (SUBS, LANES)) for h in range(blocks)]
        for gain in gains
    ]
    for part, station_ref in enumerate(station_refs):
        for group in range(station_ref.shape[0] // SUBS):
            at = pl.ds(group * SUBS, SUBS)
            station = station_ref[at, :]
            offset, block = station & (LANES - 1), station >> 7
            inside = [block == h for h in range(blocks)]
            for j, table in enumerate(tables):
                value = None
                for h in range(blocks):
                    found = jnp.take_along_axis(
                        table[h], offset, axis=1, mode="promise_in_bounds"
                    )
                    value = found if value is None else jnp.where(inside[h], found, value)
                seen_ref[part, j, at, :] = value


def tables_kernel(count, *refs):
    slot_refs, channel_ref = refs[:count], refs[count]
    station_hbms, array_hbms = refs[count + 1 : count + 3], refs[count + 3 : count + 7]
    outs = refs[count + 7 : -5]
    hot_ref, mask_ref, prod_ref, seen_ref, state_ref, own_ref, first_ref, second_ref = outs
    gains_ref, consensus_ref, dual_ref, penalty_ref, sem = refs[-5:]
    station_refs = (first_ref, second_ref)
    copies = copy_in(
        list(
            zip(
                station_hbms + array_hbms,
                station_refs + (gains_ref, consensus_ref, dual_ref, penalty_ref),
            )
        ),
        sem,
    )
    add_products(slot_refs, None, prod_ref)
    for copy in copies:
        copy.wait()
    tiles = first_ref.shape[0]
    blocks = gains_ref.shape[1] // LANES
    for h in range(blocks):
        lanes = pl.ds(h * LANES, LANES)
        penalty = penalty_ref[:, lanes]
        gain = gains_ref[:, lanes]
        target = penalty * (consensus_ref[:, lanes] - dual_ref[:, lanes])
        for j in range(SUBS):
            state_ref[pl.ds(j * SUBS + h, 1), :] = gain[j : j + 1]
            state_ref[pl.ds((SUBS + j) * SUBS + h, 1), :] = target[j : j + 1]
        state_ref[pl.ds(2 * SUBS * SUBS + h, 1), :] = penalty
    gains = [state_ref[pl.ds(j * SUBS, blocks), :] for j in range(SUBS)]
    gather_gains(gains, station_refs, seen_ref)
    place = lax.axis_index("tm")
    own_ref[:SUBS, :] = dual_ref[:, pl.ds(pl.multiple_of(place * LANES, LANES), LANES)]
    own_ref[SUBS:, :] = jnp.full((SUBS, LANES), channel_ref[0].astype(F32))
    row = lax.broadcasted_iota(jnp.int32, (LANES, LANES), 0)
    lower = lax.broadcasted_iota(jnp.int32, (PACK, LANES), 0) >= SUBS
    for part, station_ref in enumerate(station_refs):
        for tile in range(tiles):
            station = station_ref[pl.ds(tile, 1), :]
            offset, block = station & (LANES - 1), station >> 7
            lanes = pl.ds((part * tiles + tile) * LANES, LANES)
            hot_ref[:, lanes] = jnp.where(row == offset, 1.0, 0.0).astype(BF16)
            wide = jnp.broadcast_to(block, (PACK, LANES))
            for h in range(blocks):
                mask_ref[pl.ds(h * PACK, PACK), lanes] = jnp.where(wide == h, 1.0, 0.0).astype(
                    BF16
                )
            for pair in range(blocks // 2):
                mine = jnp.where(lower, 2 * pair + 1, 2 * pair)
                mask_ref[pl.ds((blocks + pair) * PACK, PACK), lanes] = jnp.where(
                    wide == mine, 1.0, 0.0
                ).astype(BF16)


def more_kernel(slot_ref, before_ref, out_ref):
    add_products([slot_ref], before_ref, out_ref)


def gram(gain):
    entry = [(gain[2 * e], gain[2 * e + 1]) for e in range(4)]
    h00 = sum(part * part for part in entry[0] + entry[2])
    h11 = sum(part * part for part in entry[1] + entry[3])
    top = mul_conj(entry[1], entry[0])
    low = mul_conj(entry[3], entry[2])
    return h00, h11, top[0] + low[0], top[1] + low[1]


def baseline_terms(prod, gain_second, gain_first):
    def num(gain, swap):
        out = []
        for i in range(2):
            for l in range(2):
                real = imag = None
                for j in range(2):
                    for k in range(2):
                        if swap:
                            index = 4 * (2 * j + i) + 2 * k + l
                        else:
                            index = 4 * (2 * i + j) + 2 * l + k
                        tr, ti = prod(2 * index), prod(2 * index + 1)
                        gr, gi = gain[2 * (2 * j + k)], gain[2 * (2 * j + k) + 1]
                        if swap:
                            addr, addi = tr * gr + ti * gi, tr * gi - ti * gr
                        else:
                            addr, addi = tr * gr - ti * gi, tr * gi + ti * gr
                        real = addr if real is None else real + addr
                        imag = addi if imag is None else imag + addi
                out.extend((real, imag))
        return out

    n00, n01, n10, n11, pr, pi, qr, qi, rr, ri, sr, si, apr, amr, api, ami = (
        prod(32 + index) for index in range(16)
    )
    h00, h11, hr, hi = gram(gain_second)
    den_first = [
        n00 * h00 + n01 * h11 + 2.0 * (pr * hr - pi * hi),
        n10 * h00 + n11 * h11 + 2.0 * (qr * hr - qi * hi),
        rr * h00 + sr * h11 + apr * hr - ami * hi,
        ri * h00 + si * h11 + api * hr + amr * hi,
    ]
    h00, h11, hr, hi = gram(gain_first)
    den_second = [
        n00 * h00 + n10 * h11 + 2.0 * (rr * hr + ri * hi),
        n01 * h00 + n11 * h11 + 2.0 * (sr * hr + si * hi),
        pr * h00 + qr * h11 + apr * hr + api * hi,
        amr * hi - pi * h00 - qi * h11 - ami * hr,
    ]
    return num(gain_second, False) + den_first, num(gain_first, True) + den_second


def store_terms(prod_ref, seen_ref, term_ref):
    for group in range(prod_ref.shape[1] // SUBS):
        at = pl.ds(group * SUBS, SUBS)
        start = group * SUBS * TERMS
        gain_first, gain_second = (
            [seen_ref[part, j, at, :] for j in range(SUBS)] for part in range(2)
        )
        both = baseline_terms(lambda index: prod_ref[index, at, :], gain_second, gain_first)
        for part, rows in enumerate(both):
            for j, row in enumerate(rows):
                where, apart = (start + j, 8) if j < 8 else (start + 8 + j, 4)
                high = row.astype(BF16).astype(F32)
                term_ref[part, pl.ds(where, SUBS, stride=TERMS), :] = high
                term_ref[part, pl.ds(where + apart, SUBS, stride=TERMS), :] = row - high


def scatter_terms(term_ref, hot_ref, mask_ref, chunk):
    rows = mask_ref.shape[0]
    tiles = term_ref.shape[1] // TERMS
    blocks = rows * 2 // (3 * PACK)
    total = None
    for part in range(2):
        for start in range(0, tiles, chunk):
            columns = []
            for tile in range(start, start + chunk):
                lanes = pl.ds((part * tiles + tile) * LANES, LANES)
                num = term_ref[part, pl.ds(tile * TERMS, PACK), :].astype(BF16)
                den = term_ref[part, pl.ds(tile * TERMS + PACK, SUBS), :]
                den = jnp.concatenate([den, den], axis=0).astype(BF16)
                column = [
                    mask_ref[pl.ds(h * PACK, PACK), lanes] * (num if h < blocks else den)
                    for h in range(rows // PACK)
                ]
                columns.append(jnp.concatenate(column, axis=0))
            lanes = pl.ds((part * tiles + start) * LANES, chunk * LANES)
            add = lax.dot_general(
                jnp.concatenate(columns, axis=1),
                hot_ref[:, lanes],
                (((1,), (1,)), ((), ())),
                preferred_element_type=F32,
            )
            total = add if total is None else total + add
    return total


def solve(num, den, gain, target, penalty):
    rhs = [tuple(num[2 * e + part] + target[2 * e + part] for part in range(2)) for e in range(4)]
    r00, r11, r01 = den[0] + penalty, den[1] + penalty, (den[2], den[3])
    scale = 0.5 / (r00 * r11 - (r01[0] * r01[0] + r01[1] * r01[1]))
    out = []
    for i in range(2):
        a, b = rhs[2 * i], rhs[2 * i + 1]
        cross = mul_conj(b, r01)
        out.extend((a[part] * r11 - cross[part]) * scale for part in range(2))
        out.append((b[0] * r00 - (a[0] * r01[0] - a[1] * r01[1])) * scale)
        out.append((b[1] * r00 - (a[0] * r01[1] + a[1] * r01[0])) * scale)
    return [value + 0.5 * old for value, old in zip(out, gain)]


def sweeps_kernel(*refs):
    hot_ref, mask_ref, before_ref, found_ref, state_ref, own_ref, first_ref, second_ref = refs[:8]
    slot_refs = refs[8:-6]
    gain_out_ref, send_ref, prod_ref, seen_ref, term_ref, total_ref = refs[-6:]
    blocks = mask_ref.shape[0] * 2 // (3 * PACK)
    add_products(slot_refs, before_ref, prod_ref)
    gains = [state_ref[pl.ds(j * SUBS, blocks), :] for j in range(SUBS)]
    target = [state_ref[pl.ds((SUBS + j) * SUBS, blocks), :] for j in range(SUBS)]
    penalty = state_ref[pl.ds(2 * SUBS * SUBS, blocks), :]
    for sweep in range(SWEEPS):
        if sweep:
            gather_gains(gains, (first_ref, second_ref), seen_ref)
        store_terms(prod_ref, found_ref if sweep == 0 else seen_ref, term_ref)
        total_ref[...] = scatter_terms(term_ref, hot_ref, mask_ref, 4)

        def rows(start, stride):
            return total_ref[pl.ds(start, blocks, stride=stride), :]

        num = [rows(j, PACK) + rows(SUBS + j, PACK) for j in range(SUBS)]
        den = [
            rows(blocks * PACK + j, SUBS) + rows(blocks * PACK + 4 + j, SUBS) for j in range(4)
        ]
        gains = solve(num, den, gains, target, penalty)
    for j in range(SUBS):
        total_ref[pl.ds(j, blocks, stride=SUBS), :] = gains[j]
    place = lax.axis_index("tm")
    part = total_ref[pl.ds(pl.multiple_of(place * SUBS, SUBS), SUBS), :]
    gain_out_ref[...] = part
    combined, mark = part + own_ref[:SUBS, :], own_ref[SUBS:, :]
    for channel in range(send_ref.shape[0]):
        send_ref[channel, :SUBS, :] = combined
        send_ref[channel, SUBS:, :] = mark


def legendre(position):
    square = position * position
    return [None, position, 1.5 * square - 0.5, (2.5 * square - 1.5) * position]


def fit_kernel(
    gram_factor, parts_ref, send_ref, consensus_hbm, dual_hbm, consensus_ref, dual_ref, sem
):
    channels = parts_ref.shape[0]
    scale = float(channels) - 1.0

    def basis(channel):
        return legendre(2.0 * channel / scale - 1.0)

    moments = [None] * 4
    for channel in range(channels):
        value = parts_ref[channel, :SUBS, :]
        for k, weight in enumerate(basis(parts_ref[channel, SUBS:, :])):
            add = value if weight is None else weight * value
            moments[k] = add if moments[k] is None else moments[k] + add
    middle = []
    for k in range(4):
        rest = moments[k]
        for earlier in range(k):
            rest = rest - gram_factor[k][earlier] * middle[earlier]
        middle.append(rest * (1.0 / gram_factor[k][k]))
    coeffs = [None] * 4
    for k in reversed(range(4)):
        rest = middle[k]
        for later in range(k + 1, 4):
            rest = rest - gram_factor[later][k] * coeffs[later]
        coeffs[k] = rest * (1.0 / gram_factor[k][k])
    own = basis(send_ref[0, SUBS:, :])
    fitted = coeffs[0]
    for k in range(1, 4):
        fitted = fitted + own[k] * coeffs[k]
    consensus_ref[...] = fitted
    dual_ref[...] = send_ref[0, :SUBS, :] - fitted
    for copy in copy_in([(consensus_ref, consensus_hbm), (dual_ref, dual_hbm)], sem):
        copy.wait()


def gram_cholesky(channels):
    x = 2.0 * np.arange(channels, dtype=np.float64) / (channels - 1.0) - 1.0
    basis = np.stack([np.ones_like(x), x, 1.5 * x * x - 0.5, (2.5 * x * x - 1.5) * x], -1)
    factor = np.linalg.cholesky(basis.T @ basis)
    return [[float(value) for value in row] for row in factor]


SPACES = {"s": pltpu.SMEM, "v": pltpu.VMEM, "h": pltpu.HBM}


def call(kernel, shapes, spaces, scratch=(), limit=8, micros=0):
    cost = pl.CostEstimate(
        flops=int(micros * 1.0e9), transcendentals=0, bytes_accessed=int(micros * 3.0e6)
    )
    run = pl.pallas_call(
        kernel,
        out_shape=shapes,
        in_specs=[pl.BlockSpec(memory_space=SPACES[space]) for space in spaces],
        out_specs=[pl.BlockSpec(memory_space=shape.memory_space) for shape in shapes],
        scratch_shapes=list(scratch),
        compiler_params=pltpu.CompilerParams(vmem_limit_bytes=limit << 20),
        cost_estimate=cost if micros else None,
    )

    def placed(*args):
        return run(
            *(
                arg if space == "s" else pltpu.with_memory_space_constraint(arg, SPACES[space])
                for arg, space in zip(args, spaces, strict=True)
            )
        )

    return placed


def shards(
    visibility,
    model_visibility,
    keep_mask,
    gains_in,
    consensus_in,
    dual_in,
    penalty,
    channel_index,
    first_station,
    second_station,
):
    baselines = visibility.shape[3]
    stations = gains_in.shape[2]
    slots = lax.axis_size("tm")
    channels = lax.axis_size("freq")
    tiles = baselines // LANES
    blocks = stations // LANES
    assert blocks == slots and blocks % 2 == 0 and channel_index.shape == (1,)
    vmem = pltpu.VMEM

    def swap(array, step):
        return lax.ppermute(array, "tm", [(i, i ^ step) for i in range(slots)])

    (own,) = call(
        widen_kernel,
        [vmem((2 * tiles * SUBS, LANES), F32)],
        "hhh",
        [
            vmem((SUBS, baselines), BF16),
            vmem((SUBS, baselines), BF16),
            vmem((1, baselines), jnp.int32),
            pltpu.SemaphoreType.DMA((3,)),
        ],
    )(
        visibility.reshape(SUBS, baselines),
        model_visibility.reshape(SUBS, baselines),
        keep_mask.reshape(1, baselines),
    )
    far = []
    step = slots // 2
    while step > 1:
        far += [swap(array, step) for array in [own, *far]]
        step //= 2
    near = [own, swap(own, 1)]
    gains, consensus, dual = (
        array.reshape(SUBS, stations) for array in (gains_in, consensus_in, dual_in)
    )
    products = vmem((PRODS, tiles, LANES), F32)
    seen = vmem((2, SUBS, tiles, LANES), F32)
    station = vmem((tiles, LANES), jnp.int32)
    wide = vmem((SUBS, stations), F32)
    tables = call(
        lambda *refs: tables_kernel(len(near), *refs),
        [
            vmem((LANES, 2 * baselines), BF16),
            vmem((blocks * 3 * PACK // 2, 2 * baselines), BF16),
            products,
            seen,
            vmem(((2 * SUBS + 1) * SUBS, LANES), F32),
            vmem((2 * SUBS, LANES), F32),
            station,
            station,
        ],
        "v" * len(near) + "shhhhhh",
        [wide, wide, wide, vmem((1, stations), F32), pltpu.SemaphoreType.DMA((6,))],
        limit=16,
        micros=4,
    )(
        *near,
        channel_index,
        first_station.reshape(tiles, LANES),
        second_station.reshape(tiles, LANES),
        gains,
        consensus,
        dual,
        penalty.reshape(1, stations),
    )
    hot, mask, summed, found, state, own, first, second = tables
    far, state = lax.optimization_barrier((far, state))
    last = [swap(array, 1) for array in far]
    for array in far:
        (summed,) = call(more_kernel, [products], "vv", micros=1)(array, summed)
    gain_part, send = call(
        sweeps_kernel,
        [vmem((SUBS, LANES), F32), vmem((channels, 2 * SUBS, LANES), F32)],
        "v" * (8 + len(last)),
        [
            products,
            seen,
            vmem((2, tiles * TERMS, LANES), F32),
            vmem((blocks * 3 * PACK // 2, LANES), F32),
        ],
        limit=16,
    )(hot, mask, summed, found, state, own, first, second, *last)
    parts = lax.all_to_all(send, "freq", 0, 0)
    factor = gram_cholesky(channels)
    out = vmem((SUBS, LANES), F32)
    consensus_out, dual_out = call(
        lambda *refs: fit_kernel(factor, *refs),
        [pltpu.HBM(out.shape, F32)] * 2,
        "vv",
        [out, out, pltpu.SemaphoreType.DMA((2,))],
    )(parts, send)
    return tuple(array[None] for array in (gain_part, consensus_out, dual_out))


def solution(mesh):
    placed = (
        P("freq", "tm", None, None),
        P("freq", "tm", None, None),
        P("freq", "tm", None),
        P("freq", None, None),
        P("freq", None, None),
        P("freq", None, None),
        P(),
        P("freq"),
        P(),
        P(),
    )
    return jax.shard_map(
        shards,
        mesh=mesh,
        in_specs=placed,
        out_specs=(P("freq", None, "tm"), P("freq", None, "tm"), P("freq", None, "tm")),
        check_vma=False,
    )
```

time: 44.8 us -> 31.5 us (0.70)
  blocking collectives: 13.1 us -> 0 us
  Pallas kernels: 19.2 us -> 8.17 us
  starting transfers between devices: 2.94 us -> 9.18 us
  waiting for transfers between devices: 6.51 us -> 11.9 us
  local copies, waits for them, and re-layouts: 1.42 us -> 0.59 us
    all_to_all x1 -> x0, blocking collectives: 13.1 us -> none  [shards(): parts = lax.all_to_all(send, 'freq', 0, 0)]
    pallas_call x5, Pallas kernels: 19.2 us -> 8.17 us  [placed(): run(*(arg if space == 's' else pltpu.with_memory_space_constraint(arg, SP...]
    all_to_all x0 -> x1, waiting for transfers between devices: none -> 6.31 us  [shards(): parts = lax.all_to_all(send, 'freq', 0, 0)]
    all_to_all x0 -> x1, starting transfers between devices: none -> 6.1 us  [shards(): parts = lax.all_to_all(send, 'freq', 0, 0)]
    ppermute x3, waiting for transfers between devices: 6.51 us -> 5.59 us  [swap(): return lax.ppermute(array, 'tm', [(i, i ^ step) for i in range(slots)])]
    unnamed x6 -> x1, local copies, waits for them, and re-layouts: 1.42 us -> 0.59 us
  transfers between devices with their start and end apart: 3 -> 4, of which waited for: 1 -> 3; matrix products, arithmetic and copies ran while one was open for 0% -> 2% of each run, Pallas kernels for 14% -> 7%
where the time goes in v2:
time: 31.5 us; the launch traced here: 31.2 us
  waiting for transfers between devices  11.9 us (38%)
  starting transfers between devices  9.18 us (29%)
  Pallas kernels  8.17 us (26%)
  between operations  1.32 us (4%)
  local copies, waits for them, and re-layouts  0.59 us (2%)
    pallas_call x5, Pallas kernels, placed(): run(*(arg if space == 's' else pltpu.with_memory_space_constraint(arg, SP...  8.17 us
    all_to_all x1, waiting for transfers between devices, shards(): parts = lax.all_to_all(send, 'freq', 0, 0)  6.31 us
    all_to_all x1, starting transfers between devices, shards(): parts = lax.all_to_all(send, 'freq', 0, 0)  6.1 us
    ppermute x3, waiting for transfers between devices, swap(): return lax.ppermute(array, 'tm', [(i, i ^ step) for i in range(slots)])  5.59 us
    ppermute x3, starting transfers between devices, swap(): return lax.ppermute(array, 'tm', [(i, i ^ step) for i in range(slots)])  3.08 us
  transfers between devices with their start and end apart: 4, of which 3 were waited for; matrix products, arithmetic and copies ran while one was open for 2% of the time, Pallas kernels for 7%

profile of v2, /device:TPU:0, one launch (start us, length us, event | category | flops | bytes accessed | tf_op | source)
XLA Modules:
  0.0 31.2 jit_solution(14009252053068045335)
XLA Ops:
  0.6 0.9 %shard_map.121.refs_0_ = f32[512,128]{1,0:T(8,128)S(1)} custom-call(bf16[8,4096]{1,0:T(8,128)(2,1)} %bitcast.13, bf16[8,4096]{1,0:T(8,128)(2,1)} %bitcast.14, s32[1,4096]{1,0:T(1,128)} %bitcast.15), custom_call_target="tpu_custom_call" | custom-call | tf_op jit(solution)/shard_map/pallas_call | solution.py:378
  1.6 0.5 %collective-permute-start = (f32[512,128]{1,0:T(8,128)S(1)}, f32[512,128]{1,0:T(8,128)S(1)}, u32[]{:S(2)}, u32[]{:S(2)}) collective-permute-start(f32[512,128]{1,0:T(8,128)S(1)} %shard_map.121.refs_0_), channel_id=1, source_target_pairs={{0,1},{1,0},{2,3},{3,2},{4,5},{5,4},{6,7},{7,6},{8,9},{9,8},{10,11... | collective-permute-start | bytes 786440 | tf_op jit(solution)/shard_map/ppermute | solution.py:410
  2.1 2.6 %collective-permute-start.1 = (f32[512,128]{1,0:T(8,128)S(1)}, f32[512,128]{1,0:T(8,128)S(1)}, u32[]{:S(2)}, u32[]{:S(2)}) collective-permute-start(f32[512,128]{1,0:T(8,128)S(1)} %shard_map.121.refs_0_), channel_id=1, source_target_pairs={{0,2},{1,3},{2,0},{3,1},{4,6},{5,7},{6,4},{7,5},{8,10},{9,11},{10,... | collective-permute-start | bytes 786440 | tf_op jit(solution)/shard_map/ppermute | solution.py:410
  5.3 0.0 collective-permute-done.refs_1_
  5.3 2.0 %shard_map.122 = (bf16[128,8192]{1,0:T(8,128)(2,1)S(1)}, bf16[96,8192]{1,0:T(8,128)(2,1)S(1)}, f32[48,32,128]{2,1,0:T(8,128)S(1)}, f32[2,8,32,128]{3,2,1,0:T(8,1...) custom-call(f32[512,128]{1,0:T(8,128)S(1)} %shard_map.121.refs_0_, ...), custom_call_target="tpu_custom_call" | custom-call | flops 4000000000 | bytes 12000000 | tf_op jit(solution)/shard_map/pallas_call | solution.py:378
  7.4 4.2 %collective-permute-done.1.slot_ref = f32[512,128]{1,0:T(8,128)S(1)} collective-permute-done((f32[512,128]{1,0:T(8,128)S(1)}, f32[512,128]{1,0:T(8,128)S(1)}, u32[]{:S(2)}, u32[]{:S(2)}) %collective-permute-start.1) | collective-permute-done | bytes 262176 | tf_op jit(solution)/shard_map/ppermute | solution.py:410
  11.6 0.0 collective-permute-start.2
  11.6 0.1 shard_map.123.refs_2_
  11.7 1.4 %collective-permute-done.2.refs_8_ = f32[512,128]{1,0:T(8,128)S(1)} collective-permute-done((f32[512,128]{1,0:T(8,128)S(1)}, f32[512,128]{1,0:T(8,128)S(1)}, u32[]{:S(2)}, u32[]{:S(2)}) %collective-permute-start.2) | collective-permute-done | bytes 262176 | tf_op jit(solution)/shard_map/ppermute | solution.py:410
  13.1 3.6 %shard_map.124 = (f32[8,128]{1,0:T(8,128)S(1)}, f32[8,16,128]{2,1,0:T(8,128)}) custom-call(bf16[128,8192]{1,0:T(8,128)(2,1)S(1)} %get-tuple-element.17.refs_0_, bf16[96,8192]{1,0:T(8,128)(2,1)S(1)} %get-tuple-element.18.refs_1_, f32[48,32,128]{2,1,0:T(8,128)S(1)} %shard_map.123.refs_2_, f32[2,8,32,128]{3,2,1,0:T(8,128)S(1)} %get-tuple-element.22.refs_3_, ...), custom_call_target="tpu_custom_call" | custom-call | tf_op jit(solution)/shard_map/pallas_call | solution.py:378
  16.7 6.1 %all-to-all-start = ((f32[8,16,128]{2,1,0:T(8,128)}), f32[8,16,128]{2,1,0:T(8,128)S(1)}, u32[]{:S(2)}, u32[]{:S(2)}) async-start(f32[8,16,128]{2,1,0:T(8,128)} %get-tuple-element.28.refs_1_), calls=%async_computation | async-start | bytes 131072 | tf_op jit(solution)/shard_map/all_to_all | solution.py:483
  22.8 0.6 %copy.13 = f32[1,8,128]{2,1,0:T(8,128)} copy(f32[1,8,128]{2,1,0:T(8,128)S(1)} %bitcast.12) | data formatting | bytes 8192
  23.3 6.3 %all-to-all-done.refs_0_ = f32[8,16,128]{2,1,0:T(8,128)S(1)} async-done(((f32[8,16,128]{2,1,0:T(8,128)}), f32[8,16,128]{2,1,0:T(8,128)S(1)}, u32[]{:S(2)}, u32[]{:S(2)}) %all-to-all-start) | async-done | bytes 65568 | tf_op jit(solution)/shard_map/all_to_all | solution.py:483
  29.7 1.5 %shard_map.125 = (f32[8,128]{1,0:T(8,128)}, f32[8,128]{1,0:T(8,128)}) custom-call(f32[8,16,128]{2,1,0:T(8,128)S(1)} %all-to-all-done.refs_0_, f32[8,16,128]{2,1,0:T(8,128)} %get-tuple-element.28.refs_1_), custom_call_target="tpu_custom_call" | custom-call | tf_op jit(solution)/shard_map/pallas_call | solution.py:378
Async XLA Ops:
  1.6 3.7 %collective-permute-start = (f32[512,128]{1,0:T(8,128)S(1)}, f32[512,128]{1,0:T(8,128)S(1)}, u32[]{:S(2)}, u32[]{:S(2)}) collective-permute-start(f32[512,128]{1,0:T(8,128)S(1)} %shard_map.121.refs_0_), channel_id=1, source_target_pairs={{0,1},{1,0},{2,3},{3,2},{4,5},{5,4},{6,7},{7,6},{8,9},{9,8},{10,11... | collective-permute-start | bytes 786440 | tf_op jit(solution)/shard_map/ppermute | solution.py:410
  2.1 9.5 %collective-permute-start.1 = (f32[512,128]{1,0:T(8,128)S(1)}, f32[512,128]{1,0:T(8,128)S(1)}, u32[]{:S(2)}, u32[]{:S(2)}) collective-permute-start(f32[512,128]{1,0:T(8,128)S(1)} %shard_map.121.refs_0_), channel_id=1, source_target_pairs={{0,2},{1,3},{2,0},{3,1},{4,6},{5,7},{6,4},{7,5},{8,10},{9,11},{10,... | collective-permute-start | bytes 786440 | tf_op jit(solution)/shard_map/ppermute | solution.py:410
  11.6 1.5 %collective-permute-start.2 = (f32[512,128]{1,0:T(8,128)S(1)}, f32[512,128]{1,0:T(8,128)S(1)}, u32[]{:S(2)}, u32[]{:S(2)}) collective-permute-start(f32[512,128]{1,0:T(8,128)S(1)} %collective-permute-done.1.slot_ref), channel_id=1, source_target_pairs={{0,1},{1,0},{2,3},{3,2},{4,5},{5,4},{6,7},{7,6},{8,9},{9,8},{10,11... | collective-permute-start | bytes 786440 | tf_op jit(solution)/shard_map/ppermute | solution.py:410
  16.7 13.0 %all-to-all-start = ((f32[8,16,128]{2,1,0:T(8,128)}), f32[8,16,128]{2,1,0:T(8,128)S(1)}, u32[]{:S(2)}, u32[]{:S(2)}) async-start(f32[8,16,128]{2,1,0:T(8,128)} %get-tuple-element.28.refs_1_), calls=%async_computation | async-start | bytes 131072 | tf_op jit(solution)/shard_map/all_to_all | solution.py:483

commit v3 on v2

--- a/solution.py
+++ b/solution.py
@@ -68,40 +68,39 @@
     return rows
 
 
-def add_products(slot_refs, before_ref, out_ref):
+def add_products(slot_refs, before_ref, out_ref, group):
     tiles = slot_refs[0].shape[0] // (2 * SUBS)
-    for group in range(tiles // SUBS):
-        at = pl.ds(group * SUBS, SUBS)
-        total = None
-        for slot_ref in slot_refs:
-            rows = slot_products(slot_ref, group, tiles)
-            total = rows if total is None else [x + y for x, y in zip(total, rows)]
-        for index, row in enumerate(total):
-            if before_ref is not None:
-                row = row + before_ref[index, at, :]
-            out_ref[index, at, :] = row
-
-
-def gather_gains(gains, station_refs, seen_ref):
-    blocks = gains[0].shape[0]
-    tables = [
-        [jnp.broadcast_to(gain[h : h + 1], (SUBS, LANES)) for h in range(blocks)]
+    at = pl.ds(group * SUBS, SUBS)
+    total = None
+    for slot_ref in slot_refs:
+        rows = slot_products(slot_ref, group, tiles)
+        total = rows if total is None else [x + y for x, y in zip(total, rows)]
+    for index, row in enumerate(total):
+        if before_ref is not None:
+            row = row + before_ref[index, at, :]
+            total[index] = row
+        out_ref[index, at, :] = row
+    return total
+
+
+def gain_tables(gains):
+    return [
+        [jnp.broadcast_to(gain[h : h + 1], (SUBS, LANES)) for h in range(gain.shape[0])]
         for gain in gains
     ]
-    for part, station_ref in enumerate(station_refs):
-        for group in range(station_ref.shape[0] // SUBS):
-            at = pl.ds(group * SUBS, SUBS)
-            station = station_ref[at, :]
-            offset, block = station & (LANES - 1), station >> 7
-            inside = [block == h for h in range(blocks)]
-            for j, table in enumerate(tables):
-                value = None
-                for h in range(blocks):
-                    found = jnp.take_along_axis(
-                        table[h], offset, axis=1, mode="promise_in_bounds"
-                    )
-                    value = found if value is None else jnp.where(inside[h], found, value)
-                seen_ref[part, j, at, :] = value
+
+
+def gather_gains(tables, station_ref, group):
+    station = station_ref[pl.ds(group * SUBS, SUBS), :]
+    offset, block = station & (LANES - 1), station >> 7
+    values = []
+    for table in tables:
+        value = None
+        for h, row in enumerate(table):
+            found = jnp.take_along_axis(row, offset, axis=1, mode="promise_in_bounds")
+            value = found if value is None else jnp.where(block == h, found, value)
+        values.append(value)
+    return values
 
 
 def tables_kernel(count, *refs):
@@ -120,10 +119,11 @@
         ),
         sem,
     )
-    add_products(slot_refs, None, prod_ref)
+    tiles = first_ref.shape[0]
+    for group in range(tiles // SUBS):
+        add_products(slot_refs, None, prod_ref, group)
     for copy in copies:
         copy.wait()
-    tiles = first_ref.shape[0]
     blocks = gains_ref.shape[1] // LANES
     for h in range(blocks):
         lanes = pl.ds(h * LANES, LANES)
@@ -135,7 +135,11 @@
             state_ref[pl.ds((SUBS + j) * SUBS + h, 1), :] = target[j : j + 1]
         state_ref[pl.ds(2 * SUBS * SUBS + h, 1), :] = penalty
     gains = [state_ref[pl.ds(j * SUBS, blocks), :] for j in range(SUBS)]
-    gather_gains(gains, station_refs, seen_ref)
+    tables = gain_tables(gains)
+    for part, station_ref in enumerate(station_refs):
+        for group in range(tiles // SUBS):
+            for j, value in enumerate(gather_gains(tables, station_ref, group)):
+                seen_ref[part, j, pl.ds(group * SUBS, SUBS), :] = value
     place = lax.axis_index("tm")
     own_ref[:SUBS, :] = dual_ref[:, pl.ds(pl.multiple_of(place * LANES, LANES), LANES)]
     own_ref[SUBS:, :] = jnp.full((SUBS, LANES), channel_ref[0].astype(F32))
@@ -146,7 +150,7 @@
             station = station_ref[pl.ds(tile, 1), :]
             offset, block = station & (LANES - 1), station >> 7
             lanes = pl.ds((part * tiles + tile) * LANES, LANES)
-            hot_ref[:, lanes] = jnp.where(row == offset, 1.0, 0.0).astype(BF16)
+            hot_ref[lanes, :] = jnp.where(row == offset, 1.0, 0.0).T.astype(BF16)
             wide = jnp.broadcast_to(block, (PACK, LANES))
             for h in range(blocks):
                 mask_ref[pl.ds(h * PACK, PACK), lanes] = jnp.where(wide == h, 1.0, 0.0).astype(
@@ -160,7 +164,8 @@
 
 
 def more_kernel(slot_ref, before_ref, out_ref):
-    add_products([slot_ref], before_ref, out_ref)
+    for group in range(out_ref.shape[1] // SUBS):
+        add_products([slot_ref], before_ref, out_ref, group)
 
 
 def gram(gain):
@@ -215,49 +220,35 @@
     return num(gain_second, False) + den_first, num(gain_first, True) + den_second
 
 
-def store_terms(prod_ref, seen_ref, term_ref):
-    for group in range(prod_ref.shape[1] // SUBS):
-        at = pl.ds(group * SUBS, SUBS)
-        start = group * SUBS * TERMS
-        gain_first, gain_second = (
-            [seen_ref[part, j, at, :] for j in range(SUBS)] for part in range(2)
-        )
-        both = baseline_terms(lambda index: prod_ref[index, at, :], gain_second, gain_first)
-        for part, rows in enumerate(both):
-            for j, row in enumerate(rows):
-                where, apart = (start + j, 8) if j < 8 else (start + 8 + j, 4)
-                high = row.astype(BF16).astype(F32)
-                term_ref[part, pl.ds(where, SUBS, stride=TERMS), :] = high
-                term_ref[part, pl.ds(where + apart, SUBS, stride=TERMS), :] = row - high
-
-
-def scatter_terms(term_ref, hot_ref, mask_ref, chunk):
+def store_terms(prod, gain_first, gain_second, group, term_ref):
+    start = group * SUBS * TERMS
+    for part, rows in enumerate(baseline_terms(prod, gain_second, gain_first)):
+        for j, row in enumerate(rows):
+            where, apart = (start + j, 8) if j < 8 else (start + 8 + j, 4)
+            high = row.astype(BF16).astype(F32)
+            term_ref[part, pl.ds(where, SUBS, stride=TERMS), :] = high
+            term_ref[part, pl.ds(where + apart, SUBS, stride=TERMS), :] = row - high
+
+
+def scatter_terms(term_ref, hot_ref, mask_ref, group, part):
     rows = mask_ref.shape[0]
     tiles = term_ref.shape[1] // TERMS
     blocks = rows * 2 // (3 * PACK)
-    total = None
-    for part in range(2):
-        for start in range(0, tiles, chunk):
-            columns = []
-            for tile in range(start, start + chunk):
-                lanes = pl.ds((part * tiles + tile) * LANES, LANES)
-                num = term_ref[part, pl.ds(tile * TERMS, PACK), :].astype(BF16)
-                den = term_ref[part, pl.ds(tile * TERMS + PACK, SUBS), :]
-                den = jnp.concatenate([den, den], axis=0).astype(BF16)
-                column = [
-                    mask_ref[pl.ds(h * PACK, PACK), lanes] * (num if h < blocks else den)
-                    for h in range(rows // PACK)
-                ]
-                columns.append(jnp.concatenate(column, axis=0))
-            lanes = pl.ds((part * tiles + start) * LANES, chunk * LANES)
-            add = lax.dot_general(
-                jnp.concatenate(columns, axis=1),
-                hot_ref[:, lanes],
-                (((1,), (1,)), ((), ())),
-                preferred_element_type=F32,
-            )
-            total = add if total is None else total + add
-    return total
+    columns = []
+    for tile in range(group * SUBS, (group + 1) * SUBS):
+        lanes = pl.ds((part * tiles + tile) * LANES, LANES)
+        num = term_ref[part, pl.ds(tile * TERMS, PACK), :].astype(BF16)
+        den = term_ref[part, pl.ds(tile * TERMS + PACK, SUBS), :]
+        den = jnp.concatenate([den, den], axis=0).astype(BF16)
+        column = [
+            mask_ref[pl.ds(h * PACK, PACK), lanes] * (num if h < blocks else den)
+            for h in range(rows // PACK)
+        ]
+        columns.append(jnp.concatenate(column, axis=0))
+    at = pl.ds((part * tiles + group * SUBS) * LANES, SUBS * LANES)
+    return jnp.dot(
+        jnp.concatenate(columns, axis=1), hot_ref[at, :], preferred_element_type=F32
+    )
 
 
 def solve(num, den, gain, target, penalty):
@@ -274,20 +265,40 @@
     return [value + 0.5 * old for value, old in zip(out, gain)]
 
 
+def own_place():
+    return lax.axis_index("tm")
+
+
 def sweeps_kernel(*refs):
     hot_ref, mask_ref, before_ref, found_ref, state_ref, own_ref, first_ref, second_ref = refs[:8]
-    slot_refs = refs[8:-6]
-    gain_out_ref, send_ref, prod_ref, seen_ref, term_ref, total_ref = refs[-6:]
+    slot_refs = refs[8:-5]
+    gain_out_ref, send_ref, prod_ref, term_ref, total_ref = refs[-5:]
     blocks = mask_ref.shape[0] * 2 // (3 * PACK)
-    add_products(slot_refs, before_ref, prod_ref)
+    groups = first_ref.shape[0] // SUBS
     gains = [state_ref[pl.ds(j * SUBS, blocks), :] for j in range(SUBS)]
     target = [state_ref[pl.ds((SUBS + j) * SUBS, blocks), :] for j in range(SUBS)]
     penalty = state_ref[pl.ds(2 * SUBS * SUBS, blocks), :]
     for sweep in range(SWEEPS):
-        if sweep:
-            gather_gains(gains, (first_ref, second_ref), seen_ref)
-        store_terms(prod_ref, found_ref if sweep == 0 else seen_ref, term_ref)
-        total_ref[...] = scatter_terms(term_ref, hot_ref, mask_ref, 4)
+        tables = gain_tables(gains) if sweep else None
+        total = None
+        for group in range(groups):
+            at = pl.ds(group * SUBS, SUBS)
+            if sweep:
+                gain_first, gain_second = (
+                    gather_gains(tables, ref, group) for ref in (first_ref, second_ref)
+                )
+            else:
+                add_products(slot_refs, before_ref, prod_ref, group)
+                gain_first, gain_second = (
+                    [found_ref[part, j, at, :] for j in range(SUBS)] for part in range(2)
+                )
+            store_terms(
+                lambda index: prod_ref[index, at, :], gain_first, gain_second, group, term_ref
+            )
+            for part in range(2):
+                add = scatter_terms(term_ref, hot_ref, mask_ref, group, part)
+                total = add if total is None else total + add
+        total_ref[...] = total
 
         def rows(start, stride):
             return total_ref[pl.ds(start, blocks, stride=stride), :]
@@ -299,7 +310,7 @@
         gains = solve(num, den, gains, target, penalty)
     for j in range(SUBS):
         total_ref[pl.ds(j, blocks, stride=SUBS), :] = gains[j]
-    place = lax.axis_index("tm")
+    place = own_place()
     part = total_ref[pl.ds(pl.multiple_of(place * SUBS, SUBS), SUBS), :]
     gain_out_ref[...] = part
     combined, mark = part + own_ref[:SUBS, :], own_ref[SUBS:, :]
@@ -313,21 +324,17 @@
     return [None, position, 1.5 * square - 0.5, (2.5 * square - 1.5) * position]
 
 
-def fit_kernel(
-    gram_factor, parts_ref, send_ref, consensus_hbm, dual_hbm, consensus_ref, dual_ref, sem
-):
-    channels = parts_ref.shape[0]
-    scale = float(channels) - 1.0
+def fit(gram_factor, parts, send):
+    scale = float(parts.shape[0]) - 1.0
 
     def basis(channel):
         return legendre(2.0 * channel / scale - 1.0)
 
-    moments = [None] * 4
-    for channel in range(channels):
-        value = parts_ref[channel, :SUBS, :]
-        for k, weight in enumerate(basis(parts_ref[channel, SUBS:, :])):
-            add = value if weight is None else weight * value
-            moments[k] = add if moments[k] is None else moments[k] + add
+    value = parts[:, :SUBS]
+    moments = [
+        jnp.sum(value if weight is None else weight * value, axis=0)
+        for weight in basis(parts[:, SUBS:])
+    ]
     middle = []
     for k in range(4):
         rest = moments[k]
@@ -340,14 +347,11 @@
         for later in range(k + 1, 4):
             rest = rest - gram_factor[later][k] * coeffs[later]
         coeffs[k] = rest * (1.0 / gram_factor[k][k])
-    own = basis(send_ref[0, SUBS:, :])
+    own = basis(send[0, SUBS:])
     fitted = coeffs[0]
     for k in range(1, 4):
         fitted = fitted + own[k] * coeffs[k]
-    consensus_ref[...] = fitted
-    dual_ref[...] = send_ref[0, :SUBS, :] - fitted
-    for copy in copy_in([(consensus_ref, consensus_hbm), (dual_ref, dual_hbm)], sem):
-        copy.wait()
+    return fitted, send[0, :SUBS] - fitted
 
 
 def gram_cholesky(channels):
@@ -440,7 +444,7 @@
     tables = call(
         lambda *refs: tables_kernel(len(near), *refs),
         [
-            vmem((LANES, 2 * baselines), BF16),
+            vmem((2 * baselines, LANES), BF16),
             vmem((blocks * 3 * PACK // 2, 2 * baselines), BF16),
             products,
             seen,
@@ -474,21 +478,13 @@
         "v" * (8 + len(last)),
         [
             products,
-            seen,
             vmem((2, tiles * TERMS, LANES), F32),
             vmem((blocks * 3 * PACK // 2, LANES), F32),
         ],
         limit=16,
     )(hot, mask, summed, found, state, own, first, second, *last)
     parts = lax.all_to_all(send, "freq", 0, 0)
-    factor = gram_cholesky(channels)
-    out = vmem((SUBS, LANES), F32)
-    consensus_out, dual_out = call(
-        lambda *refs: fit_kernel(factor, *refs),
-        [pltpu.HBM(out.shape, F32)] * 2,
-        "vv",
-        [out, out, pltpu.SemaphoreType.DMA((2,))],
-    )(parts, send)
+    consensus_out, dual_out = fit(gram_cholesky(channels), parts, send)
     return tuple(array[None] for array in (gain_part, consensus_out, dual_out))
 
 

time: 31.5 us -> 30.8 us (0.978)
  Pallas kernels: 8.17 us -> 6.12 us
  other arithmetic: 0 us -> 1.33 us
    pallas_call x5 -> x4, Pallas kernels: 8.17 us -> 6.12 us  [placed(): run(*(arg if space == 's' else pltpu.with_memory_space_constraint(arg, SP...]
    sub x0 -> x1, other arithmetic: none -> 1.31 us  [fit(): return (fitted, send[0, :SUBS] - fitted)]
where the time goes in v3:
time: 30.8 us; the launch traced here: 30.4 us
  waiting for transfers between devices  11.8 us (38%)
  starting transfers between devices  9.19 us (30%)
  Pallas kernels  6.12 us (20%)
  other arithmetic  1.33 us (4%)
  between operations  1.32 us (4%)
  local copies, waits for them, and re-layouts  0.59 us (2%)
    all_to_all x1, waiting for transfers between devices, shards(): parts = lax.all_to_all(send, 'freq', 0, 0)  6.31 us
    pallas_call x4, Pallas kernels, placed(): run(*(arg if space == 's' else pltpu.with_memory_space_constraint(arg, SP...  6.12 us
    all_to_all x1, starting transfers between devices, shards(): parts = lax.all_to_all(send, 'freq', 0, 0)  6.11 us
    ppermute x3, waiting for transfers between devices, swap(): return lax.ppermute(array, 'tm', [(i, i ^ step) for i in range(slots)])  5.54 us
    ppermute x3, starting transfers between devices, swap(): return lax.ppermute(array, 'tm', [(i, i ^ step) for i in range(slots)])  3.08 us
    sub x1, other arithmetic, fit(): return (fitted, send[0, :SUBS] - fitted)  1.31 us
  transfers between devices with their start and end apart: 4, of which 3 were waited for; matrix products, arithmetic and copies ran while one was open for 2% of the time, Pallas kernels for 7%

profile of v3, /device:TPU:0, one launch (start us, length us, event | category | flops | bytes accessed | tf_op | source)
XLA Modules:
  0.0 30.4 jit_solution(18188426288053184089)
XLA Ops:
  0.6 0.9 %shard_map.121.refs_0_ = f32[512,128]{1,0:T(8,128)S(1)} custom-call(bf16[8,4096]{1,0:T(8,128)(2,1)} %bitcast.33, bf16[8,4096]{1,0:T(8,128)(2,1)} %bitcast.34, s32[1,4096]{1,0:T(1,128)} %bitcast.35), custom_call_target="tpu_custom_call" | custom-call | tf_op jit(solution)/shard_map/pallas_call | solution.py:382
  1.6 0.5 %collective-permute-start = (f32[512,128]{1,0:T(8,128)S(1)}, f32[512,128]{1,0:T(8,128)S(1)}, u32[]{:S(2)}, u32[]{:S(2)}) collective-permute-start(f32[512,128]{1,0:T(8,128)S(1)} %shard_map.121.refs_0_), channel_id=1, source_target_pairs={{0,1},{1,0},{2,3},{3,2},{4,5},{5,4},{6,7},{7,6},{8,9},{9,8},{10,11... | collective-permute-start | bytes 786440 | tf_op jit(solution)/shard_map/ppermute | solution.py:414
  2.1 2.6 %collective-permute-start.1 = (f32[512,128]{1,0:T(8,128)S(1)}, f32[512,128]{1,0:T(8,128)S(1)}, u32[]{:S(2)}, u32[]{:S(2)}) collective-permute-start(f32[512,128]{1,0:T(8,128)S(1)} %shard_map.121.refs_0_), channel_id=1, source_target_pairs={{0,2},{1,3},{2,0},{3,1},{4,6},{5,7},{6,4},{7,5},{8,10},{9,11},{10,... | collective-permute-start | bytes 786440 | tf_op jit(solution)/shard_map/ppermute | solution.py:414
  5.3 0.0 collective-permute-done.refs_1_
  5.3 2.1 %shard_map.122 = (bf16[8192,128]{1,0:T(8,128)(2,1)S(1)}, bf16[96,8192]{1,0:T(8,128)(2,1)S(1)}, f32[48,32,128]{2,1,0:T(8,128)S(1)}, f32[2,8,32,128]{3,2,1,0:T(8,1...) custom-call(f32[512,128]{1,0:T(8,128)S(1)} %shard_map.121.refs_0_, ...), custom_call_target="tpu_custom_call" | custom-call | flops 4000000000 | bytes 12000000 | tf_op jit(solution)/shard_map/pallas_call | solution.py:382
  7.4 4.1 %collective-permute-done.1.slot_ref = f32[512,128]{1,0:T(8,128)S(1)} collective-permute-done((f32[512,128]{1,0:T(8,128)S(1)}, f32[512,128]{1,0:T(8,128)S(1)}, u32[]{:S(2)}, u32[]{:S(2)}) %collective-permute-start.1) | collective-permute-done | bytes 262176 | tf_op jit(solution)/shard_map/ppermute | solution.py:414
  11.6 0.0 collective-permute-start.2
  11.6 0.1 shard_map.123.refs_2_
  11.7 1.4 %collective-permute-done.2.refs_8_ = f32[512,128]{1,0:T(8,128)S(1)} collective-permute-done((f32[512,128]{1,0:T(8,128)S(1)}, f32[512,128]{1,0:T(8,128)S(1)}, u32[]{:S(2)}, u32[]{:S(2)}) %collective-permute-start.2) | collective-permute-done | bytes 262176 | tf_op jit(solution)/shard_map/ppermute | solution.py:414
  13.1 3.0 %shard_map.124 = (f32[8,128]{1,0:T(8,128)S(1)}, f32[8,16,128]{2,1,0:T(8,128)}) custom-call(bf16[8192,128]{1,0:T(8,128)(2,1)S(1)} %get-tuple-element.15.refs_0_, bf16[96,8192]{1,0:T(8,128)(2,1)S(1)} %get-tuple-element.16.refs_1_, f32[48,32,128]{2,1,0:T(8,128)S(1)} %shard_map.123.refs_2_, f32[2,8,32,128]{3,2,1,0:T(8,128)S(1)} %get-tuple-element.20.refs_3_, ...), custom_call_target="tpu_custom_call" | custom-call | tf_op jit(solution)/shard_map/pallas_call | solution.py:382
  16.1 6.1 %all-to-all-start = ((f32[8,16,128]{2,1,0:T(8,128)}), f32[8,16,128]{2,1,0:T(8,128)S(1)}, u32[]{:S(2)}, u32[]{:S(2)}) async-start(f32[8,16,128]{2,1,0:T(8,128)} %get-tuple-element.26), calls=%async_computation | async-start | bytes 131072 | tf_op jit(solution)/shard_map/all_to_all | solution.py:486
  22.2 0.6 %copy.13 = f32[1,8,128]{2,1,0:T(8,128)} copy(f32[1,8,128]{2,1,0:T(8,128)S(1)} %bitcast.32) | data formatting | bytes 8192
  22.8 6.3 %all-to-all-done = f32[8,16,128]{2,1,0:T(8,128)S(1)} async-done(((f32[8,16,128]{2,1,0:T(8,128)}), f32[8,16,128]{2,1,0:T(8,128)S(1)}, u32[]{:S(2)}, u32[]{:S(2)}) %all-to-all-start) | async-done | bytes 65568 | tf_op jit(solution)/shard_map/all_to_all | solution.py:486
  29.1 1.3 %slice_subtract_fusion = (f32[1,8,128]{2,1,0:T(8,128)}, f32[1,8,128]{2,1,0:T(8,128)}) fusion(f32[8,16,128]{2,1,0:T(8,128)} %get-tuple-element.26, f32[8,128]{1,0:T(8,128)S(1)} %get-tuple-element.29, f32[8,128]{1,0:T(8,128)S(1)} %get-tuple-element.30, f32[8,128]{1,0:T(8,128)S(1)} %get-tuple-element.28, f32[8,128]{1,0:T(8,128)S(1)} %get-tuple-element.27), kind=kLoop, calls=%fused_computation.12 | loop fusion | flops 47104 | bytes 32768 | tf_op jit(solution)/shard_map/sub | solution.py:354
  (1 shorter events, 0.0 us)
Async XLA Ops:
  1.6 3.7 %collective-permute-start = (f32[512,128]{1,0:T(8,128)S(1)}, f32[512,128]{1,0:T(8,128)S(1)}, u32[]{:S(2)}, u32[]{:S(2)}) collective-permute-start(f32[512,128]{1,0:T(8,128)S(1)} %shard_map.121.refs_0_), channel_id=1, source_target_pairs={{0,1},{1,0},{2,3},{3,2},{4,5},{5,4},{6,7},{7,6},{8,9},{9,8},{10,11... | collective-permute-start | bytes 786440 | tf_op jit(solution)/shard_map/ppermute | solution.py:414
  2.1 9.5 %collective-permute-start.1 = (f32[512,128]{1,0:T(8,128)S(1)}, f32[512,128]{1,0:T(8,128)S(1)}, u32[]{:S(2)}, u32[]{:S(2)}) collective-permute-start(f32[512,128]{1,0:T(8,128)S(1)} %shard_map.121.refs_0_), channel_id=1, source_target_pairs={{0,2},{1,3},{2,0},{3,1},{4,6},{5,7},{6,4},{7,5},{8,10},{9,11},{10,... | collective-permute-start | bytes 786440 | tf_op jit(solution)/shard_map/ppermute | solution.py:414
  11.6 1.5 %collective-permute-start.2 = (f32[512,128]{1,0:T(8,128)S(1)}, f32[512,128]{1,0:T(8,128)S(1)}, u32[]{:S(2)}, u32[]{:S(2)}) collective-permute-start(f32[512,128]{1,0:T(8,128)S(1)} %collective-permute-done.1.slot_ref), channel_id=1, source_target_pairs={{0,1},{1,0},{2,3},{3,2},{4,5},{5,4},{6,7},{7,6},{8,9},{9,8},{10,11... | collective-permute-start | bytes 786440 | tf_op jit(solution)/shard_map/ppermute | solution.py:414
  16.1 13.0 %all-to-all-start = ((f32[8,16,128]{2,1,0:T(8,128)}), f32[8,16,128]{2,1,0:T(8,128)S(1)}, u32[]{:S(2)}, u32[]{:S(2)}) async-start(f32[8,16,128]{2,1,0:T(8,128)} %get-tuple-element.26), calls=%async_computation | async-start | bytes 131072 | tf_op jit(solution)/shard_map/all_to_all | solution.py:486

commit v4 on v3

--- a/solution.py
+++ b/solution.py
@@ -163,9 +163,9 @@
                 ).astype(BF16)
 
 
-def more_kernel(slot_ref, before_ref, out_ref):
-    for group in range(out_ref.shape[1] // SUBS):
-        add_products([slot_ref], before_ref, out_ref, group)
+def more_kernel(before_ref, *refs):
+    for group in range(before_ref.shape[1] // SUBS):
+        add_products(refs[:-1], before_ref, refs[-1], group)
 
 
 def gram(gain):
@@ -433,7 +433,6 @@
     while step > 1:
         far += [swap(array, step) for array in [own, *far]]
         step //= 2
-    near = [own, swap(own, 1)]
     gains, consensus, dual = (
         array.reshape(SUBS, stations) for array in (gains_in, consensus_in, dual_in)
     )
@@ -442,7 +441,7 @@
     station = vmem((tiles, LANES), jnp.int32)
     wide = vmem((SUBS, stations), F32)
     tables = call(
-        lambda *refs: tables_kernel(len(near), *refs),
+        lambda *refs: tables_kernel(1, *refs),
         [
             vmem((2 * baselines, LANES), BF16),
             vmem((blocks * 3 * PACK // 2, 2 * baselines), BF16),
@@ -453,12 +452,12 @@
             station,
             station,
         ],
-        "v" * len(near) + "shhhhhh",
+        "vshhhhhh",
         [wide, wide, wide, vmem((1, stations), F32), pltpu.SemaphoreType.DMA((6,))],
         limit=16,
         micros=4,
     )(
-        *near,
+        own,
         channel_index,
         first_station.reshape(tiles, LANES),
         second_station.reshape(tiles, LANES),
@@ -467,11 +466,14 @@
         dual,
         penalty.reshape(1, stations),
     )
-    hot, mask, summed, found, state, own, first, second = tables
+    hot, mask, summed, found, state, marks, first, second = tables
+    own, state = lax.optimization_barrier((own, state))
+    near = swap(own, 1)
     far, state = lax.optimization_barrier((far, state))
     last = [swap(array, 1) for array in far]
-    for array in far:
-        (summed,) = call(more_kernel, [products], "vv", micros=1)(array, summed)
+    (summed,) = call(more_kernel, [products], "v" * (2 + len(far)), micros=1)(
+        summed, near, *far
+    )
     gain_part, send = call(
         sweeps_kernel,
         [vmem((SUBS, LANES), F32), vmem((channels, 2 * SUBS, LANES), F32)],
@@ -482,7 +484,7 @@
             vmem((blocks * 3 * PACK // 2, LANES), F32),
         ],
         limit=16,
-    )(hot, mask, summed, found, state, own, first, second, *last)
+    )(hot, mask, summed, found, state, marks, first, second, *last)
     parts = lax.all_to_all(send, "freq", 0, 0)
     consensus_out, dual_out = fit(gram_cholesky(channels), parts, send)
     return tuple(array[None] for array in (gain_part, consensus_out, dual_out))

time: 30.8 us -> 30.1 us (0.977)
  waiting for transfers between devices: 11.8 us -> 11.1 us
    ppermute x3, waiting for transfers between devices: 5.54 us -> 4.78 us  [swap(): return lax.ppermute(array, 'tm', [(i, i ^ step) for i in range(slots)])]
  transfers between devices with their start and end apart: 4 -> 4, of which waited for: 3 -> 3; matrix products, arithmetic and copies ran while one was open for 2% -> 2% of each run, Pallas kernels for 7% -> 8%
where the time goes in v4:
time: 30.1 us; the launch traced here: 29.7 us
  waiting for transfers between devices  11.1 us (37%)
  starting transfers between devices  9.17 us (30%)
  Pallas kernels  6.21 us (21%)
  other arithmetic  1.33 us (4%)
  between operations  1.32 us (4%)
  local copies, waits for them, and re-layouts  0.59 us (2%)
    all_to_all x1, waiting for transfers between devices, shards(): parts = lax.all_to_all(send, 'freq', 0, 0)  6.31 us
    pallas_call x4, Pallas kernels, placed(): run(*(arg if space == 's' else pltpu.with_memory_space_constraint(arg, SP...  6.21 us
    all_to_all x1, starting transfers between devices, shards(): parts = lax.all_to_all(send, 'freq', 0, 0)  6.09 us
    ppermute x3, waiting for transfers between devices, swap(): return lax.ppermute(array, 'tm', [(i, i ^ step) for i in range(slots)])  4.78 us
    ppermute x3, starting transfers between devices, swap(): return lax.ppermute(array, 'tm', [(i, i ^ step) for i in range(slots)])  3.08 us
    sub x1, other arithmetic, fit(): return (fitted, send[0, :SUBS] - fitted)  1.31 us
  transfers between devices with their start and end apart: 4, of which 3 were waited for; matrix products, arithmetic and copies ran while one was open for 2% of the time, Pallas kernels for 8%

profile of v4, /device:TPU:0, one launch (start us, length us, event | category | flops | bytes accessed | tf_op | source)
XLA Modules:
  0.0 29.7 jit_solution(6420084713925421256)
XLA Ops:
  0.6 0.9 %shard_map.121.refs_0_ = f32[512,128]{1,0:T(8,128)S(1)} custom-call(bf16[8,4096]{1,0:T(8,128)(2,1)} %bitcast.33, bf16[8,4096]{1,0:T(8,128)(2,1)} %bitcast.34, s32[1,4096]{1,0:T(1,128)} %bitcast.35), custom_call_target="tpu_custom_call" | custom-call | tf_op jit(solution)/shard_map/pallas_call | solution.py:382
  1.6 3.0 %collective-permute-start.1 = (f32[512,128]{1,0:T(8,128)S(1)}, f32[512,128]{1,0:T(8,128)S(1)}, u32[]{:S(2)}, u32[]{:S(2)}) collective-permute-start(f32[512,128]{1,0:T(8,128)S(1)} %shard_map.121.refs_0_), channel_id=1, source_target_pairs={{0,2},{1,3},{2,0},{3,1},{4,6},{5,7},{6,4},{7,5},{8,10},{9,11},{10,... | collective-permute-start | bytes 786440 | tf_op jit(solution)/shard_map/ppermute | solution.py:414
  5.2 2.1 %shard_map.122 = (bf16[8192,128]{1,0:T(8,128)(2,1)S(1)}, bf16[96,8192]{1,0:T(8,128)(2,1)S(1)}, f32[48,32,128]{2,1,0:T(8,128)S(1)}, f32[2,8,32,128]{3,2,1,0:T(8,1...) custom-call(f32[512,128]{1,0:T(8,128)S(1)} %shard_map.121.refs_0_, ...), custom_call_target="tpu_custom_call" | custom-call | flops 4000000000 | bytes 12000000 | tf_op jit(solution)/shard_map/pallas_call | solution.py:382
  7.3 0.1 collective-permute-start
  7.4 3.5 %collective-permute-done.1.refs_1_ = f32[512,128]{1,0:T(8,128)S(1)} collective-permute-done((f32[512,128]{1,0:T(8,128)S(1)}, f32[512,128]{1,0:T(8,128)S(1)}, u32[]{:S(2)}, u32[]{:S(2)}) %collective-permute-start.1) | collective-permute-done | bytes 262176 | tf_op jit(solution)/shard_map/ppermute | solution.py:414
  10.9 0.0 collective-permute-start.2
  10.9 0.0 collective-permute-done.refs_0_
  10.9 0.2 shard_map.123.refs_2_
  11.1 1.3 %collective-permute-done.2.refs_8_ = f32[512,128]{1,0:T(8,128)S(1)} collective-permute-done((f32[512,128]{1,0:T(8,128)S(1)}, f32[512,128]{1,0:T(8,128)S(1)}, u32[]{:S(2)}, u32[]{:S(2)}) %collective-permute-start.2) | collective-permute-done | bytes 262176 | tf_op jit(solution)/shard_map/ppermute | solution.py:414
  12.4 3.0 %shard_map.124 = (f32[8,128]{1,0:T(8,128)S(1)}, f32[8,16,128]{2,1,0:T(8,128)}) custom-call(bf16[8192,128]{1,0:T(8,128)(2,1)S(1)} %get-tuple-element.17.refs_0_, bf16[96,8192]{1,0:T(8,128)(2,1)S(1)} %get-tuple-element.18.refs_1_, f32[48,32,128]{2,1,0:T(8,128)S(1)} %shard_map.123.refs_2_, f32[2,8,32,128]{3,2,1,0:T(8,128)S(1)} %get-tuple-element.24.refs_3_, ...), custom_call_target="tpu_custom_call" | custom-call | tf_op jit(solution)/shard_map/pallas_call | solution.py:382
  15.4 6.1 %all-to-all-start = ((f32[8,16,128]{2,1,0:T(8,128)}), f32[8,16,128]{2,1,0:T(8,128)S(1)}, u32[]{:S(2)}, u32[]{:S(2)}) async-start(f32[8,16,128]{2,1,0:T(8,128)} %get-tuple-element.30), calls=%async_computation | async-start | bytes 131072 | tf_op jit(solution)/shard_map/all_to_all | solution.py:488
  21.5 0.6 %copy.13 = f32[1,8,128]{2,1,0:T(8,128)} copy(f32[1,8,128]{2,1,0:T(8,128)S(1)} %bitcast.32) | data formatting | bytes 8192
  22.1 6.3 %all-to-all-done = f32[8,16,128]{2,1,0:T(8,128)S(1)} async-done(((f32[8,16,128]{2,1,0:T(8,128)}), f32[8,16,128]{2,1,0:T(8,128)S(1)}, u32[]{:S(2)}, u32[]{:S(2)}) %all-to-all-start) | async-done | bytes 65568 | tf_op jit(solution)/shard_map/all_to_all | solution.py:488
  28.4 1.3 %slice_subtract_fusion = (f32[1,8,128]{2,1,0:T(8,128)}, f32[1,8,128]{2,1,0:T(8,128)}) fusion(f32[8,16,128]{2,1,0:T(8,128)} %get-tuple-element.30, f32[8,128]{1,0:T(8,128)S(1)} %get-tuple-element.33, f32[8,128]{1,0:T(8,128)S(1)} %get-tuple-element.34, f32[8,128]{1,0:T(8,128)S(1)} %get-tuple-element.32, f32[8,128]{1,0:T(8,128)S(1)} %get-tuple-element.31), kind=kLoop, calls=%fused_computation.12 | loop fusion | flops 47104 | bytes 32768 | tf_op jit(solution)/shard_map/sub | solution.py:354
  (1 shorter events, 0.0 us)
Async XLA Ops:
  1.6 9.3 %collective-permute-start.1 = (f32[512,128]{1,0:T(8,128)S(1)}, f32[512,128]{1,0:T(8,128)S(1)}, u32[]{:S(2)}, u32[]{:S(2)}) collective-permute-start(f32[512,128]{1,0:T(8,128)S(1)} %shard_map.121.refs_0_), channel_id=1, source_target_pairs={{0,2},{1,3},{2,0},{3,1},{4,6},{5,7},{6,4},{7,5},{8,10},{9,11},{10,... | collective-permute-start | bytes 786440 | tf_op jit(solution)/shard_map/ppermute | solution.py:414
  7.3 3.6 %collective-permute-start = (f32[512,128]{1,0:T(8,128)S(1)}, f32[512,128]{1,0:T(8,128)S(1)}, u32[]{:S(2)}, u32[]{:S(2)}) collective-permute-start(f32[512,128]{1,0:T(8,128)S(1)} %shard_map.121.refs_0_), channel_id=1, source_target_pairs={{0,1},{1,0},{2,3},{3,2},{4,5},{5,4},{6,7},{7,6},{8,9},{9,8},{10,11... | collective-permute-start | bytes 786440 | tf_op jit(solution)/shard_map/ppermute | solution.py:414
  10.9 1.5 %collective-permute-start.2 = (f32[512,128]{1,0:T(8,128)S(1)}, f32[512,128]{1,0:T(8,128)S(1)}, u32[]{:S(2)}, u32[]{:S(2)}) collective-permute-start(f32[512,128]{1,0:T(8,128)S(1)} %collective-permute-done.1.refs_1_), channel_id=1, source_target_pairs={{0,1},{1,0},{2,3},{3,2},{4,5},{5,4},{6,7},{7,6},{8,9},{9,8},{10,11... | collective-permute-start | bytes 786440 | tf_op jit(solution)/shard_map/ppermute | solution.py:414
  15.4 13.0 %all-to-all-start = ((f32[8,16,128]{2,1,0:T(8,128)}), f32[8,16,128]{2,1,0:T(8,128)S(1)}, u32[]{:S(2)}, u32[]{:S(2)}) async-start(f32[8,16,128]{2,1,0:T(8,128)} %get-tuple-element.30), calls=%async_computation | async-start | bytes 131072 | tf_op jit(solution)/shard_map/all_to_all | solution.py:488

commit v5 on v4

--- a/solution.py
+++ b/solution.py
@@ -30,22 +30,23 @@
     return copies
 
 
-def widen_kernel(vis_hbm, model_hbm, keep_hbm, out_ref, vis_ref, model_ref, keep_ref, sem):
+def widen_kernel(vis_hbm, model_hbm, keep_hbm, *refs):
+    vis_ref, model_ref, keep_ref, sem = refs[-4:]
     copies = copy_in(
         [(vis_hbm, vis_ref), (keep_hbm, keep_ref), (model_hbm, model_ref)], sem
     )
-    tiles = vis_ref.shape[1] // LANES
-    copies[0].wait()
-    for tile in range(tiles):
-        lanes = pl.ds(tile * LANES, LANES)
-        out_ref[pl.ds(tile * SUBS, SUBS), :] = vis_ref[:, lanes].astype(F32)
-    copies[1].wait()
-    copies[2].wait()
-    for tile in range(tiles):
-        lanes = pl.ds(tile * LANES, LANES)
-        out_ref[pl.ds((tiles + tile) * SUBS, SUBS), :] = model_ref[:, lanes].astype(
-            F32
-        ) * keep_ref[:, lanes].astype(F32)
+    for copy in copies:
+        copy.wait()
+    start = 0
+    for out_ref in refs[:-4]:
+        tiles = out_ref.shape[0] // (2 * SUBS)
+        for tile in range(tiles):
+            lanes = pl.ds((start + tile) * LANES, LANES)
+            out_ref[pl.ds(tile * SUBS, SUBS), :] = vis_ref[:, lanes].astype(F32)
+            out_ref[pl.ds((tiles + tile) * SUBS, SUBS), :] = model_ref[:, lanes].astype(
+                F32
+            ) * keep_ref[:, lanes].astype(F32)
+        start += tiles
 
 
 def slot_products(slot_ref, group, tiles):
@@ -106,8 +107,9 @@
 def tables_kernel(count, *refs):
     slot_refs, channel_ref = refs[:count], refs[count]
     station_hbms, array_hbms = refs[count + 1 : count + 3], refs[count + 3 : count + 7]
-    outs = refs[count + 7 : -5]
-    hot_ref, mask_ref, prod_ref, seen_ref, state_ref, own_ref, first_ref, second_ref = outs
+    prod_refs = refs[count + 7 : 2 * count + 7]
+    outs = refs[2 * count + 7 : -5]
+    hot_ref, mask_ref, seen_ref, state_ref, own_ref, first_ref, second_ref = outs
     gains_ref, consensus_ref, dual_ref, penalty_ref, sem = refs[-5:]
     station_refs = (first_ref, second_ref)
     copies = copy_in(
@@ -120,8 +122,9 @@
         sem,
     )
     tiles = first_ref.shape[0]
-    for group in range(tiles // SUBS):
-        add_products(slot_refs, None, prod_ref, group)
+    for slot_ref, prod_ref in zip(slot_refs, prod_refs, strict=True):
+        for group in range(prod_ref.shape[1] // SUBS):
+            add_products([slot_ref], None, prod_ref, group)
     for copy in copies:
         copy.wait()
     blocks = gains_ref.shape[1] // LANES
@@ -230,13 +233,13 @@
             term_ref[part, pl.ds(where + apart, SUBS, stride=TERMS), :] = row - high
 
 
-def scatter_terms(term_ref, hot_ref, mask_ref, group, part):
+def scatter_terms(term_ref, hot_ref, mask_ref, group, start, part):
     rows = mask_ref.shape[0]
-    tiles = term_ref.shape[1] // TERMS
+    tiles = hot_ref.shape[0] // (2 * LANES)
     blocks = rows * 2 // (3 * PACK)
     columns = []
     for tile in range(group * SUBS, (group + 1) * SUBS):
-        lanes = pl.ds((part * tiles + tile) * LANES, LANES)
+        lanes = pl.ds((part * tiles + start + tile) * LANES, LANES)
         num = term_ref[part, pl.ds(tile * TERMS, PACK), :].astype(BF16)
         den = term_ref[part, pl.ds(tile * TERMS + PACK, SUBS), :]
         den = jnp.concatenate([den, den], axis=0).astype(BF16)
@@ -245,9 +248,38 @@
             for h in range(rows // PACK)
         ]
         columns.append(jnp.concatenate(column, axis=0))
-    at = pl.ds((part * tiles + group * SUBS) * LANES, SUBS * LANES)
+    at = pl.ds((part * tiles + start + group * SUBS) * LANES, SUBS * LANES)
     return jnp.dot(
         jnp.concatenate(columns, axis=1), hot_ref[at, :], preferred_element_type=F32
+    )
+
+
+def piece_totals(prod_ref, gains_of, term_ref, hot_ref, mask_ref, start, total):
+    for group in range(prod_ref.shape[1] // SUBS):
+        at = pl.ds(group * SUBS, SUBS)
+        gain_first, gain_second = (gains_of(part, start // SUBS + group) for part in range(2))
+        store_terms(
+            lambda index: prod_ref[index, at, :], gain_first, gain_second, group, term_ref
+        )
+        for part in range(2):
+            add = scatter_terms(term_ref, hot_ref, mask_ref, group, start, part)
+            total = add if total is None else total + add
+    return total
+
+
+def found_gains(found_ref):
+    return lambda part, group: [
+        found_ref[part, j, pl.ds(group * SUBS, SUBS), :] for j in range(SUBS)
+    ]
+
+
+def piece_kernel(start, hot_ref, mask_ref, found_ref, before_ref, *refs):
+    slot_refs = refs[:-3]
+    prod_ref, total_ref, term_ref = refs[-3:]
+    for group in range(prod_ref.shape[1] // SUBS):
+        add_products(slot_refs, before_ref, prod_ref, group)
+    total_ref[...] = piece_totals(
+        prod_ref, found_gains(found_ref), term_ref, hot_ref, mask_ref, start, None
     )
 
 
@@ -269,35 +301,39 @@
     return lax.axis_index("tm")
 
 
-def sweeps_kernel(*refs):
-    hot_ref, mask_ref, before_ref, found_ref, state_ref, own_ref, first_ref, second_ref = refs[:8]
-    slot_refs = refs[8:-5]
-    gain_out_ref, send_ref, prod_ref, term_ref, total_ref = refs[-5:]
+def sweeps_kernel(counts, *refs):
+    pieces, slots = counts
+    hot_ref, mask_ref, found_ref, state_ref, own_ref, first_ref, second_ref = refs[:7]
+    prod_refs, partial_refs = refs[7 : 6 + pieces], refs[6 + pieces : 5 + 2 * pieces]
+    before_ref, slot_refs = refs[5 + 2 * pieces], refs[6 + 2 * pieces : 6 + 2 * pieces + slots]
+    gain_out_ref, send_ref, last_ref, total_ref = refs[6 + 2 * pieces + slots : -pieces]
+    term_refs = refs[-pieces:]
     blocks = mask_ref.shape[0] * 2 // (3 * PACK)
-    groups = first_ref.shape[0] // SUBS
     gains = [state_ref[pl.ds(j * SUBS, blocks), :] for j in range(SUBS)]
     target = [state_ref[pl.ds((SUBS + j) * SUBS, blocks), :] for j in range(SUBS)]
     penalty = state_ref[pl.ds(2 * SUBS * SUBS, blocks), :]
+    for group in range(last_ref.shape[1] // SUBS):
+        add_products(slot_refs, before_ref, last_ref, group)
+    prod_refs = (*prod_refs, last_ref)
     for sweep in range(SWEEPS):
-        tables = gain_tables(gains) if sweep else None
         total = None
-        for group in range(groups):
-            at = pl.ds(group * SUBS, SUBS)
-            if sweep:
-                gain_first, gain_second = (
-                    gather_gains(tables, ref, group) for ref in (first_ref, second_ref)
+        if sweep:
+            tables = gain_tables(gains)
+
+            def gains_of(part, group, tables=tables):
+                return gather_gains(tables, (first_ref, second_ref)[part], group)
+
+        else:
+            gains_of = found_gains(found_ref)
+            for partial_ref in partial_refs:
+                total = partial_ref[...] if total is None else total + partial_ref[...]
+        start = 0
+        for prod_ref, term_ref in zip(prod_refs, term_refs, strict=True):
+            if sweep or prod_ref is last_ref:
+                total = piece_totals(
+                    prod_ref, gains_of, term_ref, hot_ref, mask_ref, start, total
                 )
-            else:
-                add_products(slot_refs, before_ref, prod_ref, group)
-                gain_first, gain_second = (
-                    [found_ref[part, j, at, :] for j in range(SUBS)] for part in range(2)
-                )
-            store_terms(
-                lambda index: prod_ref[index, at, :], gain_first, gain_second, group, term_ref
-            )
-            for part in range(2):
-                add = scatter_terms(term_ref, hot_ref, mask_ref, group, part)
-                total = add if total is None else total + add
+            start += prod_ref.shape[1]
         total_ref[...] = total
 
         def rows(start, stride):
@@ -413,9 +449,10 @@
     def swap(array, step):
         return lax.ppermute(array, "tm", [(i, i ^ step) for i in range(slots)])
 
-    (own,) = call(
+    sizes = [tiles // 2, tiles // 2]
+    pieces = call(
         widen_kernel,
-        [vmem((2 * tiles * SUBS, LANES), F32)],
+        [vmem((2 * size * SUBS, LANES), F32) for size in sizes],
         "hhh",
         [
             vmem((SUBS, baselines), BF16),
@@ -429,35 +466,41 @@
         keep_mask.reshape(1, baselines),
     )
     far = []
-    step = slots // 2
-    while step > 1:
-        far += [swap(array, step) for array in [own, *far]]
-        step //= 2
+    for piece in pieces:
+        got = []
+        step = slots // 2
+        while step > 1:
+            got += [swap(array, step) for array in [piece, *got]]
+            step //= 2
+        far.append(got)
     gains, consensus, dual = (
         array.reshape(SUBS, stations) for array in (gains_in, consensus_in, dual_in)
     )
-    products = vmem((PRODS, tiles, LANES), F32)
+    products = [vmem((PRODS, size, LANES), F32) for size in sizes]
+    terms = [vmem((2, size * TERMS, LANES), F32) for size in sizes]
     seen = vmem((2, SUBS, tiles, LANES), F32)
     station = vmem((tiles, LANES), jnp.int32)
     wide = vmem((SUBS, stations), F32)
+    totals = vmem((blocks * 3 * PACK // 2, LANES), F32)
+    count = len(sizes)
     tables = call(
-        lambda *refs: tables_kernel(1, *refs),
+        lambda *refs: tables_kernel(count, *refs),
         [
+            *products,
             vmem((2 * baselines, LANES), BF16),
             vmem((blocks * 3 * PACK // 2, 2 * baselines), BF16),
-            products,
             seen,
             vmem(((2 * SUBS + 1) * SUBS, LANES), F32),
             vmem((2 * SUBS, LANES), F32),
             station,
             station,
         ],
-        "vshhhhhh",
+        "v" * count + "shhhhhh",
         [wide, wide, wide, vmem((1, stations), F32), pltpu.SemaphoreType.DMA((6,))],
         limit=16,
-        micros=4,
+        micros=1,
     )(
-        own,
+        *pieces,
         channel_index,
         first_station.reshape(tiles, LANES),
         second_station.reshape(tiles, LANES),
@@ -466,25 +509,47 @@
         dual,
         penalty.reshape(1, stations),
     )
-    hot, mask, summed, found, state, marks, first, second = tables
-    own, state = lax.optimization_barrier((own, state))
-    near = swap(own, 1)
-    far, state = lax.optimization_barrier((far, state))
-    last = [swap(array, 1) for array in far]
-    (summed,) = call(more_kernel, [products], "v" * (2 + len(far)), micros=1)(
-        summed, near, *far
-    )
+    summed = list(tables[:count])
+    hot, mask, found, state, own, first, second = tables[count:]
+    pieces, state = lax.optimization_barrier((pieces, state))
+    near = [swap(piece, 1) for piece in pieces]
+    far[0], state = lax.optimization_barrier((far[0], state))
+    last = [[swap(array, 1) for array in far[0]]]
+    (summed[0],) = call(more_kernel, [products[0]], "v" * (2 + len(far[0])), micros=0.001)(
+        summed[0], near[0], *far[0]
+    )
+    far[1], last[0], found = lax.optimization_barrier((far[1], last[0], found))
+    last.append([swap(array, 1) for array in far[1]])
+    (summed[1],) = call(more_kernel, [products[1]], "v" * (2 + len(far[1])), micros=0.001)(
+        summed[1], near[1], *far[1]
+    )
+    summed[0], partial = call(
+        lambda *refs: piece_kernel(0, *refs),
+        [products[0], totals],
+        "v" * (4 + len(last[0])),
+        [terms[0]],
+        limit=16,
+        micros=0.001,
+    )(hot, mask, found, summed[0], *last[0])
     gain_part, send = call(
-        sweeps_kernel,
+        lambda *refs: sweeps_kernel((count, len(last[1])), *refs),
         [vmem((SUBS, LANES), F32), vmem((channels, 2 * SUBS, LANES), F32)],
-        "v" * (8 + len(last)),
-        [
-            products,
-            vmem((2, tiles * TERMS, LANES), F32),
-            vmem((blocks * 3 * PACK // 2, LANES), F32),
-        ],
+        "v" * (10 + len(last[1])),
+        [products[1], totals, *terms],
         limit=16,
-    )(hot, mask, summed, found, state, marks, first, second, *last)
+    )(
+        hot,
+        mask,
+        found,
+        state,
+        own,
+        first,
+        second,
+        summed[0],
+        partial,
+        summed[1],
+        *last[1],
+    )
     parts = lax.all_to_all(send, "freq", 0, 0)
     consensus_out, dual_out = fit(gram_cholesky(channels), parts, send)
     return tuple(array[None] for array in (gain_part, consensus_out, dual_out))

time: 30.1 us -> 29.3 us (0.973)
  waiting for transfers between devices: 11.1 us -> 9.72 us
  starting transfers between devices: 9.17 us -> 9.66 us
    ppermute x3 -> x6, waiting for transfers between devices: 4.78 us -> 3.41 us  [swap(): return lax.ppermute(array, 'tm', [(i, i ^ step) for i in range(slots)])]
    ppermute x3 -> x6, starting transfers between devices: 3.08 us -> 3.6 us  [swap(): return lax.ppermute(array, 'tm', [(i, i ^ step) for i in range(slots)])]
    pallas_call x4 -> x6, Pallas kernels: 6.21 us -> 6.29 us  [placed(): run(*(arg if space == 's' else pltpu.with_memory_space_constraint(arg, SP...]
  transfers between devices with their start and end apart: 4 -> 7, of which waited for: 3 -> 4; matrix products, arithmetic and copies ran while one was open for 2% -> 2% of each run, Pallas kernels for 8% -> 10%
where the time goes in v5:
time: 29.3 us; the launch traced here: 28.9 us
  waiting for transfers between devices  9.72 us (33%)
  starting transfers between devices  9.66 us (33%)
  Pallas kernels  6.29 us (21%)
  between operations  1.34 us (5%)
  other arithmetic  1.33 us (5%)
  local copies, waits for them, and re-layouts  0.59 us (2%)
    all_to_all x1, waiting for transfers between devices, shards(): parts = lax.all_to_all(send, 'freq', 0, 0)  6.31 us
    pallas_call x6, Pallas kernels, placed(): run(*(arg if space == 's' else pltpu.with_memory_space_constraint(arg, SP...  6.29 us
    all_to_all x1, starting transfers between devices, shards(): parts = lax.all_to_all(send, 'freq', 0, 0)  6.07 us
    ppermute x6, starting transfers between devices, swap(): return lax.ppermute(array, 'tm', [(i, i ^ step) for i in range(slots)])  3.6 us
    ppermute x6, waiting for transfers between devices, swap(): return lax.ppermute(array, 'tm', [(i, i ^ step) for i in range(slots)])  3.41 us
    sub x1, other arithmetic, fit(): return (fitted, send[0, :SUBS] - fitted)  1.31 us
    unnamed x1, local copies, waits for them, and re-layouts  0.59 us
  transfers between devices with their start and end apart: 7, of which 4 were waited for; matrix products, arithmetic and copies ran while one was open for 2% of the time, Pallas kernels for 10%

profile of v5, /device:TPU:0, one launch (start us, length us, event | category | flops | bytes accessed | tf_op | source)
XLA Modules:
  0.0 28.9 jit_solution(1394252211872630153)
XLA Ops:
  0.6 0.9 %shard_map.121 = (f32[256,128]{1,0:T(8,128)S(1)}, f32[256,128]{1,0:T(8,128)S(1)}) custom-call(bf16[8,4096]{1,0:T(8,128)(2,1)} %bitcast.33, bf16[8,4096]{1,0:T(8,128)(2,1)} %bitcast.34, s32[1,4096]{1,0:T(1,128)} %bitcast.35), custom_call_target="tpu_custom_call" | custom-call | tf_op jit(solution)/shard_map/pallas_call | solution.py:418
  1.6 3.0 %collective-permute-start.1 = (f32[256,128]{1,0:T(8,128)S(1)}, f32[256,128]{1,0:T(8,128)S(1)}, u32[]{:S(2)}, u32[]{:S(2)}) collective-permute-start(f32[256,128]{1,0:T(8,128)S(1)} %get-tuple-element.40.refs_0_), channel_id=1, source_target_pairs={{0,2},{1,3},{2,0},{3,1},{4,6},{5,7},{6,4},{7,5},{8,10},{9,11},{10,... | collective-permute-start | bytes 393224 | tf_op jit(solution)/shard_map/ppermute | solution.py:450
  4.6 0.1 collective-permute-start
  5.3 2.1 %shard_map.122 = (f32[48,16,128]{2,1,0:T(8,128)S(1)}, f32[48,16,128]{2,1,0:T(8,128)S(1)}, bf16[8192,128]{1,0:T(8,128)(2,1)S(1)}, bf16[96,8192]{1,0:T(8,128)(2,1)...) custom-call(f32[256,128]{1,0:T(8,128)S(1)} %get-tuple-element.40.ref, ...), custom_call_target="tpu_custom_call" | custom-call | flops 1000000000 | bytes 3000000 | tf_op jit(solution)/shard_map/pallas_call | solution.py:418
  7.4 1.5 %collective-permute-done.1.refs_1_ = f32[256,128]{1,0:T(8,128)S(1)} collective-permute-done((f32[256,128]{1,0:T(8,128)S(1)}, f32[256,128]{1,0:T(8,128)S(1)}, u32[]{:S(2)}, u32[]{:S(2)}) %collective-permute-start.1) | collective-permute-done | bytes 131104 | tf_op jit(solution)/shard_map/ppermute | solution.py:450
  8.9 0.0 collective-permute-start.2
  8.9 0.5 %collective-permute-start.3 = (f32[256,128]{1,0:T(8,128)S(1)}, f32[256,128]{1,0:T(8,128)S(1)}, u32[]{:S(2)}, u32[]{:S(2)}) collective-permute-start(f32[256,128]{1,0:T(8,128)S(1)} %get-tuple-element.40.refs_0_), channel_id=1, source_target_pairs={{0,1},{1,0},{2,3},{3,2},{4,5},{5,4},{6,7},{7,6},{8,9},{9,8},{10,11... | collective-permute-start | bytes 393224 | tf_op jit(solution)/shard_map/ppermute | solution.py:450
  9.4 0.0 collective-permute-start.4
  9.4 1.5 %collective-permute-done.refs_1_ = f32[256,128]{1,0:T(8,128)S(1)} collective-permute-done((f32[256,128]{1,0:T(8,128)S(1)}, f32[256,128]{1,0:T(8,128)S(1)}, u32[]{:S(2)}, u32[]{:S(2)}) %collective-permute-start) | collective-permute-done | bytes 131104 | tf_op jit(solution)/shard_map/ppermute | solution.py:450
  10.9 0.0 collective-permute-done.2.refs_4_
  10.9 0.0 collective-permute-start.5
  10.9 0.0 collective-permute-done.3.refs_0_
  10.9 0.1 shard_map.123.refs_3_
  11.0 0.6 %shard_map.124 = (f32[48,16,128]{2,1,0:T(8,128)S(1)}, f32[96,128]{1,0:T(8,128)S(1)}) custom-call(bf16[8192,128]{1,0:T(8,128)(2,1)S(1)} %get-tuple-element.28.refs_0_, bf16[96,8192]{1,0:T(8,128)(2,1)S(1)} %get-tuple-element.29.refs_1_, f32[2,8,32,128]{3,2,1,0:T(8,128)S(1)} %get-tuple-element.34.refs_2_, f32[48,16,128]{2,1,0:T(8,128)S(1)} %shard_map.123.refs_3_, ...), custom_call_target="tpu_custom_call" | custom-call | flops 1000000 | bytes 3000 | tf_op jit(solution)/shard_map/pallas_call | solution.py:418
  11.7 0.0 collective-permute-done.4.refs_0_
  11.7 0.1 shard_map.125.refs_9_
  11.8 0.4 %collective-permute-done.5.refs_10_ = f32[256,128]{1,0:T(8,128)S(1)} collective-permute-done((f32[256,128]{1,0:T(8,128)S(1)}, f32[256,128]{1,0:T(8,128)S(1)}, u32[]{:S(2)}, u32[]{:S(2)}) %collective-permute-start.5) | collective-permute-done | bytes 131104 | tf_op jit(solution)/shard_map/ppermute | solution.py:450
  12.2 2.4 %shard_map.126 = (f32[8,128]{1,0:T(8,128)S(1)}, f32[8,16,128]{2,1,0:T(8,128)}) custom-call(bf16[8192,128]{1,0:T(8,128)(2,1)S(1)} %get-tuple-element.28.refs_0_, bf16[96,8192]{1,0:T(8,128)(2,1)S(1)} %get-tuple-element.29.refs_1_, f32[2,8,32,128]{3,2,1,0:T(8,128)S(1)} %get-tuple-element.34.refs_2_, f32[136,128]{1,0:T(8,128)S(1)} %get-tuple-element.35.refs_3_, ...), custom_call_target="tpu_custom_call" | custom-call | tf_op jit(solution)/shard_map/pallas_call | solution.py:418
  14.6 6.1 %all-to-all-start = ((f32[8,16,128]{2,1,0:T(8,128)}), f32[8,16,128]{2,1,0:T(8,128)S(1)}, u32[]{:S(2)}, u32[]{:S(2)}) async-start(f32[8,16,128]{2,1,0:T(8,128)} %get-tuple-element.48), calls=%async_computation | async-start | bytes 131072 | tf_op jit(solution)/shard_map/all_to_all | solution.py:553
  20.7 0.6 %copy.13 = f32[1,8,128]{2,1,0:T(8,128)} copy(f32[1,8,128]{2,1,0:T(8,128)S(1)} %bitcast.32) | data formatting | bytes 8192
  21.3 6.3 %all-to-all-done = f32[8,16,128]{2,1,0:T(8,128)S(1)} async-done(((f32[8,16,128]{2,1,0:T(8,128)}), f32[8,16,128]{2,1,0:T(8,128)S(1)}, u32[]{:S(2)}, u32[]{:S(2)}) %all-to-all-start) | async-done | bytes 65568 | tf_op jit(solution)/shard_map/all_to_all | solution.py:553
  27.6 1.3 %slice_subtract_fusion = (f32[1,8,128]{2,1,0:T(8,128)}, f32[1,8,128]{2,1,0:T(8,128)}) fusion(f32[8,16,128]{2,1,0:T(8,128)} %get-tuple-element.48, f32[8,128]{1,0:T(8,128)S(1)} %get-tuple-element.51, f32[8,128]{1,0:T(8,128)S(1)} %get-tuple-element.52, f32[8,128]{1,0:T(8,128)S(1)} %get-tuple-element.50, f32[8,128]{1,0:T(8,128)S(1)} %get-tuple-element.49), kind=kLoop, calls=%fused_computation.12 | loop fusion | flops 47104 | bytes 32768 | tf_op jit(solution)/shard_map/sub | solution.py:390
  (1 shorter events, 0.0 us)
Async XLA Ops:
  1.6 7.3 %collective-permute-start.1 = (f32[256,128]{1,0:T(8,128)S(1)}, f32[256,128]{1,0:T(8,128)S(1)}, u32[]{:S(2)}, u32[]{:S(2)}) collective-permute-start(f32[256,128]{1,0:T(8,128)S(1)} %get-tuple-element.40.refs_0_), channel_id=1, source_target_pairs={{0,2},{1,3},{2,0},{3,1},{4,6},{5,7},{6,4},{7,5},{8,10},{9,11},{10,... | collective-permute-start | bytes 393224 | tf_op jit(solution)/shard_map/ppermute | solution.py:450
  4.6 6.3 %collective-permute-start = (f32[256,128]{1,0:T(8,128)S(1)}, f32[256,128]{1,0:T(8,128)S(1)}, u32[]{:S(2)}, u32[]{:S(2)}) collective-permute-start(f32[256,128]{1,0:T(8,128)S(1)} %get-tuple-element.45.refs_1_), channel_id=1, source_target_pairs={{0,2},{1,3},{2,0},{3,1},{4,6},{5,7},{6,4},{7,5},{8,10},{9,11},{10,... | collective-permute-start | bytes 393224 | tf_op jit(solution)/shard_map/ppermute | solution.py:450
  8.9 2.0 %collective-permute-start.2 = (f32[256,128]{1,0:T(8,128)S(1)}, f32[256,128]{1,0:T(8,128)S(1)}, u32[]{:S(2)}, u32[]{:S(2)}) collective-permute-start(f32[256,128]{1,0:T(8,128)S(1)} %collective-permute-done.1.refs_1_), channel_id=1, source_target_pairs={{0,1},{1,0},{2,3},{3,2},{4,5},{5,4},{6,7},{7,6},{8,9},{9,8},{10,11... | collective-permute-start | bytes 393224 | tf_op jit(solution)/shard_map/ppermute | solution.py:450
  8.9 2.0 %collective-permute-start.3 = (f32[256,128]{1,0:T(8,128)S(1)}, f32[256,128]{1,0:T(8,128)S(1)}, u32[]{:S(2)}, u32[]{:S(2)}) collective-permute-start(f32[256,128]{1,0:T(8,128)S(1)} %get-tuple-element.40.refs_0_), channel_id=1, source_target_pairs={{0,1},{1,0},{2,3},{3,2},{4,5},{5,4},{6,7},{7,6},{8,9},{9,8},{10,11... | collective-permute-start | bytes 393224 | tf_op jit(solution)/shard_map/ppermute | solution.py:450
  9.4 2.3 %collective-permute-start.4 = (f32[256,128]{1,0:T(8,128)S(1)}, f32[256,128]{1,0:T(8,128)S(1)}, u32[]{:S(2)}, u32[]{:S(2)}) collective-permute-start(f32[256,128]{1,0:T(8,128)S(1)} %get-tuple-element.45.refs_1_), channel_id=1, source_target_pairs={{0,1},{1,0},{2,3},{3,2},{4,5},{5,4},{6,7},{7,6},{8,9},{9,8},{10,11... | collective-permute-start | bytes 393224 | tf_op jit(solution)/shard_map/ppermute | solution.py:450
  10.9 1.3 %collective-permute-start.5 = (f32[256,128]{1,0:T(8,128)S(1)}, f32[256,128]{1,0:T(8,128)S(1)}, u32[]{:S(2)}, u32[]{:S(2)}) collective-permute-start(f32[256,128]{1,0:T(8,128)S(1)} %collective-permute-done.refs_1_), channel_id=1, source_target_pairs={{0,1},{1,0},{2,3},{3,2},{4,5},{5,4},{6,7},{7,6},{8,9},{9,8},{10,11... | collective-permute-start | bytes 393224 | tf_op jit(solution)/shard_map/ppermute | solution.py:450
  14.6 13.0 %all-to-all-start = ((f32[8,16,128]{2,1,0:T(8,128)}), f32[8,16,128]{2,1,0:T(8,128)S(1)}, u32[]{:S(2)}, u32[]{:S(2)}) async-start(f32[8,16,128]{2,1,0:T(8,128)} %get-tuple-element.48), calls=%async_computation | async-start | bytes 131072 | tf_op jit(solution)/shard_map/all_to_all | solution.py:553

commit v6 on v5

--- a/solution.py
+++ b/solution.py
@@ -306,7 +306,7 @@
     hot_ref, mask_ref, found_ref, state_ref, own_ref, first_ref, second_ref = refs[:7]
     prod_refs, partial_refs = refs[7 : 6 + pieces], refs[6 + pieces : 5 + 2 * pieces]
     before_ref, slot_refs = refs[5 + 2 * pieces], refs[6 + 2 * pieces : 6 + 2 * pieces + slots]
-    gain_out_ref, send_ref, last_ref, total_ref = refs[6 + 2 * pieces + slots : -pieces]
+    gain_out_ref, sum_ref, send_ref, last_ref, total_ref = refs[6 + 2 * pieces + slots : -pieces]
     term_refs = refs[-pieces:]
     blocks = mask_ref.shape[0] * 2 // (3 * PACK)
     gains = [state_ref[pl.ds(j * SUBS, blocks), :] for j in range(SUBS)]
@@ -350,6 +350,7 @@
     part = total_ref[pl.ds(pl.multiple_of(place * SUBS, SUBS), SUBS), :]
     gain_out_ref[...] = part
     combined, mark = part + own_ref[:SUBS, :], own_ref[SUBS:, :]
+    sum_ref[...] = combined
     for channel in range(send_ref.shape[0]):
         send_ref[channel, :SUBS, :] = combined
         send_ref[channel, SUBS:, :] = mark
@@ -360,17 +361,22 @@
     return [None, position, 1.5 * square - 0.5, (2.5 * square - 1.5) * position]
 
 
-def fit(gram_factor, parts, send):
-    scale = float(parts.shape[0]) - 1.0
+def fit_kernel(gram_factor, parts_ref, own_ref, gain_ref, sum_ref, *refs):
+    gain_hbm, consensus_hbm, dual_hbm, consensus_ref, dual_ref, sem = refs
+    gain_copy = pltpu.make_async_copy(gain_ref, gain_hbm, sem.at[0])
+    gain_copy.start()
+    channels = parts_ref.shape[0]
+    scale = float(channels) - 1.0
 
     def basis(channel):
         return legendre(2.0 * channel / scale - 1.0)
 
-    value = parts[:, :SUBS]
-    moments = [
-        jnp.sum(value if weight is None else weight * value, axis=0)
-        for weight in basis(parts[:, SUBS:])
-    ]
+    moments = [None] * 4
+    for channel in range(channels):
+        value = parts_ref[channel, :SUBS, :]
+        for k, weight in enumerate(basis(parts_ref[channel, SUBS:, :])):
+            add = value if weight is None else weight * value
+            moments[k] = add if moments[k] is None else moments[k] + add
     middle = []
     for k in range(4):
         rest = moments[k]
@@ -383,11 +389,19 @@
         for later in range(k + 1, 4):
             rest = rest - gram_factor[later][k] * coeffs[later]
         coeffs[k] = rest * (1.0 / gram_factor[k][k])
-    own = basis(send[0, SUBS:])
+    own = basis(own_ref[SUBS:, :])
     fitted = coeffs[0]
     for k in range(1, 4):
         fitted = fitted + own[k] * coeffs[k]
-    return fitted, send[0, :SUBS] - fitted
+    consensus_ref[...] = fitted
+    dual_ref[...] = sum_ref[...] - fitted
+    consensus_copy = pltpu.make_async_copy(consensus_ref, consensus_hbm, sem.at[1])
+    dual_copy = pltpu.make_async_copy(dual_ref, dual_hbm, sem.at[2])
+    consensus_copy.start()
+    dual_copy.start()
+    gain_copy.wait()
+    consensus_copy.wait()
+    dual_copy.wait()
 
 
 def gram_cholesky(channels):
@@ -531,9 +545,10 @@
         limit=16,
         micros=0.001,
     )(hot, mask, found, summed[0], *last[0])
-    gain_part, send = call(
+    part = vmem((SUBS, LANES), F32)
+    gain_part, combined, send = call(
         lambda *refs: sweeps_kernel((count, len(last[1])), *refs),
-        [vmem((SUBS, LANES), F32), vmem((channels, 2 * SUBS, LANES), F32)],
+        [part, part, vmem((channels, 2 * SUBS, LANES), F32)],
         "v" * (10 + len(last[1])),
         [products[1], totals, *terms],
         limit=16,
@@ -551,8 +566,13 @@
         *last[1],
     )
     parts = lax.all_to_all(send, "freq", 0, 0)
-    consensus_out, dual_out = fit(gram_cholesky(channels), parts, send)
-    return tuple(array[None] for array in (gain_part, consensus_out, dual_out))
+    outs = call(
+        lambda *refs: fit_kernel(gram_cholesky(channels), *refs),
+        [pltpu.HBM((SUBS, LANES), F32)] * 3,
+        "vvvv",
+        [part, part, pltpu.SemaphoreType.DMA((3,))],
+    )(parts, own, gain_part, combined)
+    return tuple(array[None] for array in outs)
 
 
 def solution(mesh):

time: 29.3 us -> 27.7 us (0.945)
  blocking collectives: 0 us -> 12.8 us
  waiting for transfers between devices: 9.72 us -> 3.41 us
  starting transfers between devices: 9.66 us -> 3.6 us
  other arithmetic: 1.33 us -> 0 us
  local copies, waits for them, and re-layouts: 0.59 us -> 0 us
    all_to_all x0 -> x1, blocking collectives: none -> 12.8 us  [shards(): parts = lax.all_to_all(send, 'freq', 0, 0)]
    all_to_all x1 -> x0, waiting for transfers between devices: 6.31 us -> none  [shards(): parts = lax.all_to_all(send, 'freq', 0, 0)]
    all_to_all x1 -> x0, starting transfers between devices: 6.07 us -> none  [shards(): parts = lax.all_to_all(send, 'freq', 0, 0)]
    sub x1 -> x0, other arithmetic: 1.31 us -> none  [fit(): return (fitted, send[0, :SUBS] - fitted)]
    unnamed x1 -> x0, local copies, waits for them, and re-layouts: 0.59 us -> none
    pallas_call x6 -> x7, Pallas kernels: 6.29 us -> 6.34 us  [placed(): run(*(arg if space == 's' else pltpu.with_memory_space_constraint(arg, SP...]
  transfers between devices with their start and end apart: 7 -> 6, of which waited for: 4 -> 3; matrix products, arithmetic and copies ran while one was open for 2% -> 0% of each run, Pallas kernels for 10% -> 11%
where the time goes in v6:
time: 27.7 us; the launch traced here: 27.4 us
  blocking collectives  12.8 us (46%)
  Pallas kernels  6.34 us (23%)
  starting transfers between devices  3.6 us (13%)
  waiting for transfers between devices  3.41 us (12%)
  between operations  1.34 us (5%)
    all_to_all x1, blocking collectives, shards(): parts = lax.all_to_all(send, 'freq', 0, 0)  12.8 us
    pallas_call x7, Pallas kernels, placed(): run(*(arg if space == 's' else pltpu.with_memory_space_constraint(arg, SP...  6.34 us
    ppermute x6, starting transfers between devices, swap(): return lax.ppermute(array, 'tm', [(i, i ^ step) for i in range(slots)])  3.6 us
    ppermute x6, waiting for transfers between devices, swap(): return lax.ppermute(array, 'tm', [(i, i ^ step) for i in range(slots)])  3.41 us
  transfers between devices with their start and end apart: 6, of which 3 were waited for; matrix products, arithmetic and copies ran while one was open for 0% of the time, Pallas kernels for 11%

profile of v6, /device:TPU:0, one launch (start us, length us, event | category | flops | bytes accessed | tf_op | source)
XLA Modules:
  0.0 27.4 jit_solution(8977861957702402198)
XLA Ops:
  0.6 0.9 %shard_map.121 = (f32[256,128]{1,0:T(8,128)S(1)}, f32[256,128]{1,0:T(8,128)S(1)}) custom-call(bf16[8,4096]{1,0:T(8,128)(2,1)} %bitcast.12, bf16[8,4096]{1,0:T(8,128)(2,1)} %bitcast.13, s32[1,4096]{1,0:T(1,128)} %bitcast.14), custom_call_target="tpu_custom_call" | custom-call | tf_op jit(solution)/shard_map/pallas_call | solution.py:432
  1.6 3.0 %collective-permute-start.1 = (f32[256,128]{1,0:T(8,128)S(1)}, f32[256,128]{1,0:T(8,128)S(1)}, u32[]{:S(2)}, u32[]{:S(2)}) collective-permute-start(f32[256,128]{1,0:T(8,128)S(1)} %get-tuple-element.44.refs_0_), channel_id=1, source_target_pairs={{0,2},{1,3},{2,0},{3,1},{4,6},{5,7},{6,4},{7,5},{8,10},{9,11},{10,... | collective-permute-start | bytes 393224 | tf_op jit(solution)/shard_map/ppermute | solution.py:464
  4.6 0.1 collective-permute-start
  5.3 2.1 %shard_map.122 = (f32[48,16,128]{2,1,0:T(8,128)S(1)}, f32[48,16,128]{2,1,0:T(8,128)S(1)}, bf16[8192,128]{1,0:T(8,128)(2,1)S(1)}, bf16[96,8192]{1,0:T(8,128)(2,1)...) custom-call(f32[256,128]{1,0:T(8,128)S(1)} %get-tuple-element.44.ref, ...), custom_call_target="tpu_custom_call" | custom-call | flops 1000000000 | bytes 3000000 | tf_op jit(solution)/shard_map/pallas_call | solution.py:432
  7.4 1.5 %collective-permute-done.1.refs_1_ = f32[256,128]{1,0:T(8,128)S(1)} collective-permute-done((f32[256,128]{1,0:T(8,128)S(1)}, f32[256,128]{1,0:T(8,128)S(1)}, u32[]{:S(2)}, u32[]{:S(2)}) %collective-permute-start.1) | collective-permute-done | bytes 131104 | tf_op jit(solution)/shard_map/ppermute | solution.py:464
  8.9 0.0 collective-permute-start.2
  8.9 0.5 %collective-permute-start.3 = (f32[256,128]{1,0:T(8,128)S(1)}, f32[256,128]{1,0:T(8,128)S(1)}, u32[]{:S(2)}, u32[]{:S(2)}) collective-permute-start(f32[256,128]{1,0:T(8,128)S(1)} %get-tuple-element.44.refs_0_), channel_id=1, source_target_pairs={{0,1},{1,0},{2,3},{3,2},{4,5},{5,4},{6,7},{7,6},{8,9},{9,8},{10,11... | collective-permute-start | bytes 393224 | tf_op jit(solution)/shard_map/ppermute | solution.py:464
  9.4 0.0 collective-permute-start.4
  9.4 1.5 %collective-permute-done.refs_1_ = f32[256,128]{1,0:T(8,128)S(1)} collective-permute-done((f32[256,128]{1,0:T(8,128)S(1)}, f32[256,128]{1,0:T(8,128)S(1)}, u32[]{:S(2)}, u32[]{:S(2)}) %collective-permute-start) | collective-permute-done | bytes 131104 | tf_op jit(solution)/shard_map/ppermute | solution.py:464
  10.9 0.0 collective-permute-done.2.refs_4_
  10.9 0.0 collective-permute-start.5
  10.9 0.0 collective-permute-done.3.refs_0_
  10.9 0.1 shard_map.123.refs_3_
  11.0 0.6 %shard_map.124 = (f32[48,16,128]{2,1,0:T(8,128)S(1)}, f32[96,128]{1,0:T(8,128)S(1)}) custom-call(bf16[8192,128]{1,0:T(8,128)(2,1)S(1)} %get-tuple-element.32.refs_0_, bf16[96,8192]{1,0:T(8,128)(2,1)S(1)} %get-tuple-element.33.refs_1_, f32[2,8,32,128]{3,2,1,0:T(8,128)S(1)} %get-tuple-element.38.refs_2_, f32[48,16,128]{2,1,0:T(8,128)S(1)} %shard_map.123.refs_3_, ...), custom_call_target="tpu_custom_call" | custom-call | flops 1000000 | bytes 3000 | tf_op jit(solution)/shard_map/pallas_call | solution.py:432
  11.7 0.0 collective-permute-done.4.refs_0_
  11.7 0.1 shard_map.125.refs_9_
  11.8 0.4 %collective-permute-done.5.refs_10_ = f32[256,128]{1,0:T(8,128)S(1)} collective-permute-done((f32[256,128]{1,0:T(8,128)S(1)}, f32[256,128]{1,0:T(8,128)S(1)}, u32[]{:S(2)}, u32[]{:S(2)}) %collective-permute-start.5) | collective-permute-done | bytes 131104 | tf_op jit(solution)/shard_map/ppermute | solution.py:464
  12.2 1.8 %shard_map.126 = (f32[8,128]{1,0:T(8,128)S(1)}, f32[8,128]{1,0:T(8,128)S(1)}, f32[8,16,128]{2,1,0:T(8,128)S(1)}) custom-call(bf16[8192,128]{1,0:T(8,128)(2,1)S(1)} %get-tuple-element.32.refs_0_, bf16[96,8192]{1,0:T(8,128)(2,1)S(1)} %get-tuple-element.33.refs_1_, f32[2,8,32,128]{3,2,1,0:T(8,128)S(1)} %get-tuple-element.38.refs_2_, ...), custom_call_target="tpu_custom_call" | custom-call | tf_op jit(solution)/shard_map/pallas_call | solution.py:432
  14.0 12.8 %all_to_all.5.refs_0_ = f32[8,16,128]{2,1,0:T(8,128)S(1)} all-to-all(f32[8,16,128]{2,1,0:T(8,128)S(1)} %get-tuple-element.51), channel_id=1, replica_groups=mesh['freq'=8,'tm'=4] {'freq'}, dimensions={0} | all-to-all | bytes 131072 | tf_op jit(solution)/shard_map/all_to_all | solution.py:568
  26.8 0.7 %shard_map.127 = (f32[8,128]{1,0:T(8,128)}, f32[8,128]{1,0:T(8,128)}, f32[8,128]{1,0:T(8,128)}) custom-call(f32[8,16,128]{2,1,0:T(8,128)S(1)} %all_to_all.5.refs_0_, f32[16,128]{1,0:T(8,128)S(1)} %get-tuple-element.40.refs_4_.refs_1_, f32[8,128]{1,0:T(8,128)S(1)} %get-tuple-element.52.refs_2_, f32[8,128]{1,0:T(8,128)S(1)} %get-tuple-element.53.refs_3_), custom_call_target="tpu_custom_call" | custom-call | tf_op jit(solution)/shard_map/pallas_call | solution.py:432
Async XLA Ops:
  1.6 7.3 %collective-permute-start.1 = (f32[256,128]{1,0:T(8,128)S(1)}, f32[256,128]{1,0:T(8,128)S(1)}, u32[]{:S(2)}, u32[]{:S(2)}) collective-permute-start(f32[256,128]{1,0:T(8,128)S(1)} %get-tuple-element.44.refs_0_), channel_id=1, source_target_pairs={{0,2},{1,3},{2,0},{3,1},{4,6},{5,7},{6,4},{7,5},{8,10},{9,11},{10,... | collective-permute-start | bytes 393224 | tf_op jit(solution)/shard_map/ppermute | solution.py:464
  4.6 6.3 %collective-permute-start = (f32[256,128]{1,0:T(8,128)S(1)}, f32[256,128]{1,0:T(8,128)S(1)}, u32[]{:S(2)}, u32[]{:S(2)}) collective-permute-start(f32[256,128]{1,0:T(8,128)S(1)} %get-tuple-element.49.refs_1_), channel_id=1, source_target_pairs={{0,2},{1,3},{2,0},{3,1},{4,6},{5,7},{6,4},{7,5},{8,10},{9,11},{10,... | collective-permute-start | bytes 393224 | tf_op jit(solution)/shard_map/ppermute | solution.py:464
  8.9 2.0 %collective-permute-start.2 = (f32[256,128]{1,0:T(8,128)S(1)}, f32[256,128]{1,0:T(8,128)S(1)}, u32[]{:S(2)}, u32[]{:S(2)}) collective-permute-start(f32[256,128]{1,0:T(8,128)S(1)} %collective-permute-done.1.refs_1_), channel_id=1, source_target_pairs={{0,1},{1,0},{2,3},{3,2},{4,5},{5,4},{6,7},{7,6},{8,9},{9,8},{10,11... | collective-permute-start | bytes 393224 | tf_op jit(solution)/shard_map/ppermute | solution.py:464
  8.9 2.0 %collective-permute-start.3 = (f32[256,128]{1,0:T(8,128)S(1)}, f32[256,128]{1,0:T(8,128)S(1)}, u32[]{:S(2)}, u32[]{:S(2)}) collective-permute-start(f32[256,128]{1,0:T(8,128)S(1)} %get-tuple-element.44.refs_0_), channel_id=1, source_target_pairs={{0,1},{1,0},{2,3},{3,2},{4,5},{5,4},{6,7},{7,6},{8,9},{9,8},{10,11... | collective-permute-start | bytes 393224 | tf_op jit(solution)/shard_map/ppermute | solution.py:464
  9.4 2.3 %collective-permute-start.4 = (f32[256,128]{1,0:T(8,128)S(1)}, f32[256,128]{1,0:T(8,128)S(1)}, u32[]{:S(2)}, u32[]{:S(2)}) collective-permute-start(f32[256,128]{1,0:T(8,128)S(1)} %get-tuple-element.49.refs_1_), channel_id=1, source_target_pairs={{0,1},{1,0},{2,3},{3,2},{4,5},{5,4},{6,7},{7,6},{8,9},{9,8},{10,11... | collective-permute-start | bytes 393224 | tf_op jit(solution)/shard_map/ppermute | solution.py:464
  10.9 1.3 %collective-permute-start.5 = (f32[256,128]{1,0:T(8,128)S(1)}, f32[256,128]{1,0:T(8,128)S(1)}, u32[]{:S(2)}, u32[]{:S(2)}) collective-permute-start(f32[256,128]{1,0:T(8,128)S(1)} %collective-permute-done.refs_1_), channel_id=1, source_target_pairs={{0,1},{1,0},{2,3},{3,2},{4,5},{5,4},{6,7},{7,6},{8,9},{9,8},{10,11... | collective-permute-start | bytes 393224 | tf_op jit(solution)/shard_map/ppermute | solution.py:464

commit v7 on v6

--- a/solution.py
+++ b/solution.py
@@ -11,6 +11,7 @@
 SUBS = 8
 PRODS = 48
 TERMS = 24
+SENT = 9
 PACK = 16
 F32 = jnp.float32
 BF16 = jnp.bfloat16
@@ -351,9 +352,9 @@
     gain_out_ref[...] = part
     combined, mark = part + own_ref[:SUBS, :], own_ref[SUBS:, :]
     sum_ref[...] = combined
-    for channel in range(send_ref.shape[0]):
-        send_ref[channel, :SUBS, :] = combined
-        send_ref[channel, SUBS:, :] = mark
+    for channel in range(send_ref.shape[0] // SENT):
+        send_ref[pl.ds(channel * SENT, SUBS), :] = combined
+        send_ref[pl.ds(channel * SENT + SUBS, 1), :] = mark[:1]
 
 
 def legendre(position):
@@ -365,7 +366,7 @@
     gain_hbm, consensus_hbm, dual_hbm, consensus_ref, dual_ref, sem = refs
     gain_copy = pltpu.make_async_copy(gain_ref, gain_hbm, sem.at[0])
     gain_copy.start()
-    channels = parts_ref.shape[0]
+    channels = parts_ref.shape[0] // SENT
     scale = float(channels) - 1.0
 
     def basis(channel):
@@ -373,8 +374,8 @@
 
     moments = [None] * 4
     for channel in range(channels):
-        value = parts_ref[channel, :SUBS, :]
-        for k, weight in enumerate(basis(parts_ref[channel, SUBS:, :])):
+        value = parts_ref[pl.ds(channel * SENT, SUBS), :]
+        for k, weight in enumerate(basis(parts_ref[pl.ds(channel * SENT + SUBS, 1), :])):
             add = value if weight is None else weight * value
             moments[k] = add if moments[k] is None else moments[k] + add
     middle = []
@@ -548,7 +549,7 @@
     part = vmem((SUBS, LANES), F32)
     gain_part, combined, send = call(
         lambda *refs: sweeps_kernel((count, len(last[1])), *refs),
-        [part, part, vmem((channels, 2 * SUBS, LANES), F32)],
+        [part, part, vmem((channels * SENT, LANES), F32)],
         "v" * (10 + len(last[1])),
         [products[1], totals, *terms],
         limit=16,
@@ -565,7 +566,8 @@
         summed[1],
         *last[1],
     )
-    parts = lax.all_to_all(send, "freq", 0, 0)
+    parts = lax.all_to_all(send.reshape(channels, 1, SENT * LANES), "freq", 0, 0)
+    parts = parts.reshape(channels * SENT, LANES)
     outs = call(
         lambda *refs: fit_kernel(gram_cholesky(channels), *refs),
         [pltpu.HBM((SUBS, LANES), F32)] * 3,

time: 27.7 us -> 27.5 us (level)
  no operation moved by 1% of the time
where the time goes in v7:
time: 27.5 us; the launch traced here: 27.3 us
  blocking collectives  12.6 us (46%)
  Pallas kernels  6.34 us (23%)
  starting transfers between devices  3.6 us (13%)
  waiting for transfers between devices  3.41 us (12%)
  between operations  1.34 us (5%)
    all_to_all x1, blocking collectives, shards(): lax.all_to_all(send.reshape(channels, 1, SENT * LANES), 'freq', 0, 0)  12.6 us
    pallas_call x7, Pallas kernels, placed(): run(*(arg if space == 's' else pltpu.with_memory_space_constraint(arg, SP...  6.34 us
    ppermute x6, starting transfers between devices, swap(): return lax.ppermute(array, 'tm', [(i, i ^ step) for i in range(slots)])  3.6 us
    ppermute x6, waiting for transfers between devices, swap(): return lax.ppermute(array, 'tm', [(i, i ^ step) for i in range(slots)])  3.41 us
  transfers between devices with their start and end apart: 6, of which 3 were waited for; matrix products, arithmetic and copies ran while one was open for 0% of the time, Pallas kernels for 11%

profile of v7, /device:TPU:0, one launch (start us, length us, event | category | flops | bytes accessed | tf_op | source)
XLA Modules:
  0.0 27.3 jit_solution(4977097770819761093)
XLA Ops:
  0.6 0.9 %shard_map.121 = (f32[256,128]{1,0:T(8,128)S(1)}, f32[256,128]{1,0:T(8,128)S(1)}) custom-call(bf16[8,4096]{1,0:T(8,128)(2,1)} %bitcast.16, bf16[8,4096]{1,0:T(8,128)(2,1)} %bitcast.17, s32[1,4096]{1,0:T(1,128)} %bitcast.18), custom_call_target="tpu_custom_call" | custom-call | tf_op jit(solution)/shard_map/pallas_call | solution.py:433
  1.6 3.0 %collective-permute-start.1 = (f32[256,128]{1,0:T(8,128)S(1)}, f32[256,128]{1,0:T(8,128)S(1)}, u32[]{:S(2)}, u32[]{:S(2)}) collective-permute-start(f32[256,128]{1,0:T(8,128)S(1)} %get-tuple-element.44.refs_0_), channel_id=1, source_target_pairs={{0,2},{1,3},{2,0},{3,1},{4,6},{5,7},{6,4},{7,5},{8,10},{9,11},{10,... | collective-permute-start | bytes 393224 | tf_op jit(solution)/shard_map/ppermute | solution.py:465
  4.6 0.1 collective-permute-start
  5.3 2.1 %shard_map.122 = (f32[48,16,128]{2,1,0:T(8,128)S(1)}, f32[48,16,128]{2,1,0:T(8,128)S(1)}, bf16[8192,128]{1,0:T(8,128)(2,1)S(1)}, bf16[96,8192]{1,0:T(8,128)(2,1)...) custom-call(f32[256,128]{1,0:T(8,128)S(1)} %get-tuple-element.44.ref, ...), custom_call_target="tpu_custom_call" | custom-call | flops 1000000000 | bytes 3000000 | tf_op jit(solution)/shard_map/pallas_call | solution.py:433
  7.4 1.5 %collective-permute-done.1.refs_1_ = f32[256,128]{1,0:T(8,128)S(1)} collective-permute-done((f32[256,128]{1,0:T(8,128)S(1)}, f32[256,128]{1,0:T(8,128)S(1)}, u32[]{:S(2)}, u32[]{:S(2)}) %collective-permute-start.1) | collective-permute-done | bytes 131104 | tf_op jit(solution)/shard_map/ppermute | solution.py:465
  8.9 0.0 collective-permute-start.2
  8.9 0.5 %collective-permute-start.3 = (f32[256,128]{1,0:T(8,128)S(1)}, f32[256,128]{1,0:T(8,128)S(1)}, u32[]{:S(2)}, u32[]{:S(2)}) collective-permute-start(f32[256,128]{1,0:T(8,128)S(1)} %get-tuple-element.44.refs_0_), channel_id=1, source_target_pairs={{0,1},{1,0},{2,3},{3,2},{4,5},{5,4},{6,7},{7,6},{8,9},{9,8},{10,11... | collective-permute-start | bytes 393224 | tf_op jit(solution)/shard_map/ppermute | solution.py:465
  9.4 0.0 collective-permute-start.4
  9.4 1.5 %collective-permute-done.refs_1_ = f32[256,128]{1,0:T(8,128)S(1)} collective-permute-done((f32[256,128]{1,0:T(8,128)S(1)}, f32[256,128]{1,0:T(8,128)S(1)}, u32[]{:S(2)}, u32[]{:S(2)}) %collective-permute-start) | collective-permute-done | bytes 131104 | tf_op jit(solution)/shard_map/ppermute | solution.py:465
  10.9 0.0 collective-permute-done.2.refs_4_
  10.9 0.0 collective-permute-start.5
  10.9 0.0 collective-permute-done.3.refs_0_
  10.9 0.1 shard_map.123.refs_3_
  11.0 0.6 %shard_map.124 = (f32[48,16,128]{2,1,0:T(8,128)S(1)}, f32[96,128]{1,0:T(8,128)S(1)}) custom-call(bf16[8192,128]{1,0:T(8,128)(2,1)S(1)} %get-tuple-element.32.refs_0_, bf16[96,8192]{1,0:T(8,128)(2,1)S(1)} %get-tuple-element.33.refs_1_, f32[2,8,32,128]{3,2,1,0:T(8,128)S(1)} %get-tuple-element.38.refs_2_, f32[48,16,128]{2,1,0:T(8,128)S(1)} %shard_map.123.refs_3_, ...), custom_call_target="tpu_custom_call" | custom-call | flops 1000000 | bytes 3000 | tf_op jit(solution)/shard_map/pallas_call | solution.py:433
  11.7 0.0 collective-permute-done.4.refs_0_
  11.7 0.1 shard_map.125.refs_9_
  11.8 0.4 %collective-permute-done.5.refs_10_ = f32[256,128]{1,0:T(8,128)S(1)} collective-permute-done((f32[256,128]{1,0:T(8,128)S(1)}, f32[256,128]{1,0:T(8,128)S(1)}, u32[]{:S(2)}, u32[]{:S(2)}) %collective-permute-start.5) | collective-permute-done | bytes 131104 | tf_op jit(solution)/shard_map/ppermute | solution.py:465
  12.2 1.8 %shard_map.126 = (f32[8,128]{1,0:T(8,128)S(1)}, f32[8,128]{1,0:T(8,128)S(1)}, f32[72,128]{1,0:T(8,128)S(1)}) custom-call(bf16[8192,128]{1,0:T(8,128)(2,1)S(1)} %get-tuple-element.32.refs_0_, bf16[96,8192]{1,0:T(8,128)(2,1)S(1)} %get-tuple-element.33.refs_1_, f32[2,8,32,128]{3,2,1,0:T(8,128)S(1)} %get-tuple-element.38.refs_2_, ...), custom_call_target="tpu_custom_call" | custom-call | tf_op jit(solution)/shard_map/pallas_call | solution.py:433
  14.0 12.6 %all_to_all.5 = f32[8,1,1152]{2,1,0:T(1,128)S(1)} all-to-all(f32[8,1,1152]{2,1,0:T(1,128)S(1)} %bitcast.15), channel_id=1, replica_groups=mesh['freq'=8,'tm'=4] {'freq'}, dimensions={0} | all-to-all | bytes 73728 | tf_op jit(solution)/shard_map/all_to_all | solution.py:569
  26.6 0.7 %shard_map.127 = (f32[8,128]{1,0:T(8,128)}, f32[8,128]{1,0:T(8,128)}, f32[8,128]{1,0:T(8,128)}) custom-call(f32[72,128]{1,0:T(8,128)S(1)} %bitcast.14, f32[16,128]{1,0:T(8,128)S(1)} %get-tuple-element.40.refs_4_.refs_1_, f32[8,128]{1,0:T(8,128)S(1)} %get-tuple-element.52.refs_2_, f32[8,128]{1,0:T(8,128)S(1)} %get-tuple-element.53.refs_3_), custom_call_target="tpu_custom_call" | custom-call | tf_op jit(solution)/shard_map/pallas_call | solution.py:433
Async XLA Ops:
  1.6 7.3 %collective-permute-start.1 = (f32[256,128]{1,0:T(8,128)S(1)}, f32[256,128]{1,0:T(8,128)S(1)}, u32[]{:S(2)}, u32[]{:S(2)}) collective-permute-start(f32[256,128]{1,0:T(8,128)S(1)} %get-tuple-element.44.refs_0_), channel_id=1, source_target_pairs={{0,2},{1,3},{2,0},{3,1},{4,6},{5,7},{6,4},{7,5},{8,10},{9,11},{10,... | collective-permute-start | bytes 393224 | tf_op jit(solution)/shard_map/ppermute | solution.py:465
  4.6 6.3 %collective-permute-start = (f32[256,128]{1,0:T(8,128)S(1)}, f32[256,128]{1,0:T(8,128)S(1)}, u32[]{:S(2)}, u32[]{:S(2)}) collective-permute-start(f32[256,128]{1,0:T(8,128)S(1)} %get-tuple-element.49.refs_1_), channel_id=1, source_target_pairs={{0,2},{1,3},{2,0},{3,1},{4,6},{5,7},{6,4},{7,5},{8,10},{9,11},{10,... | collective-permute-start | bytes 393224 | tf_op jit(solution)/shard_map/ppermute | solution.py:465
  8.9 2.0 %collective-permute-start.2 = (f32[256,128]{1,0:T(8,128)S(1)}, f32[256,128]{1,0:T(8,128)S(1)}, u32[]{:S(2)}, u32[]{:S(2)}) collective-permute-start(f32[256,128]{1,0:T(8,128)S(1)} %collective-permute-done.1.refs_1_), channel_id=1, source_target_pairs={{0,1},{1,0},{2,3},{3,2},{4,5},{5,4},{6,7},{7,6},{8,9},{9,8},{10,11... | collective-permute-start | bytes 393224 | tf_op jit(solution)/shard_map/ppermute | solution.py:465
  8.9 2.0 %collective-permute-start.3 = (f32[256,128]{1,0:T(8,128)S(1)}, f32[256,128]{1,0:T(8,128)S(1)}, u32[]{:S(2)}, u32[]{:S(2)}) collective-permute-start(f32[256,128]{1,0:T(8,128)S(1)} %get-tuple-element.44.refs_0_), channel_id=1, source_target_pairs={{0,1},{1,0},{2,3},{3,2},{4,5},{5,4},{6,7},{7,6},{8,9},{9,8},{10,11... | collective-permute-start | bytes 393224 | tf_op jit(solution)/shard_map/ppermute | solution.py:465
  9.4 2.3 %collective-permute-start.4 = (f32[256,128]{1,0:T(8,128)S(1)}, f32[256,128]{1,0:T(8,128)S(1)}, u32[]{:S(2)}, u32[]{:S(2)}) collective-permute-start(f32[256,128]{1,0:T(8,128)S(1)} %get-tuple-element.49.refs_1_), channel_id=1, source_target_pairs={{0,1},{1,0},{2,3},{3,2},{4,5},{5,4},{6,7},{7,6},{8,9},{9,8},{10,11... | collective-permute-start | bytes 393224 | tf_op jit(solution)/shard_map/ppermute | solution.py:465
  10.9 1.3 %collective-permute-start.5 = (f32[256,128]{1,0:T(8,128)S(1)}, f32[256,128]{1,0:T(8,128)S(1)}, u32[]{:S(2)}, u32[]{:S(2)}) collective-permute-start(f32[256,128]{1,0:T(8,128)S(1)} %collective-permute-done.refs_1_), channel_id=1, source_target_pairs={{0,1},{1,0},{2,3},{3,2},{4,5},{5,4},{6,7},{7,6},{8,9},{9,8},{10,11... | collective-permute-start | bytes 393224 | tf_op jit(solution)/shard_map/ppermute | solution.py:465

commit v8 on v7

--- a/solution.py
+++ b/solution.py
@@ -31,23 +31,20 @@
     return copies
 
 
-def widen_kernel(vis_hbm, model_hbm, keep_hbm, *refs):
-    vis_ref, model_ref, keep_ref, sem = refs[-4:]
-    copies = copy_in(
-        [(vis_hbm, vis_ref), (keep_hbm, keep_ref), (model_hbm, model_ref)], sem
-    )
-    for copy in copies:
+def widen_kernel(start, vis_hbm, model_hbm, keep_hbm, out_ref, *refs):
+    sem = refs[-1]
+    lanes = pl.ds(start * LANES, refs[0].shape[1])
+    sources = (hbm.at[:, lanes] for hbm in (vis_hbm, model_hbm, keep_hbm))
+    for copy in copy_in(list(zip(sources, refs[:-1], strict=True)), sem):
         copy.wait()
-    start = 0
-    for out_ref in refs[:-4]:
-        tiles = out_ref.shape[0] // (2 * SUBS)
-        for tile in range(tiles):
-            lanes = pl.ds((start + tile) * LANES, LANES)
-            out_ref[pl.ds(tile * SUBS, SUBS), :] = vis_ref[:, lanes].astype(F32)
-            out_ref[pl.ds((tiles + tile) * SUBS, SUBS), :] = model_ref[:, lanes].astype(
-                F32
-            ) * keep_ref[:, lanes].astype(F32)
-        start += tiles
+    vis_ref, model_ref, keep_ref = refs[:-1]
+    tiles = out_ref.shape[0] // (2 * SUBS)
+    for tile in range(tiles):
+        lanes = pl.ds(tile * LANES, LANES)
+        out_ref[pl.ds(tile * SUBS, SUBS), :] = vis_ref[:, lanes].astype(F32)
+        out_ref[pl.ds((tiles + tile) * SUBS, SUBS), :] = model_ref[:, lanes].astype(
+            F32
+        ) * keep_ref[:, lanes].astype(F32)
 
 
 def slot_products(slot_ref, group, tiles):
@@ -465,21 +462,24 @@
         return lax.ppermute(array, "tm", [(i, i ^ step) for i in range(slots)])
 
     sizes = [tiles // 2, tiles // 2]
-    pieces = call(
-        widen_kernel,
-        [vmem((2 * size * SUBS, LANES), F32) for size in sizes],
-        "hhh",
-        [
-            vmem((SUBS, baselines), BF16),
-            vmem((SUBS, baselines), BF16),
-            vmem((1, baselines), jnp.int32),
-            pltpu.SemaphoreType.DMA((3,)),
-        ],
-    )(
-        visibility.reshape(SUBS, baselines),
-        model_visibility.reshape(SUBS, baselines),
-        keep_mask.reshape(1, baselines),
-    )
+    pieces = []
+    for index, size in enumerate(sizes):
+        pieces += call(
+            lambda *refs, start=sum(sizes[:index]): widen_kernel(start, *refs),
+            [vmem((2 * size * SUBS, LANES), F32)],
+            "hhh",
+            [
+                vmem((SUBS, size * LANES), BF16),
+                vmem((SUBS, size * LANES), BF16),
+                vmem((1, size * LANES), jnp.int32),
+                pltpu.SemaphoreType.DMA((3,)),
+            ],
+            micros=0.001,
+        )(
+            visibility.reshape(SUBS, baselines),
+            model_visibility.reshape(SUBS, baselines),
+            keep_mask.reshape(1, baselines),
+        )
     far = []
     for piece in pieces:
         got = []

time: 27.5 us -> 27.5 us (level)
  waiting for transfers between devices: 3.41 us -> 2.59 us
  Pallas kernels: 6.34 us -> 7.01 us
    ppermute x6, waiting for transfers between devices: 3.41 us -> 2.59 us  [swap(): return lax.ppermute(array, 'tm', [(i, i ^ step) for i in range(slots)])]
    pallas_call x7 -> x8, Pallas kernels: 6.34 us -> 7.01 us  [placed(): run(*(arg if space == 's' else pltpu.with_memory_space_constraint(arg, SP...]
  transfers between devices with their start and end apart: 6 -> 6, of which waited for: 3 -> 3; matrix products, arithmetic and copies ran while one was open for 0% -> 0% of each run, Pallas kernels for 11% -> 14%
where the time goes in v8:
time: 27.5 us; the launch traced here: 27.1 us
  blocking collectives  12.6 us (46%)
  Pallas kernels  7.01 us (25%)
  starting transfers between devices  3.6 us (13%)
  waiting for transfers between devices  2.59 us (9%)
  between operations  1.34 us (5%)
    all_to_all x1, blocking collectives, shards(): lax.all_to_all(send.reshape(channels, 1, SENT * LANES), 'freq', 0, 0)  12.6 us
    pallas_call x8, Pallas kernels, placed(): run(*(arg if space == 's' else pltpu.with_memory_space_constraint(arg, SP...  7.01 us
    ppermute x6, starting transfers between devices, swap(): return lax.ppermute(array, 'tm', [(i, i ^ step) for i in range(slots)])  3.6 us
    ppermute x6, waiting for transfers between devices, swap(): return lax.ppermute(array, 'tm', [(i, i ^ step) for i in range(slots)])  2.59 us
  transfers between devices with their start and end apart: 6, of which 3 were waited for; matrix products, arithmetic and copies ran while one was open for 0% of the time, Pallas kernels for 14%

profile of v8, /device:TPU:0, one launch (start us, length us, event | category | flops | bytes accessed | tf_op | source)
XLA Modules:
  0.0 27.1 jit_solution(10036014535510365736)
XLA Ops:
  0.6 0.8 %shard_map.121.refs_0_ = f32[256,128]{1,0:T(8,128)S(1)} custom-call(bf16[8,4096]{1,0:T(8,128)(2,1)} %bitcast.16, bf16[8,4096]{1,0:T(8,128)(2,1)} %bitcast.18, s32[1,4096]{1,0:T(1,128)} %bitcast.20), custom_call_target="tpu_custom_call" | custom-call | flops 1000000 | bytes 3000 | tf_op jit(solution)/shard_map/pallas_call | solution.py:430
  1.5 3.0 %collective-permute-start.1 = (f32[256,128]{1,0:T(8,128)S(1)}, f32[256,128]{1,0:T(8,128)S(1)}, u32[]{:S(2)}, u32[]{:S(2)}) collective-permute-start(f32[256,128]{1,0:T(8,128)S(1)} %shard_map.121.refs_0_), channel_id=1, source_target_pairs={{0,2},{1,3},{2,0},{3,1},{4,6},{5,7},{6,4},{7,5},{8,10},{9,11},{10,... | collective-permute-start | bytes 393224 | tf_op jit(solution)/shard_map/ppermute | solution.py:462
  4.5 0.8 %shard_map.122.refs_1_ = f32[256,128]{1,0:T(8,128)S(1)} custom-call(bf16[8,4096]{1,0:T(8,128)(2,1)} %bitcast.17, bf16[8,4096]{1,0:T(8,128)(2,1)} %bitcast.19, s32[1,4096]{1,0:T(1,128)} %bitcast.21), custom_call_target="tpu_custom_call" | custom-call | flops 1000000 | bytes 3000 | tf_op jit(solution)/shard_map/pallas_call | solution.py:430
  5.3 0.1 collective-permute-start
  6.0 2.1 %shard_map.123 = (f32[48,16,128]{2,1,0:T(8,128)S(1)}, f32[48,16,128]{2,1,0:T(8,128)S(1)}, bf16[8192,128]{1,0:T(8,128)(2,1)S(1)}, bf16[96,8192]{1,0:T(8,128)(2,1)...) custom-call(f32[256,128]{1,0:T(8,128)S(1)} %shard_map.121.refs_0_, ...), custom_call_target="tpu_custom_call" | custom-call | flops 1000000000 | bytes 3000000 | tf_op jit(solution)/shard_map/pallas_call | solution.py:430
  8.1 0.3 collective-permute-done.1.refs_1_
  8.4 0.0 collective-permute-start.2
  8.4 0.5 %collective-permute-start.3 = (f32[256,128]{1,0:T(8,128)S(1)}, f32[256,128]{1,0:T(8,128)S(1)}, u32[]{:S(2)}, u32[]{:S(2)}) collective-permute-start(f32[256,128]{1,0:T(8,128)S(1)} %shard_map.121.refs_0_), channel_id=1, source_target_pairs={{0,1},{1,0},{2,3},{3,2},{4,5},{5,4},{6,7},{7,6},{8,9},{9,8},{10,11... | collective-permute-start | bytes 393224 | tf_op jit(solution)/shard_map/ppermute | solution.py:462
  8.9 0.0 collective-permute-start.4
  8.9 1.9 %collective-permute-done.refs_1_ = f32[256,128]{1,0:T(8,128)S(1)} collective-permute-done((f32[256,128]{1,0:T(8,128)S(1)}, f32[256,128]{1,0:T(8,128)S(1)}, u32[]{:S(2)}, u32[]{:S(2)}) %collective-permute-start) | collective-permute-done | bytes 131104 | tf_op jit(solution)/shard_map/ppermute | solution.py:462
  10.8 0.0 collective-permute-done.2.refs_4_
  10.8 0.0 collective-permute-start.5
  10.8 0.0 collective-permute-done.3.refs_0_
  10.8 0.1 shard_map.124.refs_3_
  10.9 0.6 %shard_map.125 = (f32[48,16,128]{2,1,0:T(8,128)S(1)}, f32[96,128]{1,0:T(8,128)S(1)}) custom-call(bf16[8192,128]{1,0:T(8,128)(2,1)S(1)} %get-tuple-element.28.refs_0_, bf16[96,8192]{1,0:T(8,128)(2,1)S(1)} %get-tuple-element.29.refs_1_, f32[2,8,32,128]{3,2,1,0:T(8,128)S(1)} %get-tuple-element.34.refs_2_, f32[48,16,128]{2,1,0:T(8,128)S(1)} %shard_map.124.refs_3_, ...), custom_call_target="tpu_custom_call" | custom-call | flops 1000000 | bytes 3000 | tf_op jit(solution)/shard_map/pallas_call | solution.py:430
  11.5 0.0 collective-permute-done.4.refs_0_
  11.6 0.1 shard_map.126.refs_9_
  11.7 0.4 %collective-permute-done.5.refs_10_ = f32[256,128]{1,0:T(8,128)S(1)} collective-permute-done((f32[256,128]{1,0:T(8,128)S(1)}, f32[256,128]{1,0:T(8,128)S(1)}, u32[]{:S(2)}, u32[]{:S(2)}) %collective-permute-start.5) | collective-permute-done | bytes 131104 | tf_op jit(solution)/shard_map/ppermute | solution.py:462
  12.1 1.8 %shard_map.127 = (f32[8,128]{1,0:T(8,128)S(1)}, f32[8,128]{1,0:T(8,128)S(1)}, f32[72,128]{1,0:T(8,128)S(1)}) custom-call(bf16[8192,128]{1,0:T(8,128)(2,1)S(1)} %get-tuple-element.28.refs_0_, bf16[96,8192]{1,0:T(8,128)(2,1)S(1)} %get-tuple-element.29.refs_1_, f32[2,8,32,128]{3,2,1,0:T(8,128)S(1)} %get-tuple-element.34.refs_2_, ...), custom_call_target="tpu_custom_call" | custom-call | tf_op jit(solution)/shard_map/pallas_call | solution.py:430
  13.9 12.6 %all_to_all.5 = f32[8,1,1152]{2,1,0:T(1,128)S(1)} all-to-all(f32[8,1,1152]{2,1,0:T(1,128)S(1)} %bitcast.15), channel_id=1, replica_groups=mesh['freq'=8,'tm'=4] {'freq'}, dimensions={0} | all-to-all | bytes 73728 | tf_op jit(solution)/shard_map/all_to_all | solution.py:569
  26.5 0.7 %shard_map.128 = (f32[8,128]{1,0:T(8,128)}, f32[8,128]{1,0:T(8,128)}, f32[8,128]{1,0:T(8,128)}) custom-call(f32[72,128]{1,0:T(8,128)S(1)} %bitcast.14, f32[16,128]{1,0:T(8,128)S(1)} %get-tuple-element.36.refs_4_.refs_1_, f32[8,128]{1,0:T(8,128)S(1)} %get-tuple-element.48.refs_2_, f32[8,128]{1,0:T(8,128)S(1)} %get-tuple-element.49.refs_3_), custom_call_target="tpu_custom_call" | custom-call | tf_op jit(solution)/shard_map/pallas_call | solution.py:430
Async XLA Ops:
  1.5 6.9 %collective-permute-start.1 = (f32[256,128]{1,0:T(8,128)S(1)}, f32[256,128]{1,0:T(8,128)S(1)}, u32[]{:S(2)}, u32[]{:S(2)}) collective-permute-start(f32[256,128]{1,0:T(8,128)S(1)} %shard_map.121.refs_0_), channel_id=1, source_target_pairs={{0,2},{1,3},{2,0},{3,1},{4,6},{5,7},{6,4},{7,5},{8,10},{9,11},{10,... | collective-permute-start | bytes 393224 | tf_op jit(solution)/shard_map/ppermute | solution.py:462
  5.3 5.5 %collective-permute-start = (f32[256,128]{1,0:T(8,128)S(1)}, f32[256,128]{1,0:T(8,128)S(1)}, u32[]{:S(2)}, u32[]{:S(2)}) collective-permute-start(f32[256,128]{1,0:T(8,128)S(1)} %shard_map.122.refs_1_), channel_id=1, source_target_pairs={{0,2},{1,3},{2,0},{3,1},{4,6},{5,7},{6,4},{7,5},{8,10},{9,11},{10,... | collective-permute-start | bytes 393224 | tf_op jit(solution)/shard_map/ppermute | solution.py:462
  8.4 2.4 %collective-permute-start.2 = (f32[256,128]{1,0:T(8,128)S(1)}, f32[256,128]{1,0:T(8,128)S(1)}, u32[]{:S(2)}, u32[]{:S(2)}) collective-permute-start(f32[256,128]{1,0:T(8,128)S(1)} %collective-permute-done.1.refs_1_), channel_id=1, source_target_pairs={{0,1},{1,0},{2,3},{3,2},{4,5},{5,4},{6,7},{7,6},{8,9},{9,8},{10,11... | collective-permute-start | bytes 393224 | tf_op jit(solution)/shard_map/ppermute | solution.py:462
  8.4 2.4 %collective-permute-start.3 = (f32[256,128]{1,0:T(8,128)S(1)}, f32[256,128]{1,0:T(8,128)S(1)}, u32[]{:S(2)}, u32[]{:S(2)}) collective-permute-start(f32[256,128]{1,0:T(8,128)S(1)} %shard_map.121.refs_0_), channel_id=1, source_target_pairs={{0,1},{1,0},{2,3},{3,2},{4,5},{5,4},{6,7},{7,6},{8,9},{9,8},{10,11... | collective-permute-start | bytes 393224 | tf_op jit(solution)/shard_map/ppermute | solution.py:462
  8.9 2.7 %collective-permute-start.4 = (f32[256,128]{1,0:T(8,128)S(1)}, f32[256,128]{1,0:T(8,128)S(1)}, u32[]{:S(2)}, u32[]{:S(2)}) collective-permute-start(f32[256,128]{1,0:T(8,128)S(1)} %shard_map.122.refs_1_), channel_id=1, source_target_pairs={{0,1},{1,0},{2,3},{3,2},{4,5},{5,4},{6,7},{7,6},{8,9},{9,8},{10,11... | collective-permute-start | bytes 393224 | tf_op jit(solution)/shard_map/ppermute | solution.py:462
  10.8 1.3 %collective-permute-start.5 = (f32[256,128]{1,0:T(8,128)S(1)}, f32[256,128]{1,0:T(8,128)S(1)}, u32[]{:S(2)}, u32[]{:S(2)}) collective-permute-start(f32[256,128]{1,0:T(8,128)S(1)} %collective-permute-done.refs_1_), channel_id=1, source_target_pairs={{0,1},{1,0},{2,3},{3,2},{4,5},{5,4},{6,7},{7,6},{8,9},{9,8},{10,11... | collective-permute-start | bytes 393224 | tf_op jit(solution)/shard_map/ppermute | solution.py:462

commit v9 on v8

--- a/solution.py
+++ b/solution.py
@@ -105,8 +105,7 @@
 def tables_kernel(count, *refs):
     slot_refs, channel_ref = refs[:count], refs[count]
     station_hbms, array_hbms = refs[count + 1 : count + 3], refs[count + 3 : count + 7]
-    prod_refs = refs[count + 7 : 2 * count + 7]
-    outs = refs[2 * count + 7 : -5]
+    outs = refs[count + 7 : -5]
     hot_ref, mask_ref, seen_ref, state_ref, own_ref, first_ref, second_ref = outs
     gains_ref, consensus_ref, dual_ref, penalty_ref, sem = refs[-5:]
     station_refs = (first_ref, second_ref)
@@ -120,9 +119,6 @@
         sem,
     )
     tiles = first_ref.shape[0]
-    for slot_ref, prod_ref in zip(slot_refs, prod_refs, strict=True):
-        for group in range(prod_ref.shape[1] // SUBS):
-            add_products([slot_ref], None, prod_ref, group)
     for copy in copies:
         copy.wait()
     blocks = gains_ref.shape[1] // LANES
@@ -164,9 +160,9 @@
                 ).astype(BF16)
 
 
-def more_kernel(before_ref, *refs):
-    for group in range(before_ref.shape[1] // SUBS):
-        add_products(refs[:-1], before_ref, refs[-1], group)
+def more_kernel(*refs):
+    for group in range(refs[-1].shape[1] // SUBS):
+        add_products(refs[:-1], None, refs[-1], group)
 
 
 def gram(gain):
@@ -501,7 +497,6 @@
     tables = call(
         lambda *refs: tables_kernel(count, *refs),
         [
-            *products,
             vmem((2 * baselines, LANES), BF16),
             vmem((blocks * 3 * PACK // 2, 2 * baselines), BF16),
             seen,
@@ -524,19 +519,19 @@
         dual,
         penalty.reshape(1, stations),
     )
-    summed = list(tables[:count])
-    hot, mask, found, state, own, first, second = tables[count:]
+    summed = [None, None]
+    hot, mask, found, state, own, first, second = tables
     pieces, state = lax.optimization_barrier((pieces, state))
     near = [swap(piece, 1) for piece in pieces]
     far[0], state = lax.optimization_barrier((far[0], state))
     last = [[swap(array, 1) for array in far[0]]]
     (summed[0],) = call(more_kernel, [products[0]], "v" * (2 + len(far[0])), micros=0.001)(
-        summed[0], near[0], *far[0]
+        pieces[0], near[0], *far[0]
     )
     far[1], last[0], found = lax.optimization_barrier((far[1], last[0], found))
     last.append([swap(array, 1) for array in far[1]])
     (summed[1],) = call(more_kernel, [products[1]], "v" * (2 + len(far[1])), micros=0.001)(
-        summed[1], near[1], *far[1]
+        pieces[1], near[1], *far[1]
     )
     summed[0], partial = call(
         lambda *refs: piece_kernel(0, *refs),

time: 27.5 us -> 27.5 us (level)
  no operation moved by 1% of the time
where the time goes in v9:
time: 27.5 us; the launch traced here: 27.1 us
  blocking collectives  12.6 us (46%)
  Pallas kernels  7.06 us (26%)
  starting transfers between devices  3.6 us (13%)
  waiting for transfers between devices  2.52 us (9%)
  between operations  1.34 us (5%)
    all_to_all x1, blocking collectives, shards(): lax.all_to_all(send.reshape(channels, 1, SENT * LANES), 'freq', 0, 0)  12.6 us
    pallas_call x8, Pallas kernels, placed(): run(*(arg if space == 's' else pltpu.with_memory_space_constraint(arg, SP...  7.06 us
    ppermute x6, starting transfers between devices, swap(): return lax.ppermute(array, 'tm', [(i, i ^ step) for i in range(slots)])  3.6 us
    ppermute x6, waiting for transfers between devices, swap(): return lax.ppermute(array, 'tm', [(i, i ^ step) for i in range(slots)])  2.52 us
  transfers between devices with their start and end apart: 6, of which 3 were waited for; matrix products, arithmetic and copies ran while one was open for 0% of the time, Pallas kernels for 14%

profile of v9, /device:TPU:0, one launch (start us, length us, event | category | flops | bytes accessed | tf_op | source)
XLA Modules:
  0.0 27.1 jit_solution(5494718545256142817)
XLA Ops:
  0.6 0.8 %shard_map.121.refs_0_ = f32[256,128]{1,0:T(8,128)S(1)} custom-call(bf16[8,4096]{1,0:T(8,128)(2,1)} %bitcast.16, bf16[8,4096]{1,0:T(8,128)(2,1)} %bitcast.18, s32[1,4096]{1,0:T(1,128)} %bitcast.20), custom_call_target="tpu_custom_call" | custom-call | flops 1000000 | bytes 3000 | tf_op jit(solution)/shard_map/pallas_call | solution.py:426
  1.5 3.0 %collective-permute-start.1 = (f32[256,128]{1,0:T(8,128)S(1)}, f32[256,128]{1,0:T(8,128)S(1)}, u32[]{:S(2)}, u32[]{:S(2)}) collective-permute-start(f32[256,128]{1,0:T(8,128)S(1)} %shard_map.121.refs_0_), channel_id=1, source_target_pairs={{0,2},{1,3},{2,0},{3,1},{4,6},{5,7},{6,4},{7,5},{8,10},{9,11},{10,... | collective-permute-start | bytes 393224 | tf_op jit(solution)/shard_map/ppermute | solution.py:458
  4.5 0.8 %shard_map.122.refs_1_.refs_0_ = f32[256,128]{1,0:T(8,128)S(1)} custom-call(bf16[8,4096]{1,0:T(8,128)(2,1)} %bitcast.17, bf16[8,4096]{1,0:T(8,128)(2,1)} %bitcast.19, s32[1,4096]{1,0:T(1,128)} %bitcast.21), custom_call_target="tpu_custom_call" | custom-call | flops 1000000 | bytes 3000 | tf_op jit(solution)/shard_map/pallas_call | solution.py:426
  5.3 0.1 collective-permute-start
  6.0 2.1 %shard_map.123 = (bf16[8192,128]{1,0:T(8,128)(2,1)S(1)}, bf16[96,8192]{1,0:T(8,128)(2,1)S(1)}, f32[2,8,32,128]{3,2,1,0:T(8,128)S(1)}, f32[136,128]{1,0:T(8,128)S...) custom-call(f32[256,128]{1,0:T(8,128)S(1)} %shard_map.121.refs_0_, ...), custom_call_target="tpu_custom_call" | custom-call | flops 1000000000 | bytes 3000000 | tf_op jit(solution)/shard_map/pallas_call | solution.py:426
  8.1 0.3 collective-permute-done.1.refs_2_
  8.4 0.0 collective-permute-start.2
  8.4 0.5 %collective-permute-start.3 = (f32[256,128]{1,0:T(8,128)S(1)}, f32[256,128]{1,0:T(8,128)S(1)}, u32[]{:S(2)}, u32[]{:S(2)}) collective-permute-start(f32[256,128]{1,0:T(8,128)S(1)} %shard_map.121.refs_0_), channel_id=1, source_target_pairs={{0,1},{1,0},{2,3},{3,2},{4,5},{5,4},{6,7},{7,6},{8,9},{9,8},{10,11... | collective-permute-start | bytes 393224 | tf_op jit(solution)/shard_map/ppermute | solution.py:458
  8.9 0.0 collective-permute-start.4
  8.9 1.9 %collective-permute-done.refs_2_ = f32[256,128]{1,0:T(8,128)S(1)} collective-permute-done((f32[256,128]{1,0:T(8,128)S(1)}, f32[256,128]{1,0:T(8,128)S(1)}, u32[]{:S(2)}, u32[]{:S(2)}) %collective-permute-start) | collective-permute-done | bytes 131104 | tf_op jit(solution)/shard_map/ppermute | solution.py:458
  10.8 0.0 collective-permute-done.2.refs_4_
  10.8 0.0 collective-permute-start.5
  10.8 0.0 collective-permute-done.3.refs_1_
  10.8 0.2 shard_map.124.refs_3_
  10.9 0.6 %shard_map.125 = (f32[48,16,128]{2,1,0:T(8,128)S(1)}, f32[96,128]{1,0:T(8,128)S(1)}) custom-call(bf16[8192,128]{1,0:T(8,128)(2,1)S(1)} %get-tuple-element.26.refs_0_, bf16[96,8192]{1,0:T(8,128)(2,1)S(1)} %get-tuple-element.27.refs_1_, f32[2,8,32,128]{3,2,1,0:T(8,128)S(1)} %get-tuple-element.32.refs_2_, f32[48,16,128]{2,1,0:T(8,128)S(1)} %shard_map.124.refs_3_, ...), custom_call_target="tpu_custom_call" | custom-call | flops 1000000 | bytes 3000 | tf_op jit(solution)/shard_map/pallas_call | solution.py:426
  11.6 0.0 collective-permute-done.4.refs_1_
  11.6 0.2 shard_map.126.refs_9_
  11.8 0.4 %collective-permute-done.5.refs_10_ = f32[256,128]{1,0:T(8,128)S(1)} collective-permute-done((f32[256,128]{1,0:T(8,128)S(1)}, f32[256,128]{1,0:T(8,128)S(1)}, u32[]{:S(2)}, u32[]{:S(2)}) %collective-permute-start.5) | collective-permute-done | bytes 131104 | tf_op jit(solution)/shard_map/ppermute | solution.py:458
  12.1 1.7 %shard_map.127 = (f32[8,128]{1,0:T(8,128)S(1)}, f32[8,128]{1,0:T(8,128)S(1)}, f32[72,128]{1,0:T(8,128)S(1)}) custom-call(bf16[8192,128]{1,0:T(8,128)(2,1)S(1)} %get-tuple-element.26.refs_0_, bf16[96,8192]{1,0:T(8,128)(2,1)S(1)} %get-tuple-element.27.refs_1_, f32[2,8,32,128]{3,2,1,0:T(8,128)S(1)} %get-tuple-element.32.refs_2_, ...), custom_call_target="tpu_custom_call" | custom-call | tf_op jit(solution)/shard_map/pallas_call | solution.py:426
  13.9 12.6 %all_to_all.5 = f32[8,1,1152]{2,1,0:T(1,128)S(1)} all-to-all(f32[8,1,1152]{2,1,0:T(1,128)S(1)} %bitcast.15), channel_id=1, replica_groups=mesh['freq'=8,'tm'=4] {'freq'}, dimensions={0} | all-to-all | bytes 73728 | tf_op jit(solution)/shard_map/all_to_all | solution.py:564
  26.4 0.7 %shard_map.128 = (f32[8,128]{1,0:T(8,128)}, f32[8,128]{1,0:T(8,128)}, f32[8,128]{1,0:T(8,128)}) custom-call(f32[72,128]{1,0:T(8,128)S(1)} %bitcast.14, f32[16,128]{1,0:T(8,128)S(1)} %get-tuple-element.34.refs_4_.refs_1_, f32[8,128]{1,0:T(8,128)S(1)} %get-tuple-element.44.refs_2_, f32[8,128]{1,0:T(8,128)S(1)} %get-tuple-element.45.refs_3_), custom_call_target="tpu_custom_call" | custom-call | tf_op jit(solution)/shard_map/pallas_call | solution.py:426
Async XLA Ops:
  1.5 6.9 %collective-permute-start.1 = (f32[256,128]{1,0:T(8,128)S(1)}, f32[256,128]{1,0:T(8,128)S(1)}, u32[]{:S(2)}, u32[]{:S(2)}) collective-permute-start(f32[256,128]{1,0:T(8,128)S(1)} %shard_map.121.refs_0_), channel_id=1, source_target_pairs={{0,2},{1,3},{2,0},{3,1},{4,6},{5,7},{6,4},{7,5},{8,10},{9,11},{10,... | collective-permute-start | bytes 393224 | tf_op jit(solution)/shard_map/ppermute | solution.py:458
  5.3 5.5 %collective-permute-start = (f32[256,128]{1,0:T(8,128)S(1)}, f32[256,128]{1,0:T(8,128)S(1)}, u32[]{:S(2)}, u32[]{:S(2)}) collective-permute-start(f32[256,128]{1,0:T(8,128)S(1)} %shard_map.122.refs_1_.refs_0_), channel_id=1, source_target_pairs={{0,2},{1,3},{2,0},{3,1},{4,6},{5,7},{6,4},{7,5},{8,10},{9,11},{10,... | collective-permute-start | bytes 393224 | tf_op jit(solution)/shard_map/ppermute | solution.py:458
  8.4 2.4 %collective-permute-start.2 = (f32[256,128]{1,0:T(8,128)S(1)}, f32[256,128]{1,0:T(8,128)S(1)}, u32[]{:S(2)}, u32[]{:S(2)}) collective-permute-start(f32[256,128]{1,0:T(8,128)S(1)} %collective-permute-done.1.refs_2_), channel_id=1, source_target_pairs={{0,1},{1,0},{2,3},{3,2},{4,5},{5,4},{6,7},{7,6},{8,9},{9,8},{10,11... | collective-permute-start | bytes 393224 | tf_op jit(solution)/shard_map/ppermute | solution.py:458
  8.4 2.4 %collective-permute-start.3 = (f32[256,128]{1,0:T(8,128)S(1)}, f32[256,128]{1,0:T(8,128)S(1)}, u32[]{:S(2)}, u32[]{:S(2)}) collective-permute-start(f32[256,128]{1,0:T(8,128)S(1)} %shard_map.121.refs_0_), channel_id=1, source_target_pairs={{0,1},{1,0},{2,3},{3,2},{4,5},{5,4},{6,7},{7,6},{8,9},{9,8},{10,11... | collective-permute-start | bytes 393224 | tf_op jit(solution)/shard_map/ppermute | solution.py:458
  8.9 2.7 %collective-permute-start.4 = (f32[256,128]{1,0:T(8,128)S(1)}, f32[256,128]{1,0:T(8,128)S(1)}, u32[]{:S(2)}, u32[]{:S(2)}) collective-permute-start(f32[256,128]{1,0:T(8,128)S(1)} %shard_map.122.refs_1_.refs_0_), channel_id=1, source_target_pairs={{0,1},{1,0},{2,3},{3,2},{4,5},{5,4},{6,7},{7,6},{8,9},{9,8},{10,11... | collective-permute-start | bytes 393224 | tf_op jit(solution)/shard_map/ppermute | solution.py:458
  10.8 1.3 %collective-permute-start.5 = (f32[256,128]{1,0:T(8,128)S(1)}, f32[256,128]{1,0:T(8,128)S(1)}, u32[]{:S(2)}, u32[]{:S(2)}) collective-permute-start(f32[256,128]{1,0:T(8,128)S(1)} %collective-permute-done.refs_2_), channel_id=1, source_target_pairs={{0,1},{1,0},{2,3},{3,2},{4,5},{5,4},{6,7},{7,6},{8,9},{9,8},{10,11... | collective-permute-start | bytes 393224 | tf_op jit(solution)/shard_map/ppermute | solution.py:458
